TPU v7x, 32 devices: a whole 2x2x4 slice. The times are simulated.
32 devices in a mesh: expert: 4 (over x, core), group: 8 (over z, y).
Axes of the slice: x: 2, y: 2, z: 4, core: 2. Of those that a mesh axis runs over, the one named last changes fastest.
Arguments:
- tokens: bfloat16 [16384, 2048], P(('expert', 'group')), may hold values from -6 to 6
- routing: int32 [16384, 8], P(('expert', 'group')), may hold values from 0 to 31, as said below
- mixing: float32 [16384, 8], P(('expert', 'group')), may hold values from 0.1 to 1
- visited: int32 [4], replicated, may hold values from 0 to 31, as said below
- gate_matrix: bfloat16 [32, 2048, 768], P('expert', 'group'), may hold values from -0.125 to 0.125
- up_matrix: bfloat16 [32, 2048, 768], P('expert', 'group'), may hold values from -0.125 to 0.125
- down_matrix: bfloat16 [32, 768, 2048], P('expert', None, 'group'), may hold values from -0.21875 to 0.21875
Outputs:
- combined: bfloat16 [16384, 2048], P(('expert', 'group'))
Inputs may be any that keep to these rules, and one draw needn't show every extreme that they name: `routing`: each row names 8 different experts. In the rows of one device, each expert of visited is named by at least half of 80 (rounded up) and at most 80 rows, and for each visited expert some device has exactly 80 such rows. `visited`: 4 different experts.
All inputs are finite; a program needn't handle non-finite values.
Results may differ from a plain program's by a relative error of at most 0.0049.
Values may be sent and summed in bfloat16 or wider, within the bound.
No kernel may reach another device: no remote copies, remote signals or barrier semaphores. Data moves between devices by JAX's collectives and lax.ppermute only.
A program may use at most 128 MiB of HBM per device.

v0:
```python
import functools

import jax
import jax.numpy as jnp
from jax import lax
from jax.experimental import pallas as pl
from jax.experimental.pallas import tpu as pltpu
from jax.sharding import PartitionSpec as P


VISITS = 4
CAP = 80
AXES = ("expert", "group")
F32 = jnp.float32
BF16 = jnp.bfloat16


VMEM = pl.BlockSpec(memory_space=pltpu.VMEM)
SMEM = pl.BlockSpec(memory_space=pltpu.SMEM)
ANY = pl.BlockSpec(memory_space=pl.ANY)
HBM = pl.BlockSpec(memory_space=pltpu.HBM)


def place(sides):
    e, g = lax.axis_index("expert"), lax.axis_index("group")
    z = g // sides
    return e, e & 1, (e >> 1) & 1, z, g % sides, (z ^ (z >> 1)) & 1


def visit(k, x, ab):
    return 2 * (ab if k % 2 == 0 else 1 - ab) + (x if k < 2 else 1 - x)


def call(kernel, out_shape, in_specs, args, scratch=(), limit=16, flops=0, size=0):
    many = isinstance(out_shape, list)
    return pl.pallas_call(
        kernel,
        out_shape=out_shape,
        in_specs=in_specs,
        out_specs=[VMEM] * len(out_shape) if many else VMEM,
        scratch_shapes=list(scratch),
        compiler_params=pltpu.CompilerParams(vmem_limit_bytes=limit << 20),
        cost_estimate=pl.CostEstimate(flops=flops, bytes_accessed=size, transcendentals=0),
    )(*args)


def pick_kernel(sides, visited, routing, mixing, tokens, *outs):
    picks, high, low = outs[:VISITS], outs[VISITS], outs[VISITS + 1]
    _, _, x, _, _, ab = place(sides)
    rows = tokens.shape[0]
    lanes = lax.broadcasted_iota(jnp.int32, (rows, 128), 1)
    named, mix = routing[...], mixing[...]
    shares, members = [], jnp.zeros((rows, 128), F32)
    for k in range(VISITS):
        hit = named == visited[visit(k, x, ab)]
        shares.append(jnp.sum(jnp.where(hit, mix, 0.0), axis=1, keepdims=True))
        found = jnp.sum(jnp.where(hit, 1.0, 0.0), axis=1, keepdims=True)
        members = members + jnp.where(lanes == k, found, 0.0)
    above = lax.broadcasted_iota(jnp.int32, (rows, rows), 0) > lax.broadcasted_iota(
        jnp.int32, (rows, rows), 1
    )
    ranks = jnp.dot(
        jnp.where(above, 1.0, 0.0).astype(BF16), members.astype(BF16), preferred_element_type=F32
    )
    places = jnp.where(members > 0.5, ranks + (lanes * CAP).astype(F32), -1.0)
    slots = lax.broadcasted_iota(jnp.int32, (rows, VISITS * CAP), 1).astype(F32)
    spread = jnp.zeros((rows, VISITS * CAP), F32)
    for k in range(VISITS):
        spread = spread + jnp.where(slots == places[:, k : k + 1], shares[k], 0.0)
    top = spread.astype(BF16)
    high[...] = top
    low[...] = (spread - top.astype(F32)).astype(BF16)
    across = places.T
    slots = lax.broadcasted_iota(jnp.int32, (CAP, rows), 0).astype(F32)
    for k in range(VISITS):
        one = jnp.where(slots + float(CAP * k) == across[k : k + 1, :], 1.0, 0.0).astype(BF16)
        picks[k][...] = jnp.dot(one, tokens[...], preferred_element_type=F32).astype(BF16)


def merge_kernel(high, low, *refs):
    pieces, out = refs[:VISITS], refs[VISITS]
    values = jnp.concatenate([piece[...] for piece in pieces], axis=0)
    total = jnp.dot(high[...], values, preferred_element_type=F32)
    total = total + jnp.dot(low[...], values, preferred_element_type=F32)
    out[...] = total.astype(BF16)


def merge(high, low, pieces):
    rows, width = high.shape[0], pieces[0].shape[1]
    tile = 512
    whole = pl.BlockSpec(high.shape, lambda i: (0, 0))
    return pl.pallas_call(
        merge_kernel,
        grid=(width // tile,),
        out_shape=jax.ShapeDtypeStruct((rows, width), BF16),
        in_specs=[whole, whole] + [pl.BlockSpec((CAP, tile), lambda i: (0, i))] * VISITS,
        out_specs=pl.BlockSpec((rows, tile), lambda i: (0, i)),
        compiler_params=pltpu.CompilerParams(vmem_limit_bytes=16 << 20),
        name="merge",
    )(high, low, *pieces)


def cut_kernel(sides, held, axes, visited, *refs):
    count = len(axes)
    matrices, outs, sem = refs[:count], refs[count : 3 * count], refs[3 * count]
    _, c, x, _, _, ab = place(sides)
    copies = []
    for n, axis in enumerate(axes):
        mine, theirs = outs[2 * n], outs[2 * n + 1]
        size = mine.shape[axis + 1]
        for k in range(VISITS):
            local = lax.rem(visited[visit(k, x, ab)], held)
            for out, half in ((theirs, 1 - c), (mine, c)):
                part = pl.ds(pl.multiple_of(half * size, 128), size)
                source = matrices[n].at[local]
                source = source.at[part, :] if axis == 0 else source.at[:, part]
                copies.append(pltpu.make_async_copy(source, out.at[k], sem.at[len(copies)]))
    for copy in copies:
        copy.start()
    for copy in copies:
        copy.wait()


def cut(sides, visited, matrices, axes):
    shapes = []
    for matrix, axis in zip(matrices, axes):
        _, a, b = matrix.shape
        half = (VISITS, a // 2, b) if axis == 0 else (VISITS, a, b // 2)
        shapes += [jax.ShapeDtypeStruct(half, BF16)] * 2
    return call(
        functools.partial(cut_kernel, sides, matrices[0].shape[0], axes),
        shapes,
        [SMEM] + [HBM] * len(matrices),
        (visited, *matrices),
        [pltpu.SemaphoreType.DMA((2 * VISITS * len(matrices),))],
    )


def choose(own, out, here, there):
    @pl.when(own)
    def _():
        out[...] = here[...]

    @pl.when(jnp.logical_not(own))
    def _():
        out[...] = there[...]


def blend_kernel(sides, held, bit, visited, mine, theirs, got, mine_out, theirs_out):
    e, _, x, _, _, ab = place(sides)
    for k in range(VISITS):
        owner = visited[visit(k, x, ab)] // held
        own = (owner & bit) == (e & bit)
        choose(own, mine_out.at[k], mine.at[k], got.at[k])
        choose(own, theirs_out.at[k], theirs.at[k], got.at[VISITS + k])


def send_kernel(sides, held, visited, mine, got, out):
    _, c, x, _, _, ab = place(sides)
    for k in range(2):
        owner = visited[visit(2 + k, x, ab)] // held
        choose((owner & 1) == c, out.at[k], mine.at[2 + k], got.at[2 + k])


def keep_kernel(sides, held, visited, mine, got, far, same, other):
    _, c, x, _, _, ab = place(sides)
    for k, out in enumerate((same, other)):
        owner = visited[visit(k, x, ab)] // held
        near = ((owner >> 1) & 1) == x

        @pl.when(near)
        def _():
            choose((owner & 1) == c, out, mine.at[k], got.at[k])

        @pl.when(jnp.logical_not(near))
        def _():
            out[...] = far[k]


def load_blocks(sides, keys, blocks, held, sem, down):
    _, c, _, z, y, _ = place(sides)
    copies = []
    for n, ((plane_bits, side_bits, core), block) in enumerate(zip(keys, blocks)):
        piece = (z ^ plane_bits) * sides + (y ^ side_bits)
        rows, columns = block.shape
        if down:
            first = pl.ds(pl.multiple_of((c ^ core) * rows, 128), rows)
            spot = held.at[first, pl.ds(pl.multiple_of(piece * columns, 128), columns)]
        else:
            spot = held.at[pl.ds(pl.multiple_of(piece * rows, 128), rows), :]
        copies.append(pltpu.make_async_copy(block, spot, sem.at[n]))
    for copy in copies:
        copy.start()
    for copy in copies:
        copy.wait()


def gate_kernel(sides, keys, *refs):
    blocks, rows = refs[: len(keys)], refs[len(keys) : len(keys) + 2 * VISITS]
    out, held, sem = refs[len(keys) + 2 * VISITS :]
    load_blocks(sides, keys, blocks, held, sem, False)
    for side in range(2):
        picked = jnp.concatenate([ref[...] for ref in rows[side * VISITS : (side + 1) * VISITS]], axis=0)
        out[side] = jnp.dot(picked, held[...], preferred_element_type=F32)


def up_kernel(sides, keys, *refs):
    blocks, rows = refs[: len(keys)], refs[len(keys) : len(keys) + 2 * VISITS]
    gate, own, partner, held, sem = refs[len(keys) + 2 * VISITS :]
    load_blocks(sides, keys, blocks, held, sem, False)
    for side, out in enumerate((own, partner)):
        picked = jnp.concatenate([ref[...] for ref in rows[side * VISITS : (side + 1) * VISITS]], axis=0)
        up = jnp.dot(picked, held[...], preferred_element_type=F32)
        out[...] = (jax.nn.silu(gate[side]) * up).astype(BF16)


def down_kernel(sides, keys, *refs):
    count = len(keys)
    blocks, (own, partner), outs = refs[:count], refs[count : count + 2], refs[count + 2 : count + 2 + VISITS]
    held, hidden, sem = refs[count + 2 + VISITS :]
    _, c, _, _, _, _ = place(sides)
    inner = own.shape[1]
    hidden[:, pl.ds(pl.multiple_of(c * inner, 128), inner)] = own[...]
    hidden[:, pl.ds(pl.multiple_of((1 - c) * inner, 128), inner)] = partner[...]
    load_blocks(sides, keys, blocks, held, sem, True)
    out = jnp.dot(hidden[...], held[...], preferred_element_type=F32).astype(BF16)
    for k in range(VISITS):
        outs[k][...] = out[k * CAP : (k + 1) * CAP]


def body(mesh, tokens, routing, mixing, visited, gate_matrix, up_matrix, down_matrix):
    experts, groups = mesh.shape["expert"], mesh.shape["group"]
    planes = VISITS
    sides = groups // planes
    held = gate_matrix.shape[0]
    count, width = tokens.shape
    inner = gate_matrix.shape[2]
    total = VISITS * CAP
    shape = jax.ShapeDtypeStruct

    def swap(value, expert_bits=0, plane_bits=0, side_bits=0):
        pairs = []
        for one in range(experts):
            for two in range(groups):
                other = ((two // sides) ^ plane_bits) * sides + ((two % sides) ^ side_bits)
                pairs.append((one * groups + two, (one ^ expert_bits) * groups + other))
        return lax.ppermute(value, AXES, pairs)

    halves = list(cut(sides, visited, [gate_matrix], [1]))
    halves += cut(sides, visited, [up_matrix, down_matrix], [1, 0])
    matrices = []
    for n in range(3):
        mine, theirs = halves[2 * n : 2 * n + 2]
        bit = 4
        while bit < experts:
            got = swap(jnp.concatenate([mine, theirs], axis=0), expert_bits=bit)
            mine, theirs = call(
                functools.partial(blend_kernel, sides, held, bit),
                [shape(mine.shape, BF16)] * 2,
                [SMEM] + [VMEM] * 3,
                (visited, mine, theirs, got),
                limit=32,
            )
            bit *= 2
        matrices.append((mine, swap(theirs, expert_bits=1)))

    *picked, high, low = call(
        functools.partial(pick_kernel, sides),
        [shape((CAP, width), BF16)] * VISITS + [shape((count, total), BF16)] * 2,
        [SMEM, VMEM, VMEM, VMEM],
        (visited, routing, mixing, tokens),
        limit=24,
    )

    sent = []
    for mine, got in matrices:
        block = mine.shape[1:]
        away = call(
            functools.partial(send_kernel, sides, held),
            shape((2, *block), BF16),
            [SMEM, VMEM, VMEM],
            (visited, mine, got),
        )
        sent.append(swap(away, expert_bits=2))
    rows = [
        picked[0],
        swap(picked[1], plane_bits=1),
        swap(picked[2], expert_bits=2),
        swap(picked[3], expert_bits=2, plane_bits=1),
    ]

    pieces = []
    for n, (mine, got) in enumerate(matrices):
        block = mine.shape[1:]
        same, other = call(
            functools.partial(keep_kernel, sides, held),
            [shape(block, BF16)] * 2,
            [SMEM] + [VMEM] * 3,
            (visited, mine, got, sent[n]),
        )
        found = [
            (0, same), (1, swap(other, plane_bits=1)), (2, swap(other, plane_bits=2)), (3, swap(same, plane_bits=3))
        ]
        keys, blocks = [], []
        for plane_bits, value in found:
            for side_bits in range(sides):
                moved = value
                if side_bits:
                    moved = swap(value, side_bits=side_bits)
                keys.append((plane_bits, side_bits, 0))
                blocks.append(moved)
                if n == 2:
                    keys.append((plane_bits, side_bits, 1))
                    blocks.append(swap(moved, expert_bits=1))
        pieces.append((keys, blocks))

    rows += [swap(value, expert_bits=1) for value in rows]
    keys, blocks = pieces[0]
    work = 4 * total * width * inner // 2
    gate = call(
        functools.partial(gate_kernel, sides, keys),
        shape((2, total, inner // 2), F32),
        [ANY] * len(keys) + [VMEM] * len(rows),
        (*blocks, *rows),
        [pltpu.VMEM((width, inner // 2), BF16), pltpu.SemaphoreType.DMA((len(keys),))],
        flops=work,
    )
    keys, blocks = pieces[1]
    own, partner = call(
        functools.partial(up_kernel, sides, keys),
        [shape((total, inner // 2), BF16)] * 2,
        [ANY] * len(keys) + [VMEM] * (len(rows) + 1),
        (*blocks, *rows, gate),
        [pltpu.VMEM((width, inner // 2), BF16), pltpu.SemaphoreType.DMA((len(keys),))],
        flops=work,
    )
    partner = swap(partner, expert_bits=1)
    keys, blocks = pieces[2]
    outs = call(
        functools.partial(down_kernel, sides, keys),
        [shape((CAP, width), BF16)] * VISITS,
        [ANY] * len(keys) + [VMEM] * 2,
        (*blocks, own, partner),
        [
            pltpu.VMEM((inner, width), BF16),
            pltpu.VMEM((total, inner), BF16),
            pltpu.SemaphoreType.DMA((len(keys),)),
        ],
        flops=work,
    )
    back = [
        outs[0], swap(outs[1], plane_bits=1), swap(outs[2], expert_bits=2), swap(outs[3], expert_bits=2, plane_bits=1)
    ]
    return merge(high, low, back)


def solution(mesh):
    placed = (
        P(("expert", "group"), None),
        P(("expert", "group"), None),
        P(("expert", "group"), None),
        P(),
        P("expert", "group", None),
        P("expert", "group", None),
        P("expert", None, "group"),
    )
    return jax.shard_map(
        functools.partial(body, mesh),
        mesh=mesh,
        in_specs=placed,
        out_specs=P(("expert", "group"), None),
        check_vma=False,
    )
```

profile of v0, /device:TPU:0, one launch (start us, length us, event | category | flops | bytes accessed | tf_op | source)
XLA Modules:
  0.0 172.1 jit_solution(13276269513120461818)
XLA Ops:
  0.0 2.0 %copy-done.4 = bf16[8,256,768]{2,1,0:T(8,128)(2,1)S(1)} copy-done((bf16[8,256,768]{2,1,0:T(8,128)(2,1)S(1)}, bf16[8,256,768]{2,1,0:T(8,128)(2,1)}, u32[]{:S(2)}) %copy-start.4) | copy-done | bytes 3145752
  2.7 1.7 %shard_map.79 = (bf16[4,256,384]{2,1,0:T(8,128)(2,1)S(1)}, bf16[4,256,384]{2,1,0:T(8,128)(2,1)}) custom-call(s32[4]{0:T(128)S(1)} %copy-done.7, bf16[8,256,768]{2,1,0:T(8,128)(2,1)S(1)} %copy-done.4), custom_call_target="tpu_custom_call" | custom-call | tf_op jit(solution)/shard_map/pallas_call | solution.py:36
  5.0 1.9 %copy-done.1 = bf16[8,768,256]{2,1,0:T(8,128)(2,1)S(1)} copy-done((bf16[8,768,256]{2,1,0:T(8,128)(2,1)S(1)}, bf16[8,768,256]{2,1,0:T(8,128)(2,1)}, u32[]{:S(2)}) %copy-start.1) | copy-done | bytes 3145752
  6.9 4.1 %shard_map.74 = (bf16[4,256,384]{2,1,0:T(8,128)(2,1)S(1)}, bf16[4,256,384]{2,1,0:T(8,128)(2,1)}, bf16[4,384,256]{2,1,0:T(8,128)(2,1)S(1)}, bf16[4,384,256]{2,1,0:T(8,128)(2,1)}) custom-call(s32[4]{0:T(128)S(1)} %copy-done.7, bf16[8,256,768]{2,1,0:T(8,128)(2,1)S(1)} %copy-done, bf16[8,768,256]{2,1,0:T(8,128)(2,1)S(1)} %copy-done.1), custom_call_target="tpu_custom_call" | custom-call | tf_op jit(solution)/shard_map/pallas_call | solution.py:36
  12.6 1.6 copy-done.5
  15.1 3.2 %shard_map.73 = (bf16[80,2048]{1,0:T(8,128)(2,1)S(1)}, bf16[80,2048]{1,0:T(8,128)(2,1)S(1)}, bf16[80,2048]{1,0:T(8,128)(2,1)S(1)}, bf16[80,2048]{1,0:T(8,128)(2,...) custom-call(s32[4]{0:T(128)S(1)} %copy-done.8, s32[512,8]{1,0:T(8,128)S(1)} %copy.8.routing, ...), custom_call_target="tpu_custom_call" | custom-call | tf_op jit(solution)/shard_map/pallas_call | solution.py:36
  18.3 2.8 %collective-permute-start.26 = (bf16[80,2048]{1,0:T(8,128)(2,1)S(1)}, bf16[80,2048]{1,0:T(8,128)(2,1)S(1)}, u32[]{:S(2)}, u32[]{:S(2)}) collective-permute-start(bf16[80,2048]{1,0:T(8,128)(2,1)S(1)} %get-tuple-element.40), channel_id=1, source_target_pairs={{0,2},{1,3},{2,0},{3,1},{4,6},{5,7},{6,4},{7,5},{8,10},{9,11},{10,... | collective-permute-start | bytes 983048 | tf_op jit(solution)/shard_map/ppermute | solution.py:247
  24.5 4.8 %collective-permute-done.26.refs_9_ = bf16[80,2048]{1,0:T(8,128)(2,1)S(1)} collective-permute-done((bf16[80,2048]{1,0:T(8,128)(2,1)S(1)}, bf16[80,2048]{1,0:T(8,128)(2,1)S(1)}, u32[]{:S(2)}, u32[]{:S(2)}) %collective-permute-start.26) | collective-permute-done | bytes 327712 | tf_op jit(solution)/shard_map/ppermute | solution.py:247
  29.3 2.7 %collective-permute-start.28 = (bf16[80,2048]{1,0:T(8,128)(2,1)S(1)}, bf16[80,2048]{1,0:T(8,128)(2,1)S(1)}, u32[]{:S(2)}, u32[]{:S(2)}) collective-permute-start(bf16[80,2048]{1,0:T(8,128)(2,1)S(1)} %get-tuple-element.42), channel_id=1, source_target_pairs={{0,18},{1,19},{2,16},{3,17},{4,22},{5,23},{6,20},{7,21},{8,26},{9,... | collective-permute-start | bytes 983048 | tf_op jit(solution)/shard_map/ppermute | solution.py:247
  33.8 14.6 %collective-permute-done.27.refs_10_ = bf16[80,2048]{1,0:T(8,128)(2,1)S(1)} collective-permute-done((bf16[80,2048]{1,0:T(8,128)(2,1)S(1)}, bf16[80,2048]{1,0:T(8,128)(2,1)S(1)}, u32[]{:S(2)}, u32[]{:S(2)}) %collective-permute-start.27) | collective-permute-done | bytes 327712 | tf_op jit(solution)/shard_map/ppermute | solution.py:247
  51.8 5.1 %collective-permute-done.18.far = bf16[2,256,384]{2,1,0:T(8,128)(2,1)S(1)} collective-permute-done((bf16[2,256,384]{2,1,0:T(8,128)(2,1)S(1)}, bf16[2,256,384]{2,1,0:T(8,128)(2,1)S(1)}, u32[]{:S(2)}, u32[]{:S(2)}) %collective-permute-start.18) | collective-permute-done | bytes 393248 | tf_op jit(solution)/shard_map/ppermute | solution.py:247
  56.9 2.5 %collective-permute-start.40 = (bf16[256,384]{1,0:T(8,128)(2,1)S(1)}, bf16[256,384]{1,0:T(8,128)(2,1)S(1)}, u32[]{:S(2)}, u32[]{:S(2)}) collective-permute-start(bf16[256,384]{1,0:T(8,128)(2,1)S(1)} %get-tuple-element.45.refs_0_), channel_id=1, source_target_pairs={{0,6},{1,7},{2,4},{3,5},{4,2},{5,3},{6,0},{7,1},{8,14},{9,15},{10,... | collective-permute-start | bytes 589832 | tf_op jit(solution)/shard_map/ppermute | solution.py:247
  64.4 2.5 %collective-permute-start.24 = (bf16[256,384]{1,0:T(8,128)(2,1)S(1)}, bf16[256,384]{1,0:T(8,128)(2,1)S(1)}, u32[]{:S(2)}, u32[]{:S(2)}) collective-permute-start(bf16[256,384]{1,0:T(8,128)(2,1)S(1)} %get-tuple-element.37.refs_0_), channel_id=1, source_target_pairs={{0,6},{1,7},{2,4},{3,5},{4,2},{5,3},{6,0},{7,1},{8,14},{9,15},{10,... | collective-permute-start | bytes 589832 | tf_op jit(solution)/shard_map/ppermute | solution.py:247
  66.9 7.4 %collective-permute-start.20 = (bf16[256,384]{1,0:T(8,128)(2,1)S(1)}, bf16[256,384]{1,0:T(8,128)(2,1)S(1)}, u32[]{:S(2)}, u32[]{:S(2)}) collective-permute-start(bf16[256,384]{1,0:T(8,128)(2,1)S(1)} %get-tuple-element.38), channel_id=1, source_target_pairs={{0,2},{1,3},{2,0},{3,1},{4,6},{5,7},{6,4},{7,5},{8,10},{9,11},{10,... | collective-permute-start | bytes 589832 | tf_op jit(solution)/shard_map/ppermute | solution.py:247
  76.0 6.8 %collective-permute-done.38.refs_4_ = bf16[256,384]{1,0:T(8,128)(2,1)S(1)} collective-permute-done((bf16[256,384]{1,0:T(8,128)(2,1)S(1)}, bf16[256,384]{1,0:T(8,128)(2,1)S(1)}, u32[]{:S(2)}, u32[]{:S(2)}) %collective-permute-start.38) | collective-permute-done | bytes 196640 | tf_op jit(solution)/shard_map/ppermute | solution.py:247
  84.3 2.5 %collective-permute-start.13 = (bf16[384,256]{1,0:T(8,128)(2,1)S(1)}, bf16[384,256]{1,0:T(8,128)(2,1)S(1)}, u32[]{:S(2)}, u32[]{:S(2)}) collective-permute-start(bf16[384,256]{1,0:T(8,128)(2,1)S(1)} %get-tuple-element.33.refs_0_), channel_id=1, source_target_pairs={{0,6},{1,7},{2,4},{3,5},{4,2},{5,3},{6,0},{7,1},{8,14},{9,15},{10,... | collective-permute-start | bytes 589832 | tf_op jit(solution)/shard_map/ppermute | solution.py:247
  86.8 10.2 %collective-permute-start.9 = (bf16[384,256]{1,0:T(8,128)(2,1)S(1)}, bf16[384,256]{1,0:T(8,128)(2,1)S(1)}, u32[]{:S(2)}, u32[]{:S(2)}) collective-permute-start(bf16[384,256]{1,0:T(8,128)(2,1)S(1)} %get-tuple-element.34), channel_id=1, source_target_pairs={{0,4},{1,5},{2,6},{3,7},{4,0},{5,1},{6,2},{7,3},{8,12},{9,13},{10,... | collective-permute-start | bytes 589832 | tf_op jit(solution)/shard_map/ppermute | solution.py:247
  97.0 2.7 %collective-permute-done.22.refs_4_ = bf16[256,384]{1,0:T(8,128)(2,1)S(1)} collective-permute-done((bf16[256,384]{1,0:T(8,128)(2,1)S(1)}, bf16[256,384]{1,0:T(8,128)(2,1)S(1)}, u32[]{:S(2)}, u32[]{:S(2)}) %collective-permute-start.22) | collective-permute-done | bytes 196640 | tf_op jit(solution)/shard_map/ppermute | solution.py:247
  99.7 3.6 %collective-permute-start.3 = (bf16[384,256]{1,0:T(8,128)(2,1)S(1)}, bf16[384,256]{1,0:T(8,128)(2,1)S(1)}, u32[]{:S(2)}, u32[]{:S(2)}) collective-permute-start(bf16[384,256]{1,0:T(8,128)(2,1)S(1)} %get-tuple-element.33.refs_0_), channel_id=1, source_target_pairs={{0,1},{1,0},{2,3},{3,2},{4,5},{5,4},{6,7},{7,6},{8,9},{9,8},{10,11... | collective-permute-start | bytes 589832 | tf_op jit(solution)/shard_map/ppermute | solution.py:247
  103.3 5.8 %collective-permute-done.9.refs_8_ = bf16[384,256]{1,0:T(8,128)(2,1)S(1)} collective-permute-done((bf16[384,256]{1,0:T(8,128)(2,1)S(1)}, bf16[384,256]{1,0:T(8,128)(2,1)S(1)}, u32[]{:S(2)}, u32[]{:S(2)}) %collective-permute-start.9) | collective-permute-done | bytes 196640 | tf_op jit(solution)/shard_map/ppermute | solution.py:247
  114.7 2.2 %collective-permute-done.37.refs_3_ = bf16[256,384]{1,0:T(8,128)(2,1)S(1)} collective-permute-done((bf16[256,384]{1,0:T(8,128)(2,1)S(1)}, bf16[256,384]{1,0:T(8,128)(2,1)S(1)}, u32[]{:S(2)}, u32[]{:S(2)}) %collective-permute-start.37) | collective-permute-done | bytes 196640 | tf_op jit(solution)/shard_map/ppermute | solution.py:247
  118.4 2.7 %collective-permute-done.39.refs_5_ = bf16[256,384]{1,0:T(8,128)(2,1)S(1)} collective-permute-done((bf16[256,384]{1,0:T(8,128)(2,1)S(1)}, bf16[256,384]{1,0:T(8,128)(2,1)S(1)}, u32[]{:S(2)}, u32[]{:S(2)}) %collective-permute-start.39) | collective-permute-done | bytes 196640 | tf_op jit(solution)/shard_map/ppermute | solution.py:247
  121.1 4.2 %collective-permute-done.25.refs_7_ = bf16[256,384]{1,0:T(8,128)(2,1)S(1)} collective-permute-done((bf16[256,384]{1,0:T(8,128)(2,1)S(1)}, bf16[256,384]{1,0:T(8,128)(2,1)S(1)}, u32[]{:S(2)}, u32[]{:S(2)}) %collective-permute-start.25) | collective-permute-done | bytes 196640 | tf_op jit(solution)/shard_map/ppermute | solution.py:247
  126.8 2.7 %collective-permute-done.21.refs_3_ = bf16[256,384]{1,0:T(8,128)(2,1)S(1)} collective-permute-done((bf16[256,384]{1,0:T(8,128)(2,1)S(1)}, bf16[256,384]{1,0:T(8,128)(2,1)S(1)}, u32[]{:S(2)}, u32[]{:S(2)}) %collective-permute-start.21) | collective-permute-done | bytes 196640 | tf_op jit(solution)/shard_map/ppermute | solution.py:247
  129.6 4.2 %collective-permute-done.23.refs_5_ = bf16[256,384]{1,0:T(8,128)(2,1)S(1)} collective-permute-done((bf16[256,384]{1,0:T(8,128)(2,1)S(1)}, bf16[256,384]{1,0:T(8,128)(2,1)S(1)}, u32[]{:S(2)}, u32[]{:S(2)}) %collective-permute-start.23) | collective-permute-done | bytes 196640 | tf_op jit(solution)/shard_map/ppermute | solution.py:247
  135.2 2.7 %collective-permute-done.15.refs_14_ = bf16[384,256]{1,0:T(8,128)(2,1)S(1)} collective-permute-done((bf16[384,256]{1,0:T(8,128)(2,1)S(1)}, bf16[384,256]{1,0:T(8,128)(2,1)S(1)}, u32[]{:S(2)}, u32[]{:S(2)}) %collective-permute-start.15) | collective-permute-done | bytes 196640 | tf_op jit(solution)/shard_map/ppermute | solution.py:247
  138.0 3.7 %shard_map.82.refs_16_ = f32[2,320,384]{2,1,0:T(8,128)S(1)} custom-call(bf16[256,384]{1,0:T(8,128)(2,1)S(1)} %get-tuple-element.45.refs_0_, bf16[256,384]{1,0:T(8,128)(2,1)S(1)} %collective-permute-done.35.refs_1_, bf16[256,384]{1,0:T(8,128)(2,1)S(1)} %collective-permute-done.36.refs_2_, bf16[256,384]{1,0:T(8,128)(2,1)S(1)} %collective-permute-done.37.refs_3_, ...), custom_call_target="tpu_custom_call" | custom-call | flops 1006632960 | tf_op jit(solution)/shard_map/pallas_call | solution.py:36
  141.7 3.8 %shard_map.83 = (bf16[320,384]{1,0:T(8,128)(2,1)S(1)}, bf16[320,384]{1,0:T(8,128)(2,1)S(1)}) custom-call(bf16[256,384]{1,0:T(8,128)(2,1)S(1)} %get-tuple-element.37.refs_0_, bf16[256,384]{1,0:T(8,128)(2,1)S(1)} %collective-permute-done.19.refs_1_, bf16[256,384]{1,0:T(8,128)(2,1)S(1)} %collective-permute-done.20.refs_2_, ...), custom_call_target="tpu_custom_call" | custom-call | flops 1006632960 | tf_op jit(solution)/shard_map/pallas_call | solution.py:36
  148.4 1.9 %shard_map.84 = (bf16[80,2048]{1,0:T(8,128)(2,1)S(1)}, bf16[80,2048]{1,0:T(8,128)(2,1)S(1)}, bf16[80,2048]{1,0:T(8,128)(2,1)S(1)}, bf16[80,2048]{1,0:T(8,128)(2,1)S(1)}) custom-call(bf16[384,256]{1,0:T(8,128)(2,1)S(1)} %get-tuple-element.33.refs_0_, bf16[384,256]{1,0:T(8,128)(2,1)S(1)} %collective-permute-done.2.refs_1_, ...), custom_call_target="tpu_custom_call" | custom-call | flops 1006632960 | tf_op jit(solution)/shard_map/pallas_call | solution.py:36
  153.8 7.1 %collective-permute-done.43.refs_1_ = bf16[80,2048]{1,0:T(8,128)(2,1)S(1)} collective-permute-done((bf16[80,2048]{1,0:T(8,128)(2,1)S(1)}, bf16[80,2048]{1,0:T(8,128)(2,1)S(1)}, u32[]{:S(2)}, u32[]{:S(2)}) %collective-permute-start.43) | collective-permute-done | bytes 327712 | tf_op jit(solution)/shard_map/ppermute | solution.py:247
  160.9 6.1 %collective-permute-done.44.refs_2_ = bf16[80,2048]{1,0:T(8,128)(2,1)S(1)} collective-permute-done((bf16[80,2048]{1,0:T(8,128)(2,1)S(1)}, bf16[80,2048]{1,0:T(8,128)(2,1)S(1)}, u32[]{:S(2)}, u32[]{:S(2)}) %collective-permute-start.44) | collective-permute-done | bytes 327712 | tf_op jit(solution)/shard_map/ppermute | solution.py:247
  168.3 3.8 %merge.1 = bf16[512,2048]{1,0:T(8,128)(2,1)} custom-call(bf16[512,320]{1,0:T(8,128)(2,1)S(1)} %get-tuple-element.29.high, bf16[512,320]{1,0:T(8,128)(2,1)S(1)} %get-tuple-element.30.low, bf16[80,2048]{1,0:T(8,128)(2,1)S(1)} %get-tuple-element.49.refs_0_, bf16[80,2048]{1,0:T(8,128)(2,1)S(1)} %collective-permute-done.43.refs_1_, ...), custom_call_target="tpu_custom_call" | custom-call | tf_op jit(solution)/shard_map/merge/pallas_call | solution.py:92
  (97 shorter events, 38.0 us)
Async XLA Ops:
  4.4 16.7 %collective-permute-start.33 = (bf16[4,256,384]{2,1,0:T(8,128)(2,1)}, bf16[4,256,384]{2,1,0:T(8,128)(2,1)}, u32[]{:S(2)}, u32[]{:S(2)}) collective-permute-start(bf16[4,256,384]{2,1,0:T(8,128)(2,1)} %get-tuple-element.44), channel_id=1, source_target_pairs={{0,8},{1,9},{2,10},{3,11},{4,12},{5,13},{6,14},{7,15},{8,0},{9,1},... | collective-permute-start | bytes 2359304 | tf_op jit(solution)/shard_map/ppermute | solution.py:247
  11.0 21.0 %collective-permute-start.17 = (bf16[4,256,384]{2,1,0:T(8,128)(2,1)}, bf16[4,256,384]{2,1,0:T(8,128)(2,1)S(1)}, u32[]{:S(2)}, u32[]{:S(2)}) collective-permute-start(bf16[4,256,384]{2,1,0:T(8,128)(2,1)} %get-tuple-element.36), channel_id=1, source_target_pairs={{0,8},{1,9},{2,10},{3,11},{4,12},{5,13},{6,14},{7,15},{8,0},{9,1},... | collective-permute-start | bytes 2359304 | tf_op jit(solution)/shard_map/ppermute | solution.py:247
  11.3 21.3 %collective-permute-start = (bf16[4,384,256]{2,1,0:T(8,128)(2,1)}, bf16[4,384,256]{2,1,0:T(8,128)(2,1)S(1)}, u32[]{:S(2)}, u32[]{:S(2)}) collective-permute-start(bf16[4,384,256]{2,1,0:T(8,128)(2,1)} %get-tuple-element.32), channel_id=1, source_target_pairs={{0,8},{1,9},{2,10},{3,11},{4,12},{5,13},{6,14},{7,15},{8,0},{9,1},... | collective-permute-start | bytes 2359304 | tf_op jit(solution)/shard_map/ppermute | solution.py:247
  18.3 11.0 %collective-permute-start.26 = (bf16[80,2048]{1,0:T(8,128)(2,1)S(1)}, bf16[80,2048]{1,0:T(8,128)(2,1)S(1)}, u32[]{:S(2)}, u32[]{:S(2)}) collective-permute-start(bf16[80,2048]{1,0:T(8,128)(2,1)S(1)} %get-tuple-element.40), channel_id=1, source_target_pairs={{0,2},{1,3},{2,0},{3,1},{4,6},{5,7},{6,4},{7,5},{8,10},{9,11},{10,... | collective-permute-start | bytes 983048 | tf_op jit(solution)/shard_map/ppermute | solution.py:247
  22.4 28.1 %collective-permute-start.34 = (bf16[2,256,384]{2,1,0:T(8,128)(2,1)S(1)}, bf16[2,256,384]{2,1,0:T(8,128)(2,1)S(1)}, u32[]{:S(2)}, u32[]{:S(2)}) collective-permute-start(bf16[2,256,384]{2,1,0:T(8,128)(2,1)S(1)} %shard_map.80), channel_id=1, source_target_pairs={{0,16},{1,17},{2,18},{3,19},{4,20},{5,21},{6,22},{7,23},{8,24},{9,... | collective-permute-start | bytes 1179656 | tf_op jit(solution)/shard_map/ppermute | solution.py:247
  23.9 24.5 %collective-permute-start.27 = (bf16[80,2048]{1,0:T(8,128)(2,1)S(1)}, bf16[80,2048]{1,0:T(8,128)(2,1)S(1)}, u32[]{:S(2)}, u32[]{:S(2)}) collective-permute-start(bf16[80,2048]{1,0:T(8,128)(2,1)S(1)} %get-tuple-element.41), channel_id=1, source_target_pairs={{0,16},{1,17},{2,18},{3,19},{4,20},{5,21},{6,22},{7,23},{8,24},{9,... | collective-permute-start | bytes 983048 | tf_op jit(solution)/shard_map/ppermute | solution.py:247
  29.3 20.7 %collective-permute-start.28 = (bf16[80,2048]{1,0:T(8,128)(2,1)S(1)}, bf16[80,2048]{1,0:T(8,128)(2,1)S(1)}, u32[]{:S(2)}, u32[]{:S(2)}) collective-permute-start(bf16[80,2048]{1,0:T(8,128)(2,1)S(1)} %get-tuple-element.42), channel_id=1, source_target_pairs={{0,18},{1,19},{2,16},{3,17},{4,22},{5,23},{6,20},{7,21},{8,26},{9,... | collective-permute-start | bytes 983048 | tf_op jit(solution)/shard_map/ppermute | solution.py:247
  32.0 18.0 %collective-permute-start.29 = (bf16[80,2048]{1,0:T(8,128)(2,1)S(1)}, bf16[80,2048]{1,0:T(8,128)(2,1)S(1)}, u32[]{:S(2)}, u32[]{:S(2)}) collective-permute-start(bf16[80,2048]{1,0:T(8,128)(2,1)S(1)} %get-tuple-element.39.refs_8_), channel_id=1, source_target_pairs={{0,8},{1,9},{2,10},{3,11},{4,12},{5,13},{6,14},{7,15},{8,0},{9,1},... | collective-permute-start | bytes 983048 | tf_op jit(solution)/shard_map/ppermute | solution.py:247
  32.6 24.3 %collective-permute-start.18 = (bf16[2,256,384]{2,1,0:T(8,128)(2,1)S(1)}, bf16[2,256,384]{2,1,0:T(8,128)(2,1)S(1)}, u32[]{:S(2)}, u32[]{:S(2)}) collective-permute-start(bf16[2,256,384]{2,1,0:T(8,128)(2,1)S(1)} %shard_map.77), channel_id=1, source_target_pairs={{0,16},{1,17},{2,18},{3,19},{4,20},{5,21},{6,22},{7,23},{8,24},{9,... | collective-permute-start | bytes 1179656 | tf_op jit(solution)/shard_map/ppermute | solution.py:247
  48.5 15.9 %collective-permute-start.1 = (bf16[2,384,256]{2,1,0:T(8,128)(2,1)S(1)}, bf16[2,384,256]{2,1,0:T(8,128)(2,1)S(1)}, u32[]{:S(2)}, u32[]{:S(2)}) collective-permute-start(bf16[2,384,256]{2,1,0:T(8,128)(2,1)S(1)} %shard_map.75), channel_id=1, source_target_pairs={{0,16},{1,17},{2,18},{3,19},{4,20},{5,21},{6,22},{7,23},{8,24},{9,... | collective-permute-start | bytes 1179656 | tf_op jit(solution)/shard_map/ppermute | solution.py:247
  50.5 11.5 %collective-permute-start.32 = (bf16[80,2048]{1,0:T(8,128)(2,1)S(1)}, bf16[80,2048]{1,0:T(8,128)(2,1)S(1)}, u32[]{:S(2)}, u32[]{:S(2)}) collective-permute-start(bf16[80,2048]{1,0:T(8,128)(2,1)S(1)} %collective-permute-done.28.refs_11_), channel_id=1, source_target_pairs={{0,8},{1,9},{2,10},{3,11},{4,12},{5,13},{6,14},{7,15},{8,0},{9,1},... | collective-permute-start | bytes 983048 | tf_op jit(solution)/shard_map/ppermute | solution.py:247
  60.0 14.9 %collective-permute-start.36 = (bf16[256,384]{1,0:T(8,128)(2,1)S(1)}, bf16[256,384]{1,0:T(8,128)(2,1)S(1)}, u32[]{:S(2)}, u32[]{:S(2)}) collective-permute-start(bf16[256,384]{1,0:T(8,128)(2,1)S(1)} %get-tuple-element.46), channel_id=1, source_target_pairs={{0,2},{1,3},{2,0},{3,1},{4,6},{5,7},{6,4},{7,5},{8,10},{9,11},{10,... | collective-permute-start | bytes 589832 | tf_op jit(solution)/shard_map/ppermute | solution.py:247
  60.8 22.0 %collective-permute-start.38 = (bf16[256,384]{1,0:T(8,128)(2,1)S(1)}, bf16[256,384]{1,0:T(8,128)(2,1)S(1)}, u32[]{:S(2)}, u32[]{:S(2)}) collective-permute-start(bf16[256,384]{1,0:T(8,128)(2,1)S(1)} %get-tuple-element.46), channel_id=1, source_target_pairs={{0,4},{1,5},{2,6},{3,7},{4,0},{5,1},{6,2},{7,3},{8,12},{9,13},{10,... | collective-permute-start | bytes 589832 | tf_op jit(solution)/shard_map/ppermute | solution.py:247
  62.0 22.3 %collective-permute-start.35 = (bf16[256,384]{1,0:T(8,128)(2,1)S(1)}, bf16[256,384]{1,0:T(8,128)(2,1)S(1)}, u32[]{:S(2)}, u32[]{:S(2)}) collective-permute-start(bf16[256,384]{1,0:T(8,128)(2,1)S(1)} %get-tuple-element.45.refs_0_), channel_id=1, source_target_pairs={{0,1},{1,0},{2,3},{3,2},{4,5},{5,4},{6,7},{7,6},{8,9},{9,8},{10,11... | collective-permute-start | bytes 589832 | tf_op jit(solution)/shard_map/ppermute | solution.py:247
  64.4 22.4 %collective-permute-start.24 = (bf16[256,384]{1,0:T(8,128)(2,1)S(1)}, bf16[256,384]{1,0:T(8,128)(2,1)S(1)}, u32[]{:S(2)}, u32[]{:S(2)}) collective-permute-start(bf16[256,384]{1,0:T(8,128)(2,1)S(1)} %get-tuple-element.37.refs_0_), channel_id=1, source_target_pairs={{0,6},{1,7},{2,4},{3,5},{4,2},{5,3},{6,0},{7,1},{8,14},{9,15},{10,... | collective-permute-start | bytes 589832 | tf_op jit(solution)/shard_map/ppermute | solution.py:247
  66.9 30.1 %collective-permute-start.20 = (bf16[256,384]{1,0:T(8,128)(2,1)S(1)}, bf16[256,384]{1,0:T(8,128)(2,1)S(1)}, u32[]{:S(2)}, u32[]{:S(2)}) collective-permute-start(bf16[256,384]{1,0:T(8,128)(2,1)S(1)} %get-tuple-element.38), channel_id=1, source_target_pairs={{0,2},{1,3},{2,0},{3,1},{4,6},{5,7},{6,4},{7,5},{8,10},{9,11},{10,... | collective-permute-start | bytes 589832 | tf_op jit(solution)/shard_map/ppermute | solution.py:247
  74.9 24.7 %collective-permute-start.22 = (bf16[256,384]{1,0:T(8,128)(2,1)S(1)}, bf16[256,384]{1,0:T(8,128)(2,1)S(1)}, u32[]{:S(2)}, u32[]{:S(2)}) collective-permute-start(bf16[256,384]{1,0:T(8,128)(2,1)S(1)} %get-tuple-element.38), channel_id=1, source_target_pairs={{0,4},{1,5},{2,6},{3,7},{4,0},{5,1},{6,2},{7,3},{8,12},{9,13},{10,... | collective-permute-start | bytes 589832 | tf_op jit(solution)/shard_map/ppermute | solution.py:247
  82.8 20.5 %collective-permute-start.19 = (bf16[256,384]{1,0:T(8,128)(2,1)S(1)}, bf16[256,384]{1,0:T(8,128)(2,1)S(1)}, u32[]{:S(2)}, u32[]{:S(2)}) collective-permute-start(bf16[256,384]{1,0:T(8,128)(2,1)S(1)} %get-tuple-element.37.refs_0_), channel_id=1, source_target_pairs={{0,1},{1,0},{2,3},{3,2},{4,5},{5,4},{6,7},{7,6},{8,9},{9,8},{10,11... | collective-permute-start | bytes 589832 | tf_op jit(solution)/shard_map/ppermute | solution.py:247
  84.3 19.0 %collective-permute-start.13 = (bf16[384,256]{1,0:T(8,128)(2,1)S(1)}, bf16[384,256]{1,0:T(8,128)(2,1)S(1)}, u32[]{:S(2)}, u32[]{:S(2)}) collective-permute-start(bf16[384,256]{1,0:T(8,128)(2,1)S(1)} %get-tuple-element.33.refs_0_), channel_id=1, source_target_pairs={{0,6},{1,7},{2,4},{3,5},{4,2},{5,3},{6,0},{7,1},{8,14},{9,15},{10,... | collective-permute-start | bytes 589832 | tf_op jit(solution)/shard_map/ppermute | solution.py:247
  86.8 22.4 %collective-permute-start.9 = (bf16[384,256]{1,0:T(8,128)(2,1)S(1)}, bf16[384,256]{1,0:T(8,128)(2,1)S(1)}, u32[]{:S(2)}, u32[]{:S(2)}) collective-permute-start(bf16[384,256]{1,0:T(8,128)(2,1)S(1)} %get-tuple-element.34), channel_id=1, source_target_pairs={{0,4},{1,5},{2,6},{3,7},{4,0},{5,1},{6,2},{7,3},{8,12},{9,13},{10,... | collective-permute-start | bytes 589832 | tf_op jit(solution)/shard_map/ppermute | solution.py:247
  97.0 13.6 %collective-permute-start.5 = (bf16[384,256]{1,0:T(8,128)(2,1)S(1)}, bf16[384,256]{1,0:T(8,128)(2,1)S(1)}, u32[]{:S(2)}, u32[]{:S(2)}) collective-permute-start(bf16[384,256]{1,0:T(8,128)(2,1)S(1)} %get-tuple-element.34), channel_id=1, source_target_pairs={{0,2},{1,3},{2,0},{3,1},{4,6},{5,7},{6,4},{7,5},{8,10},{9,11},{10,... | collective-permute-start | bytes 589832 | tf_op jit(solution)/shard_map/ppermute | solution.py:247
  99.7 11.5 %collective-permute-start.3 = (bf16[384,256]{1,0:T(8,128)(2,1)S(1)}, bf16[384,256]{1,0:T(8,128)(2,1)S(1)}, u32[]{:S(2)}, u32[]{:S(2)}) collective-permute-start(bf16[384,256]{1,0:T(8,128)(2,1)S(1)} %get-tuple-element.33.refs_0_), channel_id=1, source_target_pairs={{0,1},{1,0},{2,3},{3,2},{4,5},{5,4},{6,7},{7,6},{8,9},{9,8},{10,11... | collective-permute-start | bytes 589832 | tf_op jit(solution)/shard_map/ppermute | solution.py:247
  111.2 14.2 %collective-permute-start.25 = (bf16[256,384]{1,0:T(8,128)(2,1)S(1)}, bf16[256,384]{1,0:T(8,128)(2,1)S(1)}, u32[]{:S(2)}, u32[]{:S(2)}) collective-permute-start(bf16[256,384]{1,0:T(8,128)(2,1)S(1)} %collective-permute-done.24.refs_6_), channel_id=1, source_target_pairs={{0,1},{1,0},{2,3},{3,2},{4,5},{5,4},{6,7},{7,6},{8,9},{9,8},{10,11... | collective-permute-start | bytes 589832 | tf_op jit(solution)/shard_map/ppermute | solution.py:247
  112.7 16.9 %collective-permute-start.21 = (bf16[256,384]{1,0:T(8,128)(2,1)S(1)}, bf16[256,384]{1,0:T(8,128)(2,1)S(1)}, u32[]{:S(2)}, u32[]{:S(2)}) collective-permute-start(bf16[256,384]{1,0:T(8,128)(2,1)S(1)} %collective-permute-done.20.refs_2_), channel_id=1, source_target_pairs={{0,1},{1,0},{2,3},{3,2},{4,5},{5,4},{6,7},{7,6},{8,9},{9,8},{10,11... | collective-permute-start | bytes 589832 | tf_op jit(solution)/shard_map/ppermute | solution.py:247
  113.2 20.6 %collective-permute-start.23 = (bf16[256,384]{1,0:T(8,128)(2,1)S(1)}, bf16[256,384]{1,0:T(8,128)(2,1)S(1)}, u32[]{:S(2)}, u32[]{:S(2)}) collective-permute-start(bf16[256,384]{1,0:T(8,128)(2,1)S(1)} %collective-permute-done.22.refs_4_), channel_id=1, source_target_pairs={{0,1},{1,0},{2,3},{3,2},{4,5},{5,4},{6,7},{7,6},{8,9},{9,8},{10,11... | collective-permute-start | bytes 589832 | tf_op jit(solution)/shard_map/ppermute | solution.py:247
  116.9 21.1 %collective-permute-start.15 = (bf16[384,256]{1,0:T(8,128)(2,1)S(1)}, bf16[384,256]{1,0:T(8,128)(2,1)S(1)}, u32[]{:S(2)}, u32[]{:S(2)}) collective-permute-start(bf16[384,256]{1,0:T(8,128)(2,1)S(1)} %collective-permute-done.13.refs_12_), channel_id=1, source_target_pairs={{0,1},{1,0},{2,3},{3,2},{4,5},{5,4},{6,7},{7,6},{8,9},{9,8},{10,11... | collective-permute-start | bytes 589832 | tf_op jit(solution)/shard_map/ppermute | solution.py:247
  121.1 24.4 %collective-permute-start.14 = (bf16[384,256]{1,0:T(8,128)(2,1)S(1)}, bf16[384,256]{1,0:T(8,128)(2,1)S(1)}, u32[]{:S(2)}, u32[]{:S(2)}) collective-permute-start(bf16[384,256]{1,0:T(8,128)(2,1)S(1)} %collective-permute-done.13.refs_12_), channel_id=1, source_target_pairs={{0,8},{1,9},{2,10},{3,11},{4,12},{5,13},{6,14},{7,15},{8,0},{9,1},... | collective-permute-start | bytes 589832 | tf_op jit(solution)/shard_map/ppermute | solution.py:247
  125.3 20.8 %collective-permute-start.11 = (bf16[384,256]{1,0:T(8,128)(2,1)S(1)}, bf16[384,256]{1,0:T(8,128)(2,1)S(1)}, u32[]{:S(2)}, u32[]{:S(2)}) collective-permute-start(bf16[384,256]{1,0:T(8,128)(2,1)S(1)} %collective-permute-done.9.refs_8_), channel_id=1, source_target_pairs={{0,1},{1,0},{2,3},{3,2},{4,5},{5,4},{6,7},{7,6},{8,9},{9,8},{10,11... | collective-permute-start | bytes 589832 | tf_op jit(solution)/shard_map/ppermute | solution.py:247
  129.6 17.2 %collective-permute-start.10 = (bf16[384,256]{1,0:T(8,128)(2,1)S(1)}, bf16[384,256]{1,0:T(8,128)(2,1)S(1)}, u32[]{:S(2)}, u32[]{:S(2)}) collective-permute-start(bf16[384,256]{1,0:T(8,128)(2,1)S(1)} %collective-permute-done.9.refs_8_), channel_id=1, source_target_pairs={{0,8},{1,9},{2,10},{3,11},{4,12},{5,13},{6,14},{7,15},{8,0},{9,1},... | collective-permute-start | bytes 589832 | tf_op jit(solution)/shard_map/ppermute | solution.py:247
  133.8 12.4 %collective-permute-start.7 = (bf16[384,256]{1,0:T(8,128)(2,1)S(1)}, bf16[384,256]{1,0:T(8,128)(2,1)S(1)}, u32[]{:S(2)}, u32[]{:S(2)}) collective-permute-start(bf16[384,256]{1,0:T(8,128)(2,1)S(1)} %collective-permute-done.5.refs_4_), channel_id=1, source_target_pairs={{0,1},{1,0},{2,3},{3,2},{4,5},{5,4},{6,7},{7,6},{8,9},{9,8},{10,11... | collective-permute-start | bytes 589832 | tf_op jit(solution)/shard_map/ppermute | solution.py:247
  151.3 15.7 %collective-permute-start.44 = (bf16[80,2048]{1,0:T(8,128)(2,1)S(1)}, bf16[80,2048]{1,0:T(8,128)(2,1)S(1)}, u32[]{:S(2)}, u32[]{:S(2)}) collective-permute-start(bf16[80,2048]{1,0:T(8,128)(2,1)S(1)} %get-tuple-element.51), channel_id=1, source_target_pairs={{0,16},{1,17},{2,18},{3,19},{4,20},{5,21},{6,22},{7,23},{8,24},{9,... | collective-permute-start | bytes 983048 | tf_op jit(solution)/shard_map/ppermute | solution.py:247
  152.8 15.5 %collective-permute-start.45 = (bf16[80,2048]{1,0:T(8,128)(2,1)S(1)}, bf16[80,2048]{1,0:T(8,128)(2,1)S(1)}, u32[]{:S(2)}, u32[]{:S(2)}) collective-permute-start(bf16[80,2048]{1,0:T(8,128)(2,1)S(1)} %get-tuple-element.52), channel_id=1, source_target_pairs={{0,18},{1,19},{2,16},{3,17},{4,22},{5,23},{6,20},{7,21},{8,26},{9,... | collective-permute-start | bytes 983048 | tf_op jit(solution)/shard_map/ppermute | solution.py:247
  (25 other events, 136.8 us)
where the time goes:
time: 172 us
  waiting for transfers between devices  75.3 us (44%)
  starting transfers between devices  61.3 us (36%)
  Pallas kernels  27.2 us (16%)
  local copies, waits for them, and re-layouts  8.09 us (5%)
    ppermute x46, waiting for transfers between devices, swap(): return lax.ppermute(value, AXES, pairs)  75.3 us
    ppermute x46, starting transfers between devices, swap(): return lax.ppermute(value, AXES, pairs)  61.3 us
    pallas_call x12, Pallas kernels, call(): pl.pallas_call(kernel, out_shape=out_shape, in_specs=in_specs, out_specs=...  23.3 us
    unnamed x24, local copies, waits for them, and re-layouts  8.09 us
    pallas_call x1, Pallas kernels, merge(): pl.pallas_call(merge_kernel, grid=(width // tile,), out_shape=jax.ShapeDt...  3.82 us
  transfers between devices with their start and end apart: 46, of which 20 were waited for; matrix products, arithmetic and copies ran while one was open for 1% of the time, Pallas kernels for 11%

commit v1 on v0

--- a/solution.py
+++ b/solution.py
@@ -14,6 +14,8 @@
 F32 = jnp.float32
 BF16 = jnp.bfloat16
 
+
+STEPS = (((1,), (0,)), ((1, 0),), ((1, 0),))
 
 VMEM = pl.BlockSpec(memory_space=pltpu.VMEM)
 SMEM = pl.BlockSpec(memory_space=pltpu.SMEM)
@@ -45,7 +47,7 @@
 
 
 def pick_kernel(sides, visited, routing, mixing, tokens, *outs):
-    picks, high, low = outs[:VISITS], outs[VISITS], outs[VISITS + 1]
+    picks, split = outs[:VISITS], outs[VISITS]
     _, _, x, _, _, ab = place(sides)
     rows = tokens.shape[0]
     lanes = lax.broadcasted_iota(jnp.int32, (rows, 128), 1)
@@ -67,9 +69,8 @@
     spread = jnp.zeros((rows, VISITS * CAP), F32)
     for k in range(VISITS):
         spread = spread + jnp.where(slots == places[:, k : k + 1], shares[k], 0.0)
-    top = spread.astype(BF16)
-    high[...] = top
-    low[...] = (spread - top.astype(F32)).astype(BF16)
+    top = spread.astype(BF16).astype(F32)
+    split[...] = jnp.concatenate([top, spread - top], axis=1).astype(BF16)
     across = places.T
     slots = lax.broadcasted_iota(jnp.int32, (CAP, rows), 0).astype(F32)
     for k in range(VISITS):
@@ -77,27 +78,33 @@
         picks[k][...] = jnp.dot(one, tokens[...], preferred_element_type=F32).astype(BF16)
 
 
-def merge_kernel(high, low, *refs):
-    pieces, out = refs[:VISITS], refs[VISITS]
-    values = jnp.concatenate([piece[...] for piece in pieces], axis=0)
-    total = jnp.dot(high[...], values, preferred_element_type=F32)
-    total = total + jnp.dot(low[...], values, preferred_element_type=F32)
-    out[...] = total.astype(BF16)
-
-
-def merge(high, low, pieces):
-    rows, width = high.shape[0], pieces[0].shape[1]
-    tile = 512
-    whole = pl.BlockSpec(high.shape, lambda i: (0, 0))
+def merge_kernel(half, shares, *refs):
+    pieces, out = refs[:VISITS], refs[-1]
+    values = jnp.concatenate([piece[...] for piece in pieces] * 2, axis=0)
+    out[...] = jnp.dot(shares[...], values, preferred_element_type=F32).astype(BF16)
+
+
+def merge(half, shares, pieces, before):
+    rows, (slots, width) = shares.shape[0], pieces[0].shape
+    tile = width // 2
+    ins = [pl.BlockSpec(shares.shape, lambda i, half: (0, 0))]
+    ins += [pl.BlockSpec((slots, tile), lambda i, half: (0, i))] * VISITS
+    args = [half, shares, *pieces]
+    if before is not None:
+        ins.append(ANY)
+        args.append(before)
     return pl.pallas_call(
         merge_kernel,
-        grid=(width // tile,),
-        out_shape=jax.ShapeDtypeStruct((rows, width), BF16),
-        in_specs=[whole, whole] + [pl.BlockSpec((CAP, tile), lambda i: (0, i))] * VISITS,
-        out_specs=pl.BlockSpec((rows, tile), lambda i: (0, i)),
+        grid_spec=pltpu.PrefetchScalarGridSpec(
+            num_scalar_prefetch=1,
+            grid=(width // tile,),
+            in_specs=ins,
+            out_specs=pl.BlockSpec((rows, tile), lambda i, half: (0, half[0] * (width // tile) + i)),
+        ),
+        out_shape=jax.ShapeDtypeStruct((rows, 2 * width), BF16),
+        input_output_aliases={} if before is None else {len(args) - 1: 0},
         compiler_params=pltpu.CompilerParams(vmem_limit_bytes=16 << 20),
-        name="merge",
-    )(high, low, *pieces)
+    )(*args)
 
 
 def cut_kernel(sides, held, axes, visited, *refs):
@@ -131,7 +138,7 @@
         functools.partial(cut_kernel, sides, matrices[0].shape[0], axes),
         shapes,
         [SMEM] + [HBM] * len(matrices),
-        (visited, *matrices),
+        (visited, *(pltpu.with_memory_space_constraint(matrix, pltpu.HBM) for matrix in matrices)),
         [pltpu.SemaphoreType.DMA((2 * VISITS * len(matrices),))],
     )
 
@@ -155,16 +162,16 @@
         choose(own, theirs_out.at[k], theirs.at[k], got.at[VISITS + k])
 
 
-def send_kernel(sides, held, visited, mine, got, out):
+def send_kernel(sides, held, ks, visited, mine, got, out):
     _, c, x, _, _, ab = place(sides)
-    for k in range(2):
+    for n, k in enumerate(ks):
         owner = visited[visit(2 + k, x, ab)] // held
-        choose((owner & 1) == c, out.at[k], mine.at[2 + k], got.at[2 + k])
-
-
-def keep_kernel(sides, held, visited, mine, got, far, same, other):
+        choose((owner & 1) == c, out.at[n], mine.at[2 + k], got.at[2 + k])
+
+
+def keep_kernel(sides, held, ks, visited, mine, got, far, *outs):
     _, c, x, _, _, ab = place(sides)
-    for k, out in enumerate((same, other)):
+    for n, (k, out) in enumerate(zip(ks, outs)):
         owner = visited[visit(k, x, ab)] // held
         near = ((owner >> 1) & 1) == x
 
@@ -174,7 +181,7 @@
 
         @pl.when(jnp.logical_not(near))
         def _():
-            out[...] = far[k]
+            out[...] = far[n]
 
 
 def load_blocks(sides, keys, blocks, held, sem, down):
@@ -184,6 +191,7 @@
         piece = (z ^ plane_bits) * sides + (y ^ side_bits)
         rows, columns = block.shape
         if down:
+            piece = lax.rem(piece, 2 * sides)
             first = pl.ds(pl.multiple_of((c ^ core) * rows, 128), rows)
             spot = held.at[first, pl.ds(pl.multiple_of(piece * columns, 128), columns)]
         else:
@@ -264,24 +272,25 @@
             bit *= 2
         matrices.append((mine, swap(theirs, expert_bits=1)))
 
-    *picked, high, low = call(
+    *picked, shares = call(
         functools.partial(pick_kernel, sides),
-        [shape((CAP, width), BF16)] * VISITS + [shape((count, total), BF16)] * 2,
+        [shape((CAP, width), BF16)] * VISITS + [shape((count, 2 * total), BF16)],
         [SMEM, VMEM, VMEM, VMEM],
         (visited, routing, mixing, tokens),
         limit=24,
     )
 
     sent = []
-    for mine, got in matrices:
-        block = mine.shape[1:]
-        away = call(
-            functools.partial(send_kernel, sides, held),
-            shape((2, *block), BF16),
-            [SMEM, VMEM, VMEM],
-            (visited, mine, got),
-        )
-        sent.append(swap(away, expert_bits=2))
+    for n, (mine, got) in enumerate(matrices):
+        sent.append({})
+        for ks in STEPS[n]:
+            away = call(
+                functools.partial(send_kernel, sides, held, ks),
+                shape((len(ks), *mine.shape[1:]), BF16),
+                [SMEM, VMEM, VMEM],
+                (visited, mine, got),
+            )
+            sent[n][ks] = swap(away, expert_bits=2)
     rows = [
         picked[0],
         swap(picked[1], plane_bits=1),
@@ -291,13 +300,16 @@
 
     pieces = []
     for n, (mine, got) in enumerate(matrices):
-        block = mine.shape[1:]
-        same, other = call(
-            functools.partial(keep_kernel, sides, held),
-            [shape(block, BF16)] * 2,
-            [SMEM] + [VMEM] * 3,
-            (visited, mine, got, sent[n]),
-        )
+        kept = {}
+        for ks, far in sent[n].items():
+            outs = call(
+                functools.partial(keep_kernel, sides, held, ks),
+                [shape(mine.shape[1:], BF16)] * len(ks),
+                [SMEM] + [VMEM] * 3,
+                (visited, mine, got, far),
+            )
+            kept.update(zip(ks, outs))
+        same, other = kept[0], kept[1]
         found = [
             (0, same), (1, swap(other, plane_bits=1)), (2, swap(other, plane_bits=2)), (3, swap(same, plane_bits=3))
         ]
@@ -336,22 +348,30 @@
     )
     partner = swap(partner, expert_bits=1)
     keys, blocks = pieces[2]
-    outs = call(
-        functools.partial(down_kernel, sides, keys),
-        [shape((CAP, width), BF16)] * VISITS,
-        [ANY] * len(keys) + [VMEM] * 2,
-        (*blocks, own, partner),
-        [
-            pltpu.VMEM((inner, width), BF16),
-            pltpu.VMEM((total, inner), BF16),
-            pltpu.SemaphoreType.DMA((len(keys),)),
-        ],
-        flops=work,
-    )
-    back = [
-        outs[0], swap(outs[1], plane_bits=1), swap(outs[2], expert_bits=2), swap(outs[3], expert_bits=2, plane_bits=1)
-    ]
-    return merge(high, low, back)
+    combined = None
+    for part in range(2):
+        chosen = [n for n, key in enumerate(keys) if key[0] // 2 == part]
+        outs = call(
+            functools.partial(down_kernel, sides, [keys[n] for n in chosen]),
+            [shape((CAP, width // 2), BF16)] * VISITS,
+            [ANY] * len(chosen) + [VMEM] * 2,
+            (*(blocks[n] for n in chosen), own, partner),
+            [
+                pltpu.VMEM((inner, width // 2), BF16),
+                pltpu.VMEM((total, inner), BF16),
+                pltpu.SemaphoreType.DMA((len(chosen),)),
+            ],
+            flops=work // 2,
+        )
+        back = [
+            outs[0],
+            swap(outs[1], plane_bits=1),
+            swap(outs[2], expert_bits=2),
+            swap(outs[3], expert_bits=2, plane_bits=1),
+        ]
+        half = (lax.axis_index("group") // sides // 2) ^ part
+        combined = merge(half.reshape(1), shares, back, combined)
+    return combined
 
 
 def solution(mesh):

time: 172 us -> 146 us (0.85)
  waiting for transfers between devices: 75.3 us -> 58 us
  starting transfers between devices: 61.3 us -> 52.2 us
  local copies, waits for them, and re-layouts: 8.09 us -> 5.05 us
  Pallas kernels: 27.2 us -> 29.8 us
    ppermute x46 -> x50, waiting for transfers between devices: 75.3 us -> 58 us  [swap(): return lax.ppermute(value, AXES, pairs)]
    ppermute x46 -> x50, starting transfers between devices: 61.3 us -> 52.2 us  [swap(): return lax.ppermute(value, AXES, pairs)]
    unnamed x24 -> x22, local copies, waits for them, and re-layouts: 8.09 us -> 5.05 us
    pallas_call x12 -> x15, Pallas kernels: 23.3 us -> 25.7 us  [call(): pl.pallas_call(kernel, out_shape=out_shape, in_specs=in_specs, out_specs=...]
    pallas_call x1 -> x2, Pallas kernels: 3.82 us -> 4.07 us  [merge(): pl.pallas_call(merge_kernel, grid_spec=pltpu.PrefetchScalarGridSpec(num_s...]
  transfers between devices with their start and end apart: 46 -> 50, of which waited for: 20 -> 23; matrix products, arithmetic and copies ran while one was open for 1% -> 1% of each run, Pallas kernels for 11% -> 17%
where the time goes in v1:
time: 146 us; the launch traced here: 145 us
  waiting for transfers between devices  58 us (40%)
  starting transfers between devices  52.2 us (36%)
  Pallas kernels  29.8 us (20%)
  local copies, waits for them, and re-layouts  5.05 us (3%)
    ppermute x50, waiting for transfers between devices, swap(): return lax.ppermute(value, AXES, pairs)  58 us
    ppermute x50, starting transfers between devices, swap(): return lax.ppermute(value, AXES, pairs)  52.2 us
    pallas_call x15, Pallas kernels, call(): pl.pallas_call(kernel, out_shape=out_shape, in_specs=in_specs, out_specs=...  25.7 us
    unnamed x22, local copies, waits for them, and re-layouts  5.05 us
    pallas_call x2, Pallas kernels, merge(): pl.pallas_call(merge_kernel, grid_spec=pltpu.PrefetchScalarGridSpec(num_s...  4.07 us
  transfers between devices with their start and end apart: 50, of which 23 were waited for; matrix products, arithmetic and copies ran while one was open for 1% of the time, Pallas kernels for 17%

profile of v1, /device:TPU:0, one launch (start us, length us, event | category | flops | bytes accessed | tf_op | source)
XLA Modules:
  0.0 145.4 jit_solution(14623959744908761571)
XLA Ops:
  0.7 3.0 %shard_map.79 = (bf16[4,256,384]{2,1,0:T(8,128)(2,1)S(1)}, bf16[4,256,384]{2,1,0:T(8,128)(2,1)}) custom-call(s32[4]{0:T(128)S(1)} %copy-done.6, bf16[8,256,768]{2,1,0:T(8,128)(2,1)} %refs_0_.3), custom_call_target="tpu_custom_call" | custom-call | tf_op jit(solution)/shard_map/pallas_call | solution.py:38
  4.3 3.8 %shard_map.74 = (bf16[4,256,384]{2,1,0:T(8,128)(2,1)S(1)}, bf16[4,256,384]{2,1,0:T(8,128)(2,1)}, bf16[4,384,256]{2,1,0:T(8,128)(2,1)S(1)}, bf16[4,384,256]{2,1,0:T(8,128)(2,1)}) custom-call(s32[4]{0:T(128)S(1)} %copy-done.6, bf16[8,256,768]{2,1,0:T(8,128)(2,1)} %refs_0_.2, bf16[8,768,256]{2,1,0:T(8,128)(2,1)} %refs_1_.1), custom_call_target="tpu_custom_call" | custom-call | tf_op jit(solution)/shard_map/pallas_call | solution.py:38
  10.4 1.6 %copy-done.4 = bf16[512,2048]{1,0:T(8,128)(2,1)S(1)} copy-done((bf16[512,2048]{1,0:T(8,128)(2,1)S(1)}, bf16[512,2048]{1,0:T(8,128)(2,1)}, u32[]{:S(2)}) %copy-start.4) | copy-done | bytes 2097176
  13.0 3.2 %shard_map.73 = (bf16[80,2048]{1,0:T(8,128)(2,1)S(1)}, bf16[80,2048]{1,0:T(8,128)(2,1)S(1)}, bf16[80,2048]{1,0:T(8,128)(2,1)S(1)}, bf16[80,2048]{1,0:T(8,128)(2,1)S(1)}, bf16[512,640]{1,0:T(8,128)(2,1)S(1)}) custom-call(s32[4]{0:T(128)S(1)} %copy-done.7, s32[512,8]{1,0:T(8,128)S(1)} %copy-done.5, f32[512,8]{1,0:T(8,128)S(1)} %copy.10.mixing, ...), custom_call_target="tpu_custom_call" | custom-call | tf_op jit(solution)/shard_map/pallas_call | solution.py:38
  16.2 2.6 %collective-permute-start.19 = (bf16[80,2048]{1,0:T(8,128)(2,1)S(1)}, bf16[80,2048]{1,0:T(8,128)(2,1)S(1)}, u32[]{:S(2)}, u32[]{:S(2)}) collective-permute-start(bf16[80,2048]{1,0:T(8,128)(2,1)S(1)} %get-tuple-element.40), channel_id=1, source_target_pairs={{0,2},{1,3},{2,0},{3,1},{4,6},{5,7},{6,4},{7,5},{8,10},{9,11},{10,... | collective-permute-start | bytes 983048 | tf_op jit(solution)/shard_map/ppermute | solution.py:255
  20.4 6.9 %collective-permute-done.19.refs_9_ = bf16[80,2048]{1,0:T(8,128)(2,1)S(1)} collective-permute-done((bf16[80,2048]{1,0:T(8,128)(2,1)S(1)}, bf16[80,2048]{1,0:T(8,128)(2,1)S(1)}, u32[]{:S(2)}, u32[]{:S(2)}) %collective-permute-start.19) | collective-permute-done | bytes 327712 | tf_op jit(solution)/shard_map/ppermute | solution.py:255
  27.2 2.7 %collective-permute-start.21 = (bf16[80,2048]{1,0:T(8,128)(2,1)S(1)}, bf16[80,2048]{1,0:T(8,128)(2,1)S(1)}, u32[]{:S(2)}, u32[]{:S(2)}) collective-permute-start(bf16[80,2048]{1,0:T(8,128)(2,1)S(1)} %get-tuple-element.42), channel_id=1, source_target_pairs={{0,18},{1,19},{2,16},{3,17},{4,22},{5,23},{6,20},{7,21},{8,26},{9,... | collective-permute-start | bytes 983048 | tf_op jit(solution)/shard_map/ppermute | solution.py:255
  29.9 7.8 %collective-permute-done.21.refs_11_ = bf16[80,2048]{1,0:T(8,128)(2,1)S(1)} collective-permute-done((bf16[80,2048]{1,0:T(8,128)(2,1)S(1)}, bf16[80,2048]{1,0:T(8,128)(2,1)S(1)}, u32[]{:S(2)}, u32[]{:S(2)}) %collective-permute-start.21) | collective-permute-done | bytes 327712 | tf_op jit(solution)/shard_map/ppermute | solution.py:255
  42.9 3.8 %collective-permute-done.27.far = bf16[1,256,384]{2,1,0:T(8,128)(2,1)S(1)} collective-permute-done((bf16[1,256,384]{2,1,0:T(8,128)(2,1)S(1)}, bf16[1,256,384]{2,1,0:T(8,128)(2,1)S(1)}, u32[]{:S(2)}, u32[]{:S(2)}) %collective-permute-start.27) | collective-permute-done | bytes 196640 | tf_op jit(solution)/shard_map/ppermute | solution.py:255
  48.7 2.2 %collective-permute-done.29.far = bf16[1,256,384]{2,1,0:T(8,128)(2,1)S(1)} collective-permute-done((bf16[1,256,384]{2,1,0:T(8,128)(2,1)S(1)}, bf16[1,256,384]{2,1,0:T(8,128)(2,1)S(1)}, u32[]{:S(2)}, u32[]{:S(2)}) %collective-permute-start.29) | collective-permute-done | bytes 196640 | tf_op jit(solution)/shard_map/ppermute | solution.py:255
  50.9 3.5 %collective-permute-start.34 = (bf16[256,384]{1,0:T(8,128)(2,1)S(1)}, bf16[256,384]{1,0:T(8,128)(2,1)S(1)}, u32[]{:S(2)}, u32[]{:S(2)}) collective-permute-start(bf16[256,384]{1,0:T(8,128)(2,1)S(1)} %shard_map.81.refs_0_), channel_id=1, source_target_pairs={{0,6},{1,7},{2,4},{3,5},{4,2},{5,3},{6,0},{7,1},{8,14},{9,15},{10,... | collective-permute-start | bytes 589832 | tf_op jit(solution)/shard_map/ppermute | solution.py:255
  55.6 1.6 %collective-permute-start.1 = (bf16[2,384,256]{2,1,0:T(8,128)(2,1)S(1)}, bf16[2,384,256]{2,1,0:T(8,128)(2,1)S(1)}, u32[]{:S(2)}, u32[]{:S(2)}) collective-permute-start(bf16[2,384,256]{2,1,0:T(8,128)(2,1)S(1)} %shard_map.75), channel_id=1, source_target_pairs={{0,16},{1,17},{2,18},{3,19},{4,20},{5,21},{6,22},{7,23},{8,24},{9,... | collective-permute-start | bytes 1179656 | tf_op jit(solution)/shard_map/ppermute | solution.py:255
  58.0 2.1 %collective-permute-done.34.refs_6_ = bf16[256,384]{1,0:T(8,128)(2,1)S(1)} collective-permute-done((bf16[256,384]{1,0:T(8,128)(2,1)S(1)}, bf16[256,384]{1,0:T(8,128)(2,1)S(1)}, u32[]{:S(2)}, u32[]{:S(2)}) %collective-permute-start.34) | collective-permute-done | bytes 196640 | tf_op jit(solution)/shard_map/ppermute | solution.py:255
  61.5 2.9 %collective-permute-done.30.refs_2_ = bf16[256,384]{1,0:T(8,128)(2,1)S(1)} collective-permute-done((bf16[256,384]{1,0:T(8,128)(2,1)S(1)}, bf16[256,384]{1,0:T(8,128)(2,1)S(1)}, u32[]{:S(2)}, u32[]{:S(2)}) %collective-permute-start.30) | collective-permute-done | bytes 196640 | tf_op jit(solution)/shard_map/ppermute | solution.py:255
  65.8 4.5 %collective-permute-done.32.refs_4_ = bf16[256,384]{1,0:T(8,128)(2,1)S(1)} collective-permute-done((bf16[256,384]{1,0:T(8,128)(2,1)S(1)}, bf16[256,384]{1,0:T(8,128)(2,1)S(1)}, u32[]{:S(2)}, u32[]{:S(2)}) %collective-permute-start.32) | collective-permute-done | bytes 196640 | tf_op jit(solution)/shard_map/ppermute | solution.py:255
  73.6 2.5 %collective-permute-start.17 = (bf16[256,384]{1,0:T(8,128)(2,1)S(1)}, bf16[256,384]{1,0:T(8,128)(2,1)S(1)}, u32[]{:S(2)}, u32[]{:S(2)}) collective-permute-start(bf16[256,384]{1,0:T(8,128)(2,1)S(1)} %get-tuple-element.37.refs_0_), channel_id=1, source_target_pairs={{0,6},{1,7},{2,4},{3,5},{4,2},{5,3},{6,0},{7,1},{8,14},{9,15},{10,... | collective-permute-start | bytes 589832 | tf_op jit(solution)/shard_map/ppermute | solution.py:255
  76.1 2.1 %collective-permute-start.15 = (bf16[256,384]{1,0:T(8,128)(2,1)S(1)}, bf16[256,384]{1,0:T(8,128)(2,1)S(1)}, u32[]{:S(2)}, u32[]{:S(2)}) collective-permute-start(bf16[256,384]{1,0:T(8,128)(2,1)S(1)} %get-tuple-element.38), channel_id=1, source_target_pairs={{0,4},{1,5},{2,6},{3,7},{4,0},{5,1},{6,2},{7,3},{8,12},{9,13},{10,... | collective-permute-start | bytes 589832 | tf_op jit(solution)/shard_map/ppermute | solution.py:255
  80.3 2.0 %collective-permute-done.33.refs_5_ = bf16[256,384]{1,0:T(8,128)(2,1)S(1)} collective-permute-done((bf16[256,384]{1,0:T(8,128)(2,1)S(1)}, bf16[256,384]{1,0:T(8,128)(2,1)S(1)}, u32[]{:S(2)}, u32[]{:S(2)}) %collective-permute-start.33) | collective-permute-done | bytes 196640 | tf_op jit(solution)/shard_map/ppermute | solution.py:255
  84.7 4.0 %collective-permute-done.13.refs_2_ = bf16[256,384]{1,0:T(8,128)(2,1)S(1)} collective-permute-done((bf16[256,384]{1,0:T(8,128)(2,1)S(1)}, bf16[256,384]{1,0:T(8,128)(2,1)S(1)}, u32[]{:S(2)}, u32[]{:S(2)}) %collective-permute-start.13) | collective-permute-done | bytes 196640 | tf_op jit(solution)/shard_map/ppermute | solution.py:255
  88.8 1.6 %collective-permute-start.18 = (bf16[256,384]{1,0:T(8,128)(2,1)S(1)}, bf16[256,384]{1,0:T(8,128)(2,1)S(1)}, u32[]{:S(2)}, u32[]{:S(2)}) collective-permute-start(bf16[256,384]{1,0:T(8,128)(2,1)S(1)} %collective-permute-done.17.refs_6_), channel_id=1, source_target_pairs={{0,1},{1,0},{2,3},{3,2},{4,5},{5,4},{6,7},{7,6},{8,9},{9,8},{10,11... | collective-permute-start | bytes 589832 | tf_op jit(solution)/shard_map/ppermute | solution.py:255
  92.9 2.1 %collective-permute-start.6 = (bf16[384,256]{1,0:T(8,128)(2,1)S(1)}, bf16[384,256]{1,0:T(8,128)(2,1)S(1)}, u32[]{:S(2)}, u32[]{:S(2)}) collective-permute-start(bf16[384,256]{1,0:T(8,128)(2,1)S(1)} %get-tuple-element.34.refs_0_), channel_id=1, source_target_pairs={{0,6},{1,7},{2,4},{3,5},{4,2},{5,3},{6,0},{7,1},{8,14},{9,15},{10,... | collective-permute-start | bytes 589832 | tf_op jit(solution)/shard_map/ppermute | solution.py:255
  96.5 3.2 %collective-permute-start.2 = (bf16[384,256]{1,0:T(8,128)(2,1)S(1)}, bf16[384,256]{1,0:T(8,128)(2,1)S(1)}, u32[]{:S(2)}, u32[]{:S(2)}) collective-permute-start(bf16[384,256]{1,0:T(8,128)(2,1)S(1)} %get-tuple-element.33), channel_id=1, source_target_pairs={{0,4},{1,5},{2,6},{3,7},{4,0},{5,1},{6,2},{7,3},{8,12},{9,13},{10,... | collective-permute-start | bytes 589832 | tf_op jit(solution)/shard_map/ppermute | solution.py:255
  103.8 3.7 %shard_map.84.refs_16_ = f32[2,320,384]{2,1,0:T(8,128)S(1)} custom-call(bf16[256,384]{1,0:T(8,128)(2,1)S(1)} %shard_map.81.refs_0_, bf16[256,384]{1,0:T(8,128)(2,1)S(1)} %collective-permute-done.28.refs_1_, bf16[256,384]{1,0:T(8,128)(2,1)S(1)} %collective-permute-done.30.refs_2_, bf16[256,384]{1,0:T(8,128)(2,1)S(1)} %collective-permute-done.31.refs_3_, ...), custom_call_target="tpu_custom_call" | custom-call | flops 1006632960 | tf_op jit(solution)/shard_map/pallas_call | solution.py:38
  107.6 3.8 %shard_map.85 = (bf16[320,384]{1,0:T(8,128)(2,1)S(1)}, bf16[320,384]{1,0:T(8,128)(2,1)S(1)}) custom-call(bf16[256,384]{1,0:T(8,128)(2,1)S(1)} %get-tuple-element.37.refs_0_, bf16[256,384]{1,0:T(8,128)(2,1)S(1)} %collective-permute-done.12.refs_1_, bf16[256,384]{1,0:T(8,128)(2,1)S(1)} %collective-permute-done.13.refs_2_, ...), custom_call_target="tpu_custom_call" | custom-call | flops 1006632960 | tf_op jit(solution)/shard_map/pallas_call | solution.py:38
  113.4 1.6 %collective-permute-start.8 = (bf16[384,256]{1,0:T(8,128)(2,1)S(1)}, bf16[384,256]{1,0:T(8,128)(2,1)S(1)}, u32[]{:S(2)}, u32[]{:S(2)}) collective-permute-start(bf16[384,256]{1,0:T(8,128)(2,1)S(1)} %collective-permute-done.6.refs_4_), channel_id=1, source_target_pairs={{0,1},{1,0},{2,3},{3,2},{4,5},{5,4},{6,7},{7,6},{8,9},{9,8},{10,11... | collective-permute-start | bytes 589832 | tf_op jit(solution)/shard_map/ppermute | solution.py:255
  115.9 5.2 %collective-permute-done.8.refs_6_ = bf16[384,256]{1,0:T(8,128)(2,1)S(1)} collective-permute-done((bf16[384,256]{1,0:T(8,128)(2,1)S(1)}, bf16[384,256]{1,0:T(8,128)(2,1)S(1)}, u32[]{:S(2)}, u32[]{:S(2)}) %collective-permute-start.8) | collective-permute-done | bytes 196640 | tf_op jit(solution)/shard_map/ppermute | solution.py:255
  121.2 2.7 %collective-permute-done.4.refs_2_ = bf16[384,256]{1,0:T(8,128)(2,1)S(1)} collective-permute-done((bf16[384,256]{1,0:T(8,128)(2,1)S(1)}, bf16[384,256]{1,0:T(8,128)(2,1)S(1)}, u32[]{:S(2)}, u32[]{:S(2)}) %collective-permute-start.4) | collective-permute-done | bytes 196640 | tf_op jit(solution)/shard_map/ppermute | solution.py:255
  134.3 2.9 %collective-permute-done.49.refs_3_ = bf16[80,1024]{1,0:T(8,128)(2,1)S(1)} collective-permute-done((bf16[80,1024]{1,0:T(8,128)(2,1)S(1)}, bf16[80,1024]{1,0:T(8,128)(2,1)S(1)}, u32[]{:S(2)}, u32[]{:S(2)}) %collective-permute-start.49) | collective-permute-done | bytes 163872 | tf_op jit(solution)/shard_map/ppermute | solution.py:255
  137.3 2.0 %shard_map.88.refs_4_ = bf16[512,2048]{1,0:T(8,128)(2,1)} custom-call(s32[1]{0:T(128)} %bitcast.1.half, bf16[512,640]{1,0:T(8,128)(2,1)S(1)} %copy-done.3, bf16[80,1024]{1,0:T(8,128)(2,1)S(1)} %get-tuple-element.51.refs_0_, bf16[80,1024]{1,0:T(8,128)(2,1)S(1)} %collective-permute-done.47.refs_1_, bf16[80,1024]{1,0:T(8,128)(2,1)S(1)} %collective-permute-done.48.refs_2_, ...), custom_call_target="tpu_custom_call" | custom-call | tf_op jit(solution)/shard_map/pallas_call | solution.py:96
  139.6 1.9 %collective-permute-done.38.refs_2_ = bf16[80,1024]{1,0:T(8,128)(2,1)S(1)} collective-permute-done((bf16[80,1024]{1,0:T(8,128)(2,1)S(1)}, bf16[80,1024]{1,0:T(8,128)(2,1)S(1)}, u32[]{:S(2)}, u32[]{:S(2)}) %collective-permute-start.38) | collective-permute-done | bytes 163872 | tf_op jit(solution)/shard_map/ppermute | solution.py:255
  141.5 1.8 %collective-permute-done.39.refs_3_ = bf16[80,1024]{1,0:T(8,128)(2,1)S(1)} collective-permute-done((bf16[80,1024]{1,0:T(8,128)(2,1)S(1)}, bf16[80,1024]{1,0:T(8,128)(2,1)S(1)}, u32[]{:S(2)}, u32[]{:S(2)}) %collective-permute-start.39) | collective-permute-done | bytes 163872 | tf_op jit(solution)/shard_map/ppermute | solution.py:255
  143.3 2.0 %shard_map.89 = bf16[512,2048]{1,0:T(8,128)(2,1)} custom-call(s32[1]{0:T(128)} %bitcast.half, bf16[512,640]{1,0:T(8,128)(2,1)S(1)} %copy-done.3, bf16[80,1024]{1,0:T(8,128)(2,1)S(1)} %get-tuple-element.47.refs_0_, bf16[80,1024]{1,0:T(8,128)(2,1)S(1)} %collective-permute-done.37.refs_1_, ...), custom_call_target="tpu_custom_call", output_to_operand_aliasing={{}: (6, {})} | custom-call | tf_op jit(solution)/shard_map/pallas_call | solution.py:96
  (107 shorter events, 47.7 us)
Async XLA Ops:
  3.7 34.5 %collective-permute-start.26 = (bf16[4,256,384]{2,1,0:T(8,128)(2,1)}, bf16[4,256,384]{2,1,0:T(8,128)(2,1)S(1)}, u32[]{:S(2)}, u32[]{:S(2)}) collective-permute-start(bf16[4,256,384]{2,1,0:T(8,128)(2,1)} %get-tuple-element.44), channel_id=1, source_target_pairs={{0,8},{1,9},{2,10},{3,11},{4,12},{5,13},{6,14},{7,15},{8,0},{9,1},... | collective-permute-start | bytes 2359304 | tf_op jit(solution)/shard_map/ppermute | solution.py:255
  8.9 29.9 %collective-permute-start.10 = (bf16[4,256,384]{2,1,0:T(8,128)(2,1)}, bf16[4,256,384]{2,1,0:T(8,128)(2,1)}, u32[]{:S(2)}, u32[]{:S(2)}) collective-permute-start(bf16[4,256,384]{2,1,0:T(8,128)(2,1)} %get-tuple-element.36), channel_id=1, source_target_pairs={{0,8},{1,9},{2,10},{3,11},{4,12},{5,13},{6,14},{7,15},{8,0},{9,1},... | collective-permute-start | bytes 2359304 | tf_op jit(solution)/shard_map/ppermute | solution.py:255
  9.0 31.9 %collective-permute-start = (bf16[4,384,256]{2,1,0:T(8,128)(2,1)}, bf16[4,384,256]{2,1,0:T(8,128)(2,1)S(1)}, u32[]{:S(2)}, u32[]{:S(2)}) collective-permute-start(bf16[4,384,256]{2,1,0:T(8,128)(2,1)} %get-tuple-element.32), channel_id=1, source_target_pairs={{0,8},{1,9},{2,10},{3,11},{4,12},{5,13},{6,14},{7,15},{8,0},{9,1},... | collective-permute-start | bytes 2359304 | tf_op jit(solution)/shard_map/ppermute | solution.py:255
  16.2 11.0 %collective-permute-start.19 = (bf16[80,2048]{1,0:T(8,128)(2,1)S(1)}, bf16[80,2048]{1,0:T(8,128)(2,1)S(1)}, u32[]{:S(2)}, u32[]{:S(2)}) collective-permute-start(bf16[80,2048]{1,0:T(8,128)(2,1)S(1)} %get-tuple-element.40), channel_id=1, source_target_pairs={{0,2},{1,3},{2,0},{3,1},{4,6},{5,7},{6,4},{7,5},{8,10},{9,11},{10,... | collective-permute-start | bytes 983048 | tf_op jit(solution)/shard_map/ppermute | solution.py:255
  18.9 11.0 %collective-permute-start.20 = (bf16[80,2048]{1,0:T(8,128)(2,1)S(1)}, bf16[80,2048]{1,0:T(8,128)(2,1)S(1)}, u32[]{:S(2)}, u32[]{:S(2)}) collective-permute-start(bf16[80,2048]{1,0:T(8,128)(2,1)S(1)} %get-tuple-element.41), channel_id=1, source_target_pairs={{0,16},{1,17},{2,18},{3,19},{4,20},{5,21},{6,22},{7,23},{8,24},{9,... | collective-permute-start | bytes 983048 | tf_op jit(solution)/shard_map/ppermute | solution.py:255
  27.2 10.4 %collective-permute-start.21 = (bf16[80,2048]{1,0:T(8,128)(2,1)S(1)}, bf16[80,2048]{1,0:T(8,128)(2,1)S(1)}, u32[]{:S(2)}, u32[]{:S(2)}) collective-permute-start(bf16[80,2048]{1,0:T(8,128)(2,1)S(1)} %get-tuple-element.42), channel_id=1, source_target_pairs={{0,18},{1,19},{2,16},{3,17},{4,22},{5,23},{6,20},{7,21},{8,26},{9,... | collective-permute-start | bytes 983048 | tf_op jit(solution)/shard_map/ppermute | solution.py:255
  37.7 18.0 %collective-permute-start.23 = (bf16[80,2048]{1,0:T(8,128)(2,1)S(1)}, bf16[80,2048]{1,0:T(8,128)(2,1)S(1)}, u32[]{:S(2)}, u32[]{:S(2)}) collective-permute-start(bf16[80,2048]{1,0:T(8,128)(2,1)S(1)} %collective-permute-done.19.refs_9_), channel_id=1, source_target_pairs={{0,8},{1,9},{2,10},{3,11},{4,12},{5,13},{6,14},{7,15},{8,0},{9,1},... | collective-permute-start | bytes 983048 | tf_op jit(solution)/shard_map/ppermute | solution.py:255
  37.7 19.5 %collective-permute-start.24 = (bf16[80,2048]{1,0:T(8,128)(2,1)S(1)}, bf16[80,2048]{1,0:T(8,128)(2,1)S(1)}, u32[]{:S(2)}, u32[]{:S(2)}) collective-permute-start(bf16[80,2048]{1,0:T(8,128)(2,1)S(1)} %collective-permute-done.20.refs_10_), channel_id=1, source_target_pairs={{0,8},{1,9},{2,10},{3,11},{4,12},{5,13},{6,14},{7,15},{8,0},{9,1},... | collective-permute-start | bytes 983048 | tf_op jit(solution)/shard_map/ppermute | solution.py:255
  38.2 19.0 %collective-permute-start.25 = (bf16[80,2048]{1,0:T(8,128)(2,1)S(1)}, bf16[80,2048]{1,0:T(8,128)(2,1)S(1)}, u32[]{:S(2)}, u32[]{:S(2)}) collective-permute-start(bf16[80,2048]{1,0:T(8,128)(2,1)S(1)} %collective-permute-done.21.refs_11_), channel_id=1, source_target_pairs={{0,8},{1,9},{2,10},{3,11},{4,12},{5,13},{6,14},{7,15},{8,0},{9,1},... | collective-permute-start | bytes 983048 | tf_op jit(solution)/shard_map/ppermute | solution.py:255
  40.9 10.0 %collective-permute-start.29 = (bf16[1,256,384]{2,1,0:T(8,128)(2,1)S(1)}, bf16[1,256,384]{2,1,0:T(8,128)(2,1)S(1)}, u32[]{:S(2)}, u32[]{:S(2)}) collective-permute-start(bf16[1,256,384]{2,1,0:T(8,128)(2,1)S(1)} %shard_map.82), channel_id=1, source_target_pairs={{0,16},{1,17},{2,18},{3,19},{4,20},{5,21},{6,22},{7,23},{8,24},{9,... | collective-permute-start | bytes 589832 | tf_op jit(solution)/shard_map/ppermute | solution.py:255
  46.7 25.1 %collective-permute-start.11 = (bf16[2,256,384]{2,1,0:T(8,128)(2,1)S(1)}, bf16[2,256,384]{2,1,0:T(8,128)(2,1)S(1)}, u32[]{:S(2)}, u32[]{:S(2)}) collective-permute-start(bf16[2,256,384]{2,1,0:T(8,128)(2,1)S(1)} %shard_map.77), channel_id=1, source_target_pairs={{0,16},{1,17},{2,18},{3,19},{4,20},{5,21},{6,22},{7,23},{8,24},{9,... | collective-permute-start | bytes 1179656 | tf_op jit(solution)/shard_map/ppermute | solution.py:255
  55.6 20.5 %collective-permute-start.1 = (bf16[2,384,256]{2,1,0:T(8,128)(2,1)S(1)}, bf16[2,384,256]{2,1,0:T(8,128)(2,1)S(1)}, u32[]{:S(2)}, u32[]{:S(2)}) collective-permute-start(bf16[2,384,256]{2,1,0:T(8,128)(2,1)S(1)} %shard_map.75), channel_id=1, source_target_pairs={{0,16},{1,17},{2,18},{3,19},{4,20},{5,21},{6,22},{7,23},{8,24},{9,... | collective-permute-start | bytes 1179656 | tf_op jit(solution)/shard_map/ppermute | solution.py:255
  57.2 13.1 %collective-permute-start.32 = (bf16[256,384]{1,0:T(8,128)(2,1)S(1)}, bf16[256,384]{1,0:T(8,128)(2,1)S(1)}, u32[]{:S(2)}, u32[]{:S(2)}) collective-permute-start(bf16[256,384]{1,0:T(8,128)(2,1)S(1)} %shard_map.83), channel_id=1, source_target_pairs={{0,4},{1,5},{2,6},{3,7},{4,0},{5,1},{6,2},{7,3},{8,12},{9,13},{10,... | collective-permute-start | bytes 589832 | tf_op jit(solution)/shard_map/ppermute | solution.py:255
  60.1 13.5 %collective-permute-start.28 = (bf16[256,384]{1,0:T(8,128)(2,1)S(1)}, bf16[256,384]{1,0:T(8,128)(2,1)S(1)}, u32[]{:S(2)}, u32[]{:S(2)}) collective-permute-start(bf16[256,384]{1,0:T(8,128)(2,1)S(1)} %shard_map.81.refs_0_), channel_id=1, source_target_pairs={{0,1},{1,0},{2,3},{3,2},{4,5},{5,4},{6,7},{7,6},{8,9},{9,8},{10,11... | collective-permute-start | bytes 589832 | tf_op jit(solution)/shard_map/ppermute | solution.py:255
  64.4 11.7 %collective-permute-start.35 = (bf16[256,384]{1,0:T(8,128)(2,1)S(1)}, bf16[256,384]{1,0:T(8,128)(2,1)S(1)}, u32[]{:S(2)}, u32[]{:S(2)}) collective-permute-start(bf16[256,384]{1,0:T(8,128)(2,1)S(1)} %collective-permute-done.34.refs_6_), channel_id=1, source_target_pairs={{0,1},{1,0},{2,3},{3,2},{4,5},{5,4},{6,7},{7,6},{8,9},{9,8},{10,11... | collective-permute-start | bytes 589832 | tf_op jit(solution)/shard_map/ppermute | solution.py:255
  71.8 10.5 %collective-permute-start.33 = (bf16[256,384]{1,0:T(8,128)(2,1)S(1)}, bf16[256,384]{1,0:T(8,128)(2,1)S(1)}, u32[]{:S(2)}, u32[]{:S(2)}) collective-permute-start(bf16[256,384]{1,0:T(8,128)(2,1)S(1)} %collective-permute-done.32.refs_4_), channel_id=1, source_target_pairs={{0,1},{1,0},{2,3},{3,2},{4,5},{5,4},{6,7},{7,6},{8,9},{9,8},{10,11... | collective-permute-start | bytes 589832 | tf_op jit(solution)/shard_map/ppermute | solution.py:255
  76.1 12.6 %collective-permute-start.13 = (bf16[256,384]{1,0:T(8,128)(2,1)S(1)}, bf16[256,384]{1,0:T(8,128)(2,1)S(1)}, u32[]{:S(2)}, u32[]{:S(2)}) collective-permute-start(bf16[256,384]{1,0:T(8,128)(2,1)S(1)} %get-tuple-element.38), channel_id=1, source_target_pairs={{0,2},{1,3},{2,0},{3,1},{4,6},{5,7},{6,4},{7,5},{8,10},{9,11},{10,... | collective-permute-start | bytes 589832 | tf_op jit(solution)/shard_map/ppermute | solution.py:255
  76.1 14.3 %collective-permute-start.15 = (bf16[256,384]{1,0:T(8,128)(2,1)S(1)}, bf16[256,384]{1,0:T(8,128)(2,1)S(1)}, u32[]{:S(2)}, u32[]{:S(2)}) collective-permute-start(bf16[256,384]{1,0:T(8,128)(2,1)S(1)} %get-tuple-element.38), channel_id=1, source_target_pairs={{0,4},{1,5},{2,6},{3,7},{4,0},{5,1},{6,2},{7,3},{8,12},{9,13},{10,... | collective-permute-start | bytes 589832 | tf_op jit(solution)/shard_map/ppermute | solution.py:255
  78.2 13.7 %collective-permute-start.12 = (bf16[256,384]{1,0:T(8,128)(2,1)S(1)}, bf16[256,384]{1,0:T(8,128)(2,1)S(1)}, u32[]{:S(2)}, u32[]{:S(2)}) collective-permute-start(bf16[256,384]{1,0:T(8,128)(2,1)S(1)} %get-tuple-element.37.refs_0_), channel_id=1, source_target_pairs={{0,1},{1,0},{2,3},{3,2},{4,5},{5,4},{6,7},{7,6},{8,9},{9,8},{10,11... | collective-permute-start | bytes 589832 | tf_op jit(solution)/shard_map/ppermute | solution.py:255
  82.3 10.6 %collective-permute-start.43 = (bf16[384,256]{1,0:T(8,128)(2,1)S(1)}, bf16[384,256]{1,0:T(8,128)(2,1)S(1)}, u32[]{:S(2)}, u32[]{:S(2)}) collective-permute-start(bf16[384,256]{1,0:T(8,128)(2,1)S(1)} %get-tuple-element.33), channel_id=1, source_target_pairs={{0,2},{1,3},{2,0},{3,1},{4,6},{5,7},{6,4},{7,5},{8,10},{9,11},{10,... | collective-permute-start | bytes 589832 | tf_op jit(solution)/shard_map/ppermute | solution.py:255
  90.5 10.3 %collective-permute-start.14 = (bf16[256,384]{1,0:T(8,128)(2,1)S(1)}, bf16[256,384]{1,0:T(8,128)(2,1)S(1)}, u32[]{:S(2)}, u32[]{:S(2)}) collective-permute-start(bf16[256,384]{1,0:T(8,128)(2,1)S(1)} %collective-permute-done.13.refs_2_), channel_id=1, source_target_pairs={{0,1},{1,0},{2,3},{3,2},{4,5},{5,4},{6,7},{7,6},{8,9},{9,8},{10,11... | collective-permute-start | bytes 589832 | tf_op jit(solution)/shard_map/ppermute | solution.py:255
  92.0 11.8 %collective-permute-start.16 = (bf16[256,384]{1,0:T(8,128)(2,1)S(1)}, bf16[256,384]{1,0:T(8,128)(2,1)S(1)}, u32[]{:S(2)}, u32[]{:S(2)}) collective-permute-start(bf16[256,384]{1,0:T(8,128)(2,1)S(1)} %collective-permute-done.15.refs_4_), channel_id=1, source_target_pairs={{0,1},{1,0},{2,3},{3,2},{4,5},{5,4},{6,7},{7,6},{8,9},{9,8},{10,11... | collective-permute-start | bytes 589832 | tf_op jit(solution)/shard_map/ppermute | solution.py:255
  92.9 18.5 %collective-permute-start.40 = (bf16[384,256]{1,0:T(8,128)(2,1)S(1)}, bf16[384,256]{1,0:T(8,128)(2,1)S(1)}, u32[]{:S(2)}, u32[]{:S(2)}) collective-permute-start(bf16[384,256]{1,0:T(8,128)(2,1)S(1)} %get-tuple-element.34.refs_0_), channel_id=1, source_target_pairs={{0,8},{1,9},{2,10},{3,11},{4,12},{5,13},{6,14},{7,15},{8,0},{9,1},... | collective-permute-start | bytes 589832 | tf_op jit(solution)/shard_map/ppermute | solution.py:255
  92.9 19.0 %collective-permute-start.6 = (bf16[384,256]{1,0:T(8,128)(2,1)S(1)}, bf16[384,256]{1,0:T(8,128)(2,1)S(1)}, u32[]{:S(2)}, u32[]{:S(2)}) collective-permute-start(bf16[384,256]{1,0:T(8,128)(2,1)S(1)} %get-tuple-element.34.refs_0_), channel_id=1, source_target_pairs={{0,6},{1,7},{2,4},{3,5},{4,2},{5,3},{6,0},{7,1},{8,14},{9,15},{10,... | collective-permute-start | bytes 589832 | tf_op jit(solution)/shard_map/ppermute | solution.py:255
  96.5 16.9 %collective-permute-start.2 = (bf16[384,256]{1,0:T(8,128)(2,1)S(1)}, bf16[384,256]{1,0:T(8,128)(2,1)S(1)}, u32[]{:S(2)}, u32[]{:S(2)}) collective-permute-start(bf16[384,256]{1,0:T(8,128)(2,1)S(1)} %get-tuple-element.33), channel_id=1, source_target_pairs={{0,4},{1,5},{2,6},{3,7},{4,0},{5,1},{6,2},{7,3},{8,12},{9,13},{10,... | collective-permute-start | bytes 589832 | tf_op jit(solution)/shard_map/ppermute | solution.py:255
  100.7 14.2 %collective-permute-start.45 = (bf16[384,256]{1,0:T(8,128)(2,1)S(1)}, bf16[384,256]{1,0:T(8,128)(2,1)S(1)}, u32[]{:S(2)}, u32[]{:S(2)}) collective-permute-start(bf16[384,256]{1,0:T(8,128)(2,1)S(1)} %collective-permute-done.43.refs_4_), channel_id=1, source_target_pairs={{0,1},{1,0},{2,3},{3,2},{4,5},{5,4},{6,7},{7,6},{8,9},{9,8},{10,11... | collective-permute-start | bytes 589832 | tf_op jit(solution)/shard_map/ppermute | solution.py:255
  103.8 11.6 %collective-permute-start.42 = (bf16[384,256]{1,0:T(8,128)(2,1)S(1)}, bf16[384,256]{1,0:T(8,128)(2,1)S(1)}, u32[]{:S(2)}, u32[]{:S(2)}) collective-permute-start(bf16[384,256]{1,0:T(8,128)(2,1)S(1)} %collective-permute-done.41.refs_2_), channel_id=1, source_target_pairs={{0,8},{1,9},{2,10},{3,11},{4,12},{5,13},{6,14},{7,15},{8,0},{9,1},... | collective-permute-start | bytes 589832 | tf_op jit(solution)/shard_map/ppermute | solution.py:255
  111.4 12.9 %collective-permute-start.36 = (bf16[320,384]{1,0:T(8,128)(2,1)S(1)}, bf16[320,384]{1,0:T(8,128)(2,1)S(1)}, u32[]{:S(2)}, u32[]{:S(2)}) collective-permute-start(bf16[320,384]{1,0:T(8,128)(2,1)S(1)} %get-tuple-element.46), channel_id=1, source_target_pairs={{0,8},{1,9},{2,10},{3,11},{4,12},{5,13},{6,14},{7,15},{8,0},{9,1},... | collective-permute-start | bytes 737288 | tf_op jit(solution)/shard_map/ppermute | solution.py:255
  115.4 10.5 %collective-permute-start.7 = (bf16[384,256]{1,0:T(8,128)(2,1)S(1)}, bf16[384,256]{1,0:T(8,128)(2,1)S(1)}, u32[]{:S(2)}, u32[]{:S(2)}) collective-permute-start(bf16[384,256]{1,0:T(8,128)(2,1)S(1)} %collective-permute-done.6.refs_4_), channel_id=1, source_target_pairs={{0,8},{1,9},{2,10},{3,11},{4,12},{5,13},{6,14},{7,15},{8,0},{9,1},... | collective-permute-start | bytes 589832 | tf_op jit(solution)/shard_map/ppermute | solution.py:255
  127.4 9.9 %collective-permute-start.49 = (bf16[80,1024]{1,0:T(8,128)(2,1)S(1)}, bf16[80,1024]{1,0:T(8,128)(2,1)S(1)}, u32[]{:S(2)}, u32[]{:S(2)}) collective-permute-start(bf16[80,1024]{1,0:T(8,128)(2,1)S(1)} %get-tuple-element.54), channel_id=1, source_target_pairs={{0,18},{1,19},{2,16},{3,17},{4,22},{5,23},{6,20},{7,21},{8,26},{9,... | collective-permute-start | bytes 491528 | tf_op jit(solution)/shard_map/ppermute | solution.py:255
  130.6 10.9 %collective-permute-start.38 = (bf16[80,1024]{1,0:T(8,128)(2,1)S(1)}, bf16[80,1024]{1,0:T(8,128)(2,1)S(1)}, u32[]{:S(2)}, u32[]{:S(2)}) collective-permute-start(bf16[80,1024]{1,0:T(8,128)(2,1)S(1)} %get-tuple-element.49), channel_id=1, source_target_pairs={{0,16},{1,17},{2,18},{3,19},{4,20},{5,21},{6,22},{7,23},{8,24},{9,... | collective-permute-start | bytes 491528 | tf_op jit(solution)/shard_map/ppermute | solution.py:255
  132.5 10.8 %collective-permute-start.39 = (bf16[80,1024]{1,0:T(8,128)(2,1)S(1)}, bf16[80,1024]{1,0:T(8,128)(2,1)S(1)}, u32[]{:S(2)}, u32[]{:S(2)}) collective-permute-start(bf16[80,1024]{1,0:T(8,128)(2,1)S(1)} %get-tuple-element.50), channel_id=1, source_target_pairs={{0,18},{1,19},{2,16},{3,17},{4,22},{5,23},{6,20},{7,21},{8,26},{9,... | collective-permute-start | bytes 491528 | tf_op jit(solution)/shard_map/ppermute | solution.py:255
  (28 other events, 246.7 us)

commit v2 on v1

v2 whole, which is shorter than its diff:
```python
import functools

import jax
import jax.numpy as jnp
from jax import lax
from jax.experimental import pallas as pl
from jax.experimental.pallas import tpu as pltpu
from jax.sharding import PartitionSpec as P


VISITS = 4
CAP = 80
AXES = ("expert", "group")
F32 = jnp.float32
BF16 = jnp.bfloat16


STEPS = (((1,), (0,)), ((1, 0),), ((1, 0),))

GROUPS = ((0, 1), (2, 3))

VMEM = pl.BlockSpec(memory_space=pltpu.VMEM)
SMEM = pl.BlockSpec(memory_space=pltpu.SMEM)
ANY = pl.BlockSpec(memory_space=pl.ANY)
HBM = pl.BlockSpec(memory_space=pltpu.HBM)


def place(sides):
    e, g = lax.axis_index("expert"), lax.axis_index("group")
    z = g // sides
    return e, e & 1, (e >> 1) & 1, z, g % sides, (z ^ (z >> 1)) & 1


def visit(k, x, ab):
    return 2 * (ab if k % 2 == 0 else 1 - ab) + (x if k < 2 else 1 - x)


def call(kernel, out_shape, in_specs, args, scratch=(), limit=8, flops=0):
    many = isinstance(out_shape, list)
    size = sum(array.size * array.dtype.itemsize for array in (*args, *(out_shape if many else [out_shape])))
    return pl.pallas_call(
        kernel,
        out_shape=out_shape,
        in_specs=in_specs,
        out_specs=[VMEM] * len(out_shape) if many else VMEM,
        scratch_shapes=list(scratch),
        compiler_params=pltpu.CompilerParams(vmem_limit_bytes=limit << 20),
        cost_estimate=pl.CostEstimate(flops=flops, bytes_accessed=size, transcendentals=0),
    )(*args)


def pick_kernel(sides, axes, visited, routing, mixing, tokens, *refs):
    count = len(axes)
    matrices, refs = refs[:count], refs[count:]
    picks, shares, refs = refs[:VISITS], refs[VISITS], refs[VISITS + 1 :]
    outs, (held, sem, cut_sem) = refs[: 2 * count], refs[2 * count :]
    copy = pltpu.make_async_copy(tokens, held, sem)
    copy.start()
    copies = []
    for n, (matrix, axis) in enumerate(zip(matrices, axes)):
        pair = outs[2 * n : 2 * n + 2]
        copies += cut_copies(sides, matrix.shape[0], axis, (0, 1), visited, matrix, pair, cut_sem.at[n])
    _, _, x, _, _, ab = place(sides)
    names, rows = routing.shape
    named, mix = routing[...], mixing[...]
    lines = lax.broadcasted_iota(jnp.int32, (names, rows), 0)
    weights, members = [], jnp.zeros((names, rows), F32)
    for k in range(VISITS):
        hit = named == visited[visit(k, x, ab)]
        weights.append(jnp.sum(jnp.where(hit, mix, 0.0), axis=0, keepdims=True))
        found = jnp.sum(jnp.where(hit, 1.0, 0.0), axis=0, keepdims=True)
        members = members + jnp.where(lines == k, found, 0.0)
    before = lax.broadcasted_iota(jnp.int32, (rows, rows), 0) < lax.broadcasted_iota(
        jnp.int32, (rows, rows), 1
    )
    ranks = jnp.dot(
        members.astype(BF16), jnp.where(before, 1.0, 0.0).astype(BF16), preferred_element_type=F32
    )
    places = jnp.where(members > 0.5, ranks, -1.0)
    slots = lax.broadcasted_iota(jnp.int32, (CAP, rows), 0).astype(F32)
    taken = [slots == places[k : k + 1, :] for k in range(VISITS)]
    copy.wait()
    for k in range(VISITS):
        one = jnp.where(taken[k], 1.0, 0.0).astype(BF16)
        picks[k][...] = jnp.dot(one, held[...], preferred_element_type=F32).astype(BF16)
    spread = jnp.concatenate([jnp.where(taken[k], weights[k], 0.0) for k in range(VISITS)], axis=0)
    top = spread.astype(BF16).astype(F32)
    shares[...] = jnp.concatenate([top, spread - top], axis=0).T.astype(BF16)
    for copy in copies:
        copy.wait()


def merge_kernel(half, parity, shares, *refs):
    pieces, out = refs[:-1], refs[-1]
    if len(pieces) >= 2 * VISITS:
        first = pl.program_id(0) == parity[0]
        values = []
        for k in range(VISITS):
            one, two = pieces[k][...], pieces[VISITS + k][...]
            values.append(jnp.where(first if k % 2 == 0 else jnp.logical_not(first), one, two))
    else:
        values = [piece[...] for piece in pieces[:VISITS]]
    out[...] = jnp.dot(shares[...], jnp.concatenate(values * 2, axis=0), preferred_element_type=F32).astype(BF16)


def merge(half, parity, shares, pieces, before, width):
    rows, tile = shares.shape[0], width // VISITS
    ins = [pl.BlockSpec(shares.shape, lambda i, half, parity: (0, 0))]
    for array, first, step in pieces:
        ins.append(
            pl.BlockSpec((array.shape[0], tile), lambda i, half, parity, first=first, step=step: (0, first + step * i))
        )
    args = [half, parity, shares, *(array for array, _, _ in pieces)]
    if before is not None:
        ins.append(ANY)
        args.append(before)
    return pl.pallas_call(
        merge_kernel,
        grid_spec=pltpu.PrefetchScalarGridSpec(
            num_scalar_prefetch=2,
            grid=(2,),
            in_specs=ins,
            out_specs=pl.BlockSpec((rows, tile), lambda i, half, parity: (0, half[0] * 2 + i)),
        ),
        out_shape=jax.ShapeDtypeStruct((rows, width), BF16),
        input_output_aliases={} if before is None else {len(args) - 1: 0},
        compiler_params=pltpu.CompilerParams(vmem_limit_bytes=8 << 20),
        cost_estimate=pl.CostEstimate(
            flops=4 * shares.size * tile, bytes_accessed=2 * shares.size * 2, transcendentals=0
        ),
    )(*args)


def cut_copies(sides, held, axis, halves, visited, matrix, outs, sem):
    _, c, x, _, _, ab = place(sides)
    size = outs[0].shape[axis + 1]
    copies = []
    for out, half in zip(outs, halves):
        part = pl.ds(pl.multiple_of((1 - c if half else c) * size, 128), size)
        for k in range(VISITS):
            source = matrix.at[lax.rem(visited[visit(k, x, ab)], held)]
            source = source.at[part, :] if axis == 0 else source.at[:, part]
            copies.append(pltpu.make_async_copy(source, out.at[k], sem.at[len(copies)]))
    for copy in copies:
        copy.start()
    return copies


def half_shape(matrix, axis):
    _, a, b = matrix.shape
    return jax.ShapeDtypeStruct((VISITS, a // 2, b) if axis == 0 else (VISITS, a, b // 2), BF16)


def cut_kernel(sides, held, axis, halves, visited, matrix, *refs):
    for copy in cut_copies(sides, held, axis, halves, visited, matrix, refs[:-1], refs[-1]):
        copy.wait()


def cut(sides, visited, matrix, axis, halves):
    return call(
        functools.partial(cut_kernel, sides, matrix.shape[0], axis, halves),
        [half_shape(matrix, axis)] * len(halves),
        [SMEM, HBM],
        (visited, pltpu.with_memory_space_constraint(matrix, pltpu.HBM)),
        [pltpu.SemaphoreType.DMA((VISITS * len(halves),))],
        limit=2,
    )


def choose(own, out, here, there):
    @pl.when(own)
    def _():
        out[...] = here[...]

    @pl.when(jnp.logical_not(own))
    def _():
        out[...] = there[...]


def blend_kernel(sides, held, bit, visited, mine, theirs, got, mine_out, theirs_out):
    e, _, x, _, _, ab = place(sides)
    for k in range(VISITS):
        owner = visited[visit(k, x, ab)] // held
        own = (owner & bit) == (e & bit)
        choose(own, mine_out.at[k], mine.at[k], got.at[k])
        choose(own, theirs_out.at[k], theirs.at[k], got.at[VISITS + k])


def send_kernel(sides, held, ks, visited, mine, got, out):
    _, c, x, _, _, ab = place(sides)
    for n, k in enumerate(ks):
        owner = visited[visit(2 + k, x, ab)] // held
        choose((owner & 1) == c, out.at[n], mine.at[2 + k], got.at[2 + k])


def keep_kernel(sides, held, ks, visited, mine, got, far, *outs):
    _, c, x, _, _, ab = place(sides)
    for n, (k, out) in enumerate(zip(ks, outs)):
        owner = visited[visit(k, x, ab)] // held
        near = ((owner >> 1) & 1) == x

        @pl.when(near)
        def _():
            choose((owner & 1) == c, out, mine.at[k], got.at[k])

        @pl.when(jnp.logical_not(near))
        def _():
            out[...] = far[n]


def load_blocks(sides, keys, blocks, held, sem, spots=None):
    _, c, _, z, y, _ = place(sides)
    copies = []
    for n, ((plane_bits, side_bits, core), block) in enumerate(zip(keys, blocks)):
        rows, columns = block.shape
        if spots is None:
            piece = (z ^ plane_bits) * sides + (y ^ side_bits)
            spot = held.at[pl.ds(pl.multiple_of(piece * rows, 128), rows), :]
        else:
            tile, moves = spots[plane_bits]
            piece = (tile + ((z ^ plane_bits) & 1 if moves else 0)) * sides + (y ^ side_bits)
            first = pl.ds(pl.multiple_of((c ^ core) * rows, 128), rows)
            spot = held.at[first, pl.ds(pl.multiple_of(piece * columns, 128), columns)]
        copies.append(pltpu.make_async_copy(block, spot, sem.at[n]))
    for copy in copies:
        copy.start()
    for copy in copies:
        copy.wait()


def gate_kernel(sides, keys, *refs):
    blocks, rows = refs[: len(keys)], refs[len(keys) : len(keys) + 2 * VISITS]
    out, held, sem = refs[len(keys) + 2 * VISITS :]
    load_blocks(sides, keys, blocks, held, sem)
    for side in range(2):
        picked = jnp.concatenate([ref[...] for ref in rows[side * VISITS : (side + 1) * VISITS]], axis=0)
        out[side] = jnp.dot(picked, held[...], preferred_element_type=F32)


def up_kernel(sides, keys, *refs):
    blocks, rows = refs[: len(keys)], refs[len(keys) : len(keys) + 2 * VISITS]
    gate, own, partner, held, sem = refs[len(keys) + 2 * VISITS :]
    load_blocks(sides, keys, blocks, held, sem)
    for side, out in enumerate((own, partner)):
        picked = jnp.concatenate([ref[...] for ref in rows[side * VISITS : (side + 1) * VISITS]], axis=0)
        up = jnp.dot(picked, held[...], preferred_element_type=F32)
        out[...] = (jax.nn.silu(gate[side]) * up).astype(BF16)


def down_kernel(sides, keys, spots, *refs):
    count = len(keys)
    blocks, (own, partner), outs = refs[:count], refs[count : count + 2], refs[count + 2 : count + 2 + VISITS]
    held, hidden, sem = refs[count + 2 + VISITS :]
    _, c, _, _, _, _ = place(sides)
    inner = own.shape[1]
    hidden[:, pl.ds(pl.multiple_of(c * inner, 128), inner)] = own[...]
    hidden[:, pl.ds(pl.multiple_of((1 - c) * inner, 128), inner)] = partner[...]
    load_blocks(sides, keys, blocks, held, sem, spots)
    out = jnp.dot(hidden[...], held[...], preferred_element_type=F32).astype(BF16)
    for k in range(VISITS):
        outs[k][...] = out[k * CAP : (k + 1) * CAP]


def body(mesh, tokens, routing, mixing, visited, gate_matrix, up_matrix, down_matrix):
    experts, groups = mesh.shape["expert"], mesh.shape["group"]
    planes = VISITS
    sides = groups // planes
    held = gate_matrix.shape[0]
    count, width = tokens.shape
    inner = gate_matrix.shape[2]
    total = VISITS * CAP
    shape = jax.ShapeDtypeStruct
    z = lax.axis_index("group") // sides

    def swap(value, expert_bits=0, plane_bits=0, side_bits=0):
        pairs = []
        for one in range(experts):
            for two in range(groups):
                other = ((two // sides) ^ plane_bits) * sides + ((two % sides) ^ side_bits)
                pairs.append((one * groups + two, (one ^ expert_bits) * groups + other))
        return lax.ppermute(value, AXES, pairs)

    (theirs,) = cut(sides, visited, gate_matrix, 1, (1,))
    (mine,) = cut(sides, visited, gate_matrix, 1, (0,))
    others, axes = (up_matrix, down_matrix), (1, 0)
    outs = call(
        functools.partial(pick_kernel, sides, axes),
        [shape((CAP, width), BF16)] * VISITS
        + [shape((count, 2 * total), BF16)]
        + [half_shape(matrix, axis) for matrix, axis in zip(others, axes) for _ in range(2)],
        [SMEM, VMEM, VMEM] + [HBM] * 3,
        (
            visited,
            routing.T,
            mixing.T,
            *(pltpu.with_memory_space_constraint(array, pltpu.HBM) for array in (tokens, *others)),
        ),
        [
            pltpu.VMEM(tokens.shape, BF16),
            pltpu.SemaphoreType.DMA,
            pltpu.SemaphoreType.DMA((2, 2 * VISITS)),
        ],
        limit=12,
    )
    picked, shares = outs[:VISITS], outs[VISITS]
    matrices = []
    for mine, theirs in ((mine, theirs), outs[VISITS + 1 : VISITS + 3], outs[VISITS + 3 :]):
        bit = 4
        while bit < experts:
            got = swap(jnp.concatenate([mine, theirs], axis=0), expert_bits=bit)
            mine, theirs = call(
                functools.partial(blend_kernel, sides, held, bit),
                [shape(mine.shape, BF16)] * 2,
                [SMEM] + [VMEM] * 3,
                (visited, mine, theirs, got),
                limit=32,
            )
            bit *= 2
        matrices.append((mine, swap(theirs, expert_bits=1)))

    sent = []
    for n, (mine, got) in enumerate(matrices):
        sent.append({})
        for ks in STEPS[n]:
            away = call(
                functools.partial(send_kernel, sides, held, ks),
                shape((len(ks), *mine.shape[1:]), BF16),
                [SMEM, VMEM, VMEM],
                (visited, mine, got),
                limit=2,
            )
            sent[n][ks] = swap(away, expert_bits=2)
    rows = [
        picked[0],
        swap(picked[1], plane_bits=1),
        swap(picked[2], expert_bits=2),
        swap(picked[3], expert_bits=2, plane_bits=1),
    ]

    pieces = []
    for n, (mine, got) in enumerate(matrices):
        kept = {}
        for ks, far in sent[n].items():
            outs = call(
                functools.partial(keep_kernel, sides, held, ks),
                [shape(mine.shape[1:], BF16)] * len(ks),
                [SMEM] + [VMEM] * 3,
                (visited, mine, got, far),
                limit=2,
            )
            kept.update(zip(ks, outs))
        same, other = kept[0], kept[1]
        found = [
            (0, same), (1, swap(other, plane_bits=1)), (2, swap(other, plane_bits=2)), (3, swap(same, plane_bits=3))
        ]
        keys, blocks = [], []
        for plane_bits, value in found:
            for side_bits in range(sides):
                moved = value
                if side_bits:
                    moved = swap(value, side_bits=side_bits)
                keys.append((plane_bits, side_bits, 0))
                blocks.append(moved)
                if n == 2:
                    keys.append((plane_bits, side_bits, 1))
                    blocks.append(swap(moved, expert_bits=1))
        pieces.append((keys, blocks))

    rows += [swap(value, expert_bits=1) for value in rows]
    keys, blocks = pieces[0]
    work = 4 * total * width * inner // 2
    gate = call(
        functools.partial(gate_kernel, sides, keys),
        shape((2, total, inner // 2), F32),
        [ANY] * len(keys) + [VMEM] * len(rows),
        (*blocks, *rows),
        [pltpu.VMEM((width, inner // 2), BF16), pltpu.SemaphoreType.DMA((len(keys),))],
        flops=work,
    )
    keys, blocks = pieces[1]
    own, partner = call(
        functools.partial(up_kernel, sides, keys),
        [shape((total, inner // 2), BF16)] * 2,
        [ANY] * len(keys) + [VMEM] * (len(rows) + 1),
        (*blocks, *rows, gate),
        [pltpu.VMEM((width, inner // 2), BF16), pltpu.SemaphoreType.DMA((len(keys),))],
        flops=work,
    )
    partner = swap(partner, expert_bits=1)
    keys, blocks = pieces[2]
    parity, near, far = ((value).reshape(1) for value in (z % 2, z // 2, 1 - z // 2))
    found = {}
    for group in GROUPS:
        spots = {}
        for plane in group:
            moves = plane ^ 1 in group
            spots[plane] = (spots[plane ^ 1][0] if plane ^ 1 in spots else len(spots), moves)
        chosen = [n for n, key in enumerate(keys) if key[0] in group]
        columns = len(group) * width // planes
        outs = call(
            functools.partial(down_kernel, sides, [keys[n] for n in chosen], spots),
            [shape((CAP, columns), BF16)] * VISITS,
            [ANY] * len(chosen) + [VMEM] * 2,
            (*(blocks[n] for n in chosen), own, partner),
            [
                pltpu.VMEM((inner, columns), BF16),
                pltpu.VMEM((total, inner), BF16),
                pltpu.SemaphoreType.DMA((len(chosen),)),
            ],
            flops=work * len(group) // planes,
        )
        back = [
            outs[0],
            swap(outs[1], plane_bits=1),
            swap(outs[2], expert_bits=2),
            swap(outs[3], expert_bits=2, plane_bits=1),
        ]
        for plane in group:
            found[plane] = [(array, spots[plane][0], int(spots[plane][1])) for array in back]
    combined = merge(near, parity, shares, found[0], None, width)
    last = found[2] if found[2][0][2] else found[2] + found[3]
    combined = merge(far, parity, shares, last, combined, width)
    return combined


def solution(mesh):
    placed = (
        P(("expert", "group"), None),
        P(("expert", "group"), None),
        P(("expert", "group"), None),
        P(),
        P("expert", "group", None),
        P("expert", "group", None),
        P("expert", None, "group"),
    )
    return jax.shard_map(
        functools.partial(body, mesh),
        mesh=mesh,
        in_specs=placed,
        out_specs=P(("expert", "group"), None),
        check_vma=False,
    )
```

time: 146 us -> 137 us (0.938)
  local copies, waits for them, and re-layouts: 5.05 us -> 2.09 us
  Pallas kernels: 29.8 us -> 27.2 us
  starting transfers between devices: 52.2 us -> 50.2 us
    unnamed x22 -> x6, local copies, waits for them, and re-layouts: 5.05 us -> 2.09 us
    pallas_call x15, Pallas kernels: 25.7 us -> 23.2 us  [call(): pl.pallas_call(kernel, out_shape=out_shape, in_specs=in_specs, out_specs=...]
    ppermute x50, starting transfers between devices: 52.2 us -> 50.2 us  [swap(): return lax.ppermute(value, AXES, pairs)]
  transfers between devices with their start and end apart: 50 -> 50, of which waited for: 23 -> 22; matrix products, arithmetic and copies ran while one was open for 1% -> 0% of each run, Pallas kernels for 17% -> 15%
where the time goes in v2:
time: 137 us
  waiting for transfers between devices  57 us (42%)
  starting transfers between devices  50.2 us (37%)
  Pallas kernels  27.2 us (20%)
  local copies, waits for them, and re-layouts  2.09 us (2%)
    ppermute x50, waiting for transfers between devices, swap(): return lax.ppermute(value, AXES, pairs)  57 us
    ppermute x50, starting transfers between devices, swap(): return lax.ppermute(value, AXES, pairs)  50.2 us
    pallas_call x15, Pallas kernels, call(): pl.pallas_call(kernel, out_shape=out_shape, in_specs=in_specs, out_specs=...  23.2 us
    pallas_call x2, Pallas kernels, merge(): pl.pallas_call(merge_kernel, grid_spec=pltpu.PrefetchScalarGridSpec(num_s...  4.07 us
  transfers between devices with their start and end apart: 50, of which 22 were waited for; matrix products, arithmetic and copies ran while one was open for 0% of the time, Pallas kernels for 15%

profile of v2, /device:TPU:0, one launch (start us, length us, event | category | flops | bytes accessed | tf_op | source)
XLA Modules:
  0.0 136.7 jit_solution(7506124895860680572)
XLA Ops:
  2.1 5.0 %shard_map.73 = (bf16[80,2048]{1,0:T(8,128)(2,1)S(1)}, bf16[80,2048]{1,0:T(8,128)(2,1)S(1)}, bf16[80,2048]{1,0:T(8,128)(2,1)S(1)}, bf16[80,2048]{1,0:T(8,128)(2,...) custom-call(s32[4]{0:T(128)S(1)} %copy-done, ...), custom_call_target="tpu_custom_call" | custom-call | bytes 13533200 | tf_op jit(solution)/shard_map/pallas_call | solution.py:41
  7.2 3.1 %collective-permute-start.19 = (bf16[80,2048]{1,0:T(8,128)(2,1)S(1)}, bf16[80,2048]{1,0:T(8,128)(2,1)S(1)}, u32[]{:S(2)}, u32[]{:S(2)}) collective-permute-start(bf16[80,2048]{1,0:T(8,128)(2,1)S(1)} %get-tuple-element.38), channel_id=1, source_target_pairs={{0,2},{1,3},{2,0},{3,1},{4,6},{5,7},{6,4},{7,5},{8,10},{9,11},{10,... | collective-permute-start | bytes 983048 | tf_op jit(solution)/shard_map/ppermute | solution.py:281
  10.3 1.8 %shard_map.79 = bf16[4,256,384]{2,1,0:T(8,128)(2,1)S(1)} custom-call(s32[4]{0:T(128)S(1)} %copy-done, bf16[8,256,768]{2,1,0:T(8,128)(2,1)} %matrix.3), custom_call_target="tpu_custom_call" | custom-call | bytes 3932176 | tf_op jit(solution)/shard_map/pallas_call | solution.py:41
  14.2 4.7 %collective-permute-done.19.refs_9_ = bf16[80,2048]{1,0:T(8,128)(2,1)S(1)} collective-permute-done((bf16[80,2048]{1,0:T(8,128)(2,1)S(1)}, bf16[80,2048]{1,0:T(8,128)(2,1)S(1)}, u32[]{:S(2)}, u32[]{:S(2)}) %collective-permute-start.19) | collective-permute-done | bytes 327712 | tf_op jit(solution)/shard_map/ppermute | solution.py:281
  18.8 10.6 %collective-permute-done.20.refs_10_ = bf16[80,2048]{1,0:T(8,128)(2,1)S(1)} collective-permute-done((bf16[80,2048]{1,0:T(8,128)(2,1)S(1)}, bf16[80,2048]{1,0:T(8,128)(2,1)S(1)}, u32[]{:S(2)}, u32[]{:S(2)}) %collective-permute-start.20) | collective-permute-done | bytes 327712 | tf_op jit(solution)/shard_map/ppermute | solution.py:281
  31.5 1.8 %shard_map.78.mine = bf16[4,256,384]{2,1,0:T(8,128)(2,1)S(1)} custom-call(s32[4]{0:T(128)S(1)} %copy-done, bf16[8,256,768]{2,1,0:T(8,128)(2,1)} %matrix.3), custom_call_target="tpu_custom_call" | custom-call | bytes 3932176 | tf_op jit(solution)/shard_map/pallas_call | solution.py:41
  34.0 1.6 %collective-permute-start.27 = (bf16[1,256,384]{2,1,0:T(8,128)(2,1)S(1)}, bf16[1,256,384]{2,1,0:T(8,128)(2,1)S(1)}, u32[]{:S(2)}, u32[]{:S(2)}) collective-permute-start(bf16[1,256,384]{2,1,0:T(8,128)(2,1)S(1)} %shard_map.80), channel_id=1, source_target_pairs={{0,16},{1,17},{2,18},{3,19},{4,20},{5,21},{6,22},{7,23},{8,24},{9,... | collective-permute-start | bytes 589832 | tf_op jit(solution)/shard_map/ppermute | solution.py:281
  37.4 4.4 %collective-permute-done.27.far = bf16[1,256,384]{2,1,0:T(8,128)(2,1)S(1)} collective-permute-done((bf16[1,256,384]{2,1,0:T(8,128)(2,1)S(1)}, bf16[1,256,384]{2,1,0:T(8,128)(2,1)S(1)}, u32[]{:S(2)}, u32[]{:S(2)}) %collective-permute-start.27) | collective-permute-done | bytes 196640 | tf_op jit(solution)/shard_map/ppermute | solution.py:281
  43.9 2.5 %collective-permute-start.34 = (bf16[256,384]{1,0:T(8,128)(2,1)S(1)}, bf16[256,384]{1,0:T(8,128)(2,1)S(1)}, u32[]{:S(2)}, u32[]{:S(2)}) collective-permute-start(bf16[256,384]{1,0:T(8,128)(2,1)S(1)} %shard_map.81.refs_0_), channel_id=1, source_target_pairs={{0,6},{1,7},{2,4},{3,5},{4,2},{5,3},{6,0},{7,1},{8,14},{9,15},{10,... | collective-permute-start | bytes 589832 | tf_op jit(solution)/shard_map/ppermute | solution.py:281
  49.0 2.2 %collective-permute-start.32 = (bf16[256,384]{1,0:T(8,128)(2,1)S(1)}, bf16[256,384]{1,0:T(8,128)(2,1)S(1)}, u32[]{:S(2)}, u32[]{:S(2)}) collective-permute-start(bf16[256,384]{1,0:T(8,128)(2,1)S(1)} %shard_map.83), channel_id=1, source_target_pairs={{0,4},{1,5},{2,6},{3,7},{4,0},{5,1},{6,2},{7,3},{8,12},{9,13},{10,... | collective-permute-start | bytes 589832 | tf_op jit(solution)/shard_map/ppermute | solution.py:281
  53.5 2.7 %collective-permute-done.30.refs_2_ = bf16[256,384]{1,0:T(8,128)(2,1)S(1)} collective-permute-done((bf16[256,384]{1,0:T(8,128)(2,1)S(1)}, bf16[256,384]{1,0:T(8,128)(2,1)S(1)}, u32[]{:S(2)}, u32[]{:S(2)}) %collective-permute-start.30) | collective-permute-done | bytes 196640 | tf_op jit(solution)/shard_map/ppermute | solution.py:281
  57.7 4.7 %collective-permute-done.32.refs_4_ = bf16[256,384]{1,0:T(8,128)(2,1)S(1)} collective-permute-done((bf16[256,384]{1,0:T(8,128)(2,1)S(1)}, bf16[256,384]{1,0:T(8,128)(2,1)S(1)}, u32[]{:S(2)}, u32[]{:S(2)}) %collective-permute-start.32) | collective-permute-done | bytes 196640 | tf_op jit(solution)/shard_map/ppermute | solution.py:281
  65.1 2.7 %collective-permute-start.17 = (bf16[256,384]{1,0:T(8,128)(2,1)S(1)}, bf16[256,384]{1,0:T(8,128)(2,1)S(1)}, u32[]{:S(2)}, u32[]{:S(2)}) collective-permute-start(bf16[256,384]{1,0:T(8,128)(2,1)S(1)} %get-tuple-element.35.refs_0_), channel_id=1, source_target_pairs={{0,6},{1,7},{2,4},{3,5},{4,2},{5,3},{6,0},{7,1},{8,14},{9,15},{10,... | collective-permute-start | bytes 589832 | tf_op jit(solution)/shard_map/ppermute | solution.py:281
  67.8 2.4 %collective-permute-start.15 = (bf16[256,384]{1,0:T(8,128)(2,1)S(1)}, bf16[256,384]{1,0:T(8,128)(2,1)S(1)}, u32[]{:S(2)}, u32[]{:S(2)}) collective-permute-start(bf16[256,384]{1,0:T(8,128)(2,1)S(1)} %get-tuple-element.36), channel_id=1, source_target_pairs={{0,4},{1,5},{2,6},{3,7},{4,0},{5,1},{6,2},{7,3},{8,12},{9,13},{10,... | collective-permute-start | bytes 589832 | tf_op jit(solution)/shard_map/ppermute | solution.py:281
  70.2 1.5 %collective-permute-start.12 = (bf16[256,384]{1,0:T(8,128)(2,1)S(1)}, bf16[256,384]{1,0:T(8,128)(2,1)S(1)}, u32[]{:S(2)}, u32[]{:S(2)}) collective-permute-start(bf16[256,384]{1,0:T(8,128)(2,1)S(1)} %get-tuple-element.35.refs_0_), channel_id=1, source_target_pairs={{0,1},{1,0},{2,3},{3,2},{4,5},{5,4},{6,7},{7,6},{8,9},{9,8},{10,11... | collective-permute-start | bytes 589832 | tf_op jit(solution)/shard_map/ppermute | solution.py:281
  72.4 2.1 %collective-permute-done.33.refs_5_ = bf16[256,384]{1,0:T(8,128)(2,1)S(1)} collective-permute-done((bf16[256,384]{1,0:T(8,128)(2,1)S(1)}, bf16[256,384]{1,0:T(8,128)(2,1)S(1)}, u32[]{:S(2)}, u32[]{:S(2)}) %collective-permute-start.33) | collective-permute-done | bytes 196640 | tf_op jit(solution)/shard_map/ppermute | solution.py:281
  74.8 1.5 %collective-permute-start.41 = (bf16[384,256]{1,0:T(8,128)(2,1)S(1)}, bf16[384,256]{1,0:T(8,128)(2,1)S(1)}, u32[]{:S(2)}, u32[]{:S(2)}) collective-permute-start(bf16[384,256]{1,0:T(8,128)(2,1)S(1)} %get-tuple-element.32.refs_0_), channel_id=1, source_target_pairs={{0,1},{1,0},{2,3},{3,2},{4,5},{5,4},{6,7},{7,6},{8,9},{9,8},{10,11... | collective-permute-start | bytes 589832 | tf_op jit(solution)/shard_map/ppermute | solution.py:281
  76.3 3.7 %collective-permute-done.13.refs_2_ = bf16[256,384]{1,0:T(8,128)(2,1)S(1)} collective-permute-done((bf16[256,384]{1,0:T(8,128)(2,1)S(1)}, bf16[256,384]{1,0:T(8,128)(2,1)S(1)}, u32[]{:S(2)}, u32[]{:S(2)}) %collective-permute-start.13) | collective-permute-done | bytes 196640 | tf_op jit(solution)/shard_map/ppermute | solution.py:281
  85.0 2.5 %collective-permute-start.6 = (bf16[384,256]{1,0:T(8,128)(2,1)S(1)}, bf16[384,256]{1,0:T(8,128)(2,1)S(1)}, u32[]{:S(2)}, u32[]{:S(2)}) collective-permute-start(bf16[384,256]{1,0:T(8,128)(2,1)S(1)} %get-tuple-element.32.refs_0_), channel_id=1, source_target_pairs={{0,6},{1,7},{2,4},{3,5},{4,2},{5,3},{6,0},{7,1},{8,14},{9,15},{10,... | collective-permute-start | bytes 589832 | tf_op jit(solution)/shard_map/ppermute | solution.py:281
  87.8 3.2 %collective-permute-start.2 = (bf16[384,256]{1,0:T(8,128)(2,1)S(1)}, bf16[384,256]{1,0:T(8,128)(2,1)S(1)}, u32[]{:S(2)}, u32[]{:S(2)}) collective-permute-start(bf16[384,256]{1,0:T(8,128)(2,1)S(1)} %get-tuple-element.31), channel_id=1, source_target_pairs={{0,4},{1,5},{2,6},{3,7},{4,0},{5,1},{6,2},{7,3},{8,12},{9,13},{10,... | collective-permute-start | bytes 589832 | tf_op jit(solution)/shard_map/ppermute | solution.py:281
  92.0 1.5 %collective-permute-start.45 = (bf16[384,256]{1,0:T(8,128)(2,1)S(1)}, bf16[384,256]{1,0:T(8,128)(2,1)S(1)}, u32[]{:S(2)}, u32[]{:S(2)}) collective-permute-start(bf16[384,256]{1,0:T(8,128)(2,1)S(1)} %collective-permute-done.43.refs_4_), channel_id=1, source_target_pairs={{0,1},{1,0},{2,3},{3,2},{4,5},{5,4},{6,7},{7,6},{8,9},{9,8},{10,11... | collective-permute-start | bytes 589832 | tf_op jit(solution)/shard_map/ppermute | solution.py:281
  93.5 2.2 %collective-permute-done.16.refs_5_ = bf16[256,384]{1,0:T(8,128)(2,1)S(1)} collective-permute-done((bf16[256,384]{1,0:T(8,128)(2,1)S(1)}, bf16[256,384]{1,0:T(8,128)(2,1)S(1)}, u32[]{:S(2)}, u32[]{:S(2)}) %collective-permute-start.16) | collective-permute-done | bytes 196640 | tf_op jit(solution)/shard_map/ppermute | solution.py:281
  95.7 3.7 %shard_map.84.refs_16_ = f32[2,320,384]{2,1,0:T(8,128)S(1)} custom-call(bf16[256,384]{1,0:T(8,128)(2,1)S(1)} %shard_map.81.refs_0_, bf16[256,384]{1,0:T(8,128)(2,1)S(1)} %collective-permute-done.28.refs_1_, bf16[256,384]{1,0:T(8,128)(2,1)S(1)} %collective-permute-done.30.refs_2_, bf16[256,384]{1,0:T(8,128)(2,1)S(1)} %collective-permute-done.31.refs_3_, ...), custom_call_target="tpu_custom_call" | custom-call | flops 1006632960 | bytes 5177344 | tf_op jit(solution)/shard_map/pallas_call | solution.py:41
  99.4 3.8 %shard_map.85 = (bf16[320,384]{1,0:T(8,128)(2,1)S(1)}, bf16[320,384]{1,0:T(8,128)(2,1)S(1)}) custom-call(bf16[256,384]{1,0:T(8,128)(2,1)S(1)} %get-tuple-element.35.refs_0_, bf16[256,384]{1,0:T(8,128)(2,1)S(1)} %collective-permute-done.12.refs_1_, bf16[256,384]{1,0:T(8,128)(2,1)S(1)} %collective-permute-done.13.refs_2_, ...), custom_call_target="tpu_custom_call" | custom-call | flops 1006632960 | bytes 5668864 | tf_op jit(solution)/shard_map/pallas_call | solution.py:41
  105.4 1.5 %collective-permute-start.8 = (bf16[384,256]{1,0:T(8,128)(2,1)S(1)}, bf16[384,256]{1,0:T(8,128)(2,1)S(1)}, u32[]{:S(2)}, u32[]{:S(2)}) collective-permute-start(bf16[384,256]{1,0:T(8,128)(2,1)S(1)} %collective-permute-done.6.refs_4_), channel_id=1, source_target_pairs={{0,1},{1,0},{2,3},{3,2},{4,5},{5,4},{6,7},{7,6},{8,9},{9,8},{10,11... | collective-permute-start | bytes 589832 | tf_op jit(solution)/shard_map/ppermute | solution.py:281
  107.9 5.2 %collective-permute-done.8.refs_6_ = bf16[384,256]{1,0:T(8,128)(2,1)S(1)} collective-permute-done((bf16[384,256]{1,0:T(8,128)(2,1)S(1)}, bf16[384,256]{1,0:T(8,128)(2,1)S(1)}, u32[]{:S(2)}, u32[]{:S(2)}) %collective-permute-start.8) | collective-permute-done | bytes 196640 | tf_op jit(solution)/shard_map/ppermute | solution.py:281
  113.2 2.2 %collective-permute-done.4.refs_2_ = bf16[384,256]{1,0:T(8,128)(2,1)S(1)} collective-permute-done((bf16[384,256]{1,0:T(8,128)(2,1)S(1)}, bf16[384,256]{1,0:T(8,128)(2,1)S(1)}, u32[]{:S(2)}, u32[]{:S(2)}) %collective-permute-start.4) | collective-permute-done | bytes 196640 | tf_op jit(solution)/shard_map/ppermute | solution.py:281
  118.8 1.7 %collective-permute-start.49 = (bf16[80,1024]{1,0:T(8,128)(2,1)S(1)}, bf16[80,1024]{1,0:T(8,128)(2,1)S(1)}, u32[]{:S(2)}, u32[]{:S(2)}) collective-permute-start(bf16[80,1024]{1,0:T(8,128)(2,1)S(1)} %get-tuple-element.50), channel_id=1, source_target_pairs={{0,18},{1,19},{2,16},{3,17},{4,22},{5,23},{6,20},{7,21},{8,26},{9,... | collective-permute-start | bytes 491528 | tf_op jit(solution)/shard_map/ppermute | solution.py:281
  125.3 3.3 %collective-permute-done.48.refs_2_ = bf16[80,1024]{1,0:T(8,128)(2,1)S(1)} collective-permute-done((bf16[80,1024]{1,0:T(8,128)(2,1)S(1)}, bf16[80,1024]{1,0:T(8,128)(2,1)S(1)}, u32[]{:S(2)}, u32[]{:S(2)}) %collective-permute-start.48) | collective-permute-done | bytes 163872 | tf_op jit(solution)/shard_map/ppermute | solution.py:281
  128.6 2.0 %shard_map.88.refs_4_ = bf16[512,2048]{1,0:T(8,128)(2,1)} custom-call(s32[1]{0:T(128)} %bitcast.4.half, s32[1]{0:T(128)} %bitcast.1.parity, bf16[512,640]{1,0:T(8,128)(2,1)S(1)} %get-tuple-element.28.shares, bf16[80,1024]{1,0:T(8,128)(2,1)S(1)} %get-tuple-element.47.refs_0_, bf16[80,1024]{1,0:T(8,128)(2,1)S(1)} %collective-permute-done.47.refs_1_, ...), custom_call_target="tpu_custom_call" | custom-call | flops 671088640 | bytes 1310720 | tf_op jit(solution)/shard_map/pallas_call | solution.py:117
  131.1 3.5 %collective-permute-done.38.refs_2_ = bf16[80,1024]{1,0:T(8,128)(2,1)S(1)} collective-permute-done((bf16[80,1024]{1,0:T(8,128)(2,1)S(1)}, bf16[80,1024]{1,0:T(8,128)(2,1)S(1)}, u32[]{:S(2)}, u32[]{:S(2)}) %collective-permute-start.38) | collective-permute-done | bytes 163872 | tf_op jit(solution)/shard_map/ppermute | solution.py:281
  134.7 2.0 %shard_map.89 = bf16[512,2048]{1,0:T(8,128)(2,1)} custom-call(s32[1]{0:T(128)} %bitcast.half, s32[1]{0:T(128)} %bitcast.1.parity, bf16[512,640]{1,0:T(8,128)(2,1)S(1)} %get-tuple-element.28.shares, bf16[80,1024]{1,0:T(8,128)(2,1)S(1)} %get-tuple-element.43.refs_0_, ...), custom_call_target="tpu_custom_call", output_to_operand_aliasing={{}: (7, {})} | custom-call | flops 671088640 | bytes 1310720 | tf_op jit(solution)/shard_map/pallas_call | solution.py:117
  (91 shorter events, 39.0 us)
Async XLA Ops:
  7.2 11.7 %collective-permute-start.19 = (bf16[80,2048]{1,0:T(8,128)(2,1)S(1)}, bf16[80,2048]{1,0:T(8,128)(2,1)S(1)}, u32[]{:S(2)}, u32[]{:S(2)}) collective-permute-start(bf16[80,2048]{1,0:T(8,128)(2,1)S(1)} %get-tuple-element.38), channel_id=1, source_target_pairs={{0,2},{1,3},{2,0},{3,1},{4,6},{5,7},{6,4},{7,5},{8,10},{9,11},{10,... | collective-permute-start | bytes 983048 | tf_op jit(solution)/shard_map/ppermute | solution.py:281
  12.1 19.1 %collective-permute-start.26 = (bf16[4,256,384]{2,1,0:T(8,128)(2,1)S(1)}, bf16[4,256,384]{2,1,0:T(8,128)(2,1)S(1)}, u32[]{:S(2)}, u32[]{:S(2)}) collective-permute-start(bf16[4,256,384]{2,1,0:T(8,128)(2,1)S(1)} %shard_map.79), channel_id=1, source_target_pairs={{0,8},{1,9},{2,10},{3,11},{4,12},{5,13},{6,14},{7,15},{8,0},{9,1},... | collective-permute-start | bytes 2359304 | tf_op jit(solution)/shard_map/ppermute | solution.py:281
  12.2 23.9 %collective-permute-start.10 = (bf16[4,256,384]{2,1,0:T(8,128)(2,1)S(1)}, bf16[4,256,384]{2,1,0:T(8,128)(2,1)S(1)}, u32[]{:S(2)}, u32[]{:S(2)}) collective-permute-start(bf16[4,256,384]{2,1,0:T(8,128)(2,1)S(1)} %get-tuple-element.34), channel_id=1, source_target_pairs={{0,8},{1,9},{2,10},{3,11},{4,12},{5,13},{6,14},{7,15},{8,0},{9,1},... | collective-permute-start | bytes 2359304 | tf_op jit(solution)/shard_map/ppermute | solution.py:281
  12.7 16.7 %collective-permute-start.20 = (bf16[80,2048]{1,0:T(8,128)(2,1)S(1)}, bf16[80,2048]{1,0:T(8,128)(2,1)S(1)}, u32[]{:S(2)}, u32[]{:S(2)}) collective-permute-start(bf16[80,2048]{1,0:T(8,128)(2,1)S(1)} %get-tuple-element.39), channel_id=1, source_target_pairs={{0,16},{1,17},{2,18},{3,19},{4,20},{5,21},{6,22},{7,23},{8,24},{9,... | collective-permute-start | bytes 983048 | tf_op jit(solution)/shard_map/ppermute | solution.py:281
  14.2 15.2 %collective-permute-start.21 = (bf16[80,2048]{1,0:T(8,128)(2,1)S(1)}, bf16[80,2048]{1,0:T(8,128)(2,1)S(1)}, u32[]{:S(2)}, u32[]{:S(2)}) collective-permute-start(bf16[80,2048]{1,0:T(8,128)(2,1)S(1)} %get-tuple-element.40), channel_id=1, source_target_pairs={{0,18},{1,19},{2,16},{3,17},{4,22},{5,23},{6,20},{7,21},{8,26},{9,... | collective-permute-start | bytes 983048 | tf_op jit(solution)/shard_map/ppermute | solution.py:281
  18.8 25.1 %collective-permute-start = (bf16[4,384,256]{2,1,0:T(8,128)(2,1)S(1)}, bf16[4,384,256]{2,1,0:T(8,128)(2,1)S(1)}, u32[]{:S(2)}, u32[]{:S(2)}) collective-permute-start(bf16[4,384,256]{2,1,0:T(8,128)(2,1)S(1)} %get-tuple-element.30), channel_id=1, source_target_pairs={{0,8},{1,9},{2,10},{3,11},{4,12},{5,13},{6,14},{7,15},{8,0},{9,1},... | collective-permute-start | bytes 2359304 | tf_op jit(solution)/shard_map/ppermute | solution.py:281
  31.0 17.3 %collective-permute-start.24 = (bf16[80,2048]{1,0:T(8,128)(2,1)S(1)}, bf16[80,2048]{1,0:T(8,128)(2,1)S(1)}, u32[]{:S(2)}, u32[]{:S(2)}) collective-permute-start(bf16[80,2048]{1,0:T(8,128)(2,1)S(1)} %collective-permute-done.20.refs_10_), channel_id=1, source_target_pairs={{0,8},{1,9},{2,10},{3,11},{4,12},{5,13},{6,14},{7,15},{8,0},{9,1},... | collective-permute-start | bytes 983048 | tf_op jit(solution)/shard_map/ppermute | solution.py:281
  31.2 17.9 %collective-permute-start.25 = (bf16[80,2048]{1,0:T(8,128)(2,1)S(1)}, bf16[80,2048]{1,0:T(8,128)(2,1)S(1)}, u32[]{:S(2)}, u32[]{:S(2)}) collective-permute-start(bf16[80,2048]{1,0:T(8,128)(2,1)S(1)} %collective-permute-done.21.refs_11_), channel_id=1, source_target_pairs={{0,8},{1,9},{2,10},{3,11},{4,12},{5,13},{6,14},{7,15},{8,0},{9,1},... | collective-permute-start | bytes 983048 | tf_op jit(solution)/shard_map/ppermute | solution.py:281
  36.1 10.9 %collective-permute-start.29 = (bf16[1,256,384]{2,1,0:T(8,128)(2,1)S(1)}, bf16[1,256,384]{2,1,0:T(8,128)(2,1)S(1)}, u32[]{:S(2)}, u32[]{:S(2)}) collective-permute-start(bf16[1,256,384]{2,1,0:T(8,128)(2,1)S(1)} %shard_map.82), channel_id=1, source_target_pairs={{0,16},{1,17},{2,18},{3,19},{4,20},{5,21},{6,22},{7,23},{8,24},{9,... | collective-permute-start | bytes 589832 | tf_op jit(solution)/shard_map/ppermute | solution.py:281
  41.8 22.2 %collective-permute-start.11 = (bf16[2,256,384]{2,1,0:T(8,128)(2,1)S(1)}, bf16[2,256,384]{2,1,0:T(8,128)(2,1)S(1)}, u32[]{:S(2)}, u32[]{:S(2)}) collective-permute-start(bf16[2,256,384]{2,1,0:T(8,128)(2,1)S(1)} %shard_map.76), channel_id=1, source_target_pairs={{0,16},{1,17},{2,18},{3,19},{4,20},{5,21},{6,22},{7,23},{8,24},{9,... | collective-permute-start | bytes 1179656 | tf_op jit(solution)/shard_map/ppermute | solution.py:281
  47.1 20.7 %collective-permute-start.1 = (bf16[2,384,256]{2,1,0:T(8,128)(2,1)S(1)}, bf16[2,384,256]{2,1,0:T(8,128)(2,1)S(1)}, u32[]{:S(2)}, u32[]{:S(2)}) collective-permute-start(bf16[2,384,256]{2,1,0:T(8,128)(2,1)S(1)} %shard_map.74), channel_id=1, source_target_pairs={{0,16},{1,17},{2,18},{3,19},{4,20},{5,21},{6,22},{7,23},{8,24},{9,... | collective-permute-start | bytes 1179656 | tf_op jit(solution)/shard_map/ppermute | solution.py:281
  49.0 13.4 %collective-permute-start.32 = (bf16[256,384]{1,0:T(8,128)(2,1)S(1)}, bf16[256,384]{1,0:T(8,128)(2,1)S(1)}, u32[]{:S(2)}, u32[]{:S(2)}) collective-permute-start(bf16[256,384]{1,0:T(8,128)(2,1)S(1)} %shard_map.83), channel_id=1, source_target_pairs={{0,4},{1,5},{2,6},{3,7},{4,0},{5,1},{6,2},{7,3},{8,12},{9,13},{10,... | collective-permute-start | bytes 589832 | tf_op jit(solution)/shard_map/ppermute | solution.py:281
  52.0 13.1 %collective-permute-start.28 = (bf16[256,384]{1,0:T(8,128)(2,1)S(1)}, bf16[256,384]{1,0:T(8,128)(2,1)S(1)}, u32[]{:S(2)}, u32[]{:S(2)}) collective-permute-start(bf16[256,384]{1,0:T(8,128)(2,1)S(1)} %shard_map.81.refs_0_), channel_id=1, source_target_pairs={{0,1},{1,0},{2,3},{3,2},{4,5},{5,4},{6,7},{7,6},{8,9},{9,8},{10,11... | collective-permute-start | bytes 589832 | tf_op jit(solution)/shard_map/ppermute | solution.py:281
  56.2 11.6 %collective-permute-start.35 = (bf16[256,384]{1,0:T(8,128)(2,1)S(1)}, bf16[256,384]{1,0:T(8,128)(2,1)S(1)}, u32[]{:S(2)}, u32[]{:S(2)}) collective-permute-start(bf16[256,384]{1,0:T(8,128)(2,1)S(1)} %collective-permute-done.34.refs_6_), channel_id=1, source_target_pairs={{0,1},{1,0},{2,3},{3,2},{4,5},{5,4},{6,7},{7,6},{8,9},{9,8},{10,11... | collective-permute-start | bytes 589832 | tf_op jit(solution)/shard_map/ppermute | solution.py:281
  64.0 10.5 %collective-permute-start.33 = (bf16[256,384]{1,0:T(8,128)(2,1)S(1)}, bf16[256,384]{1,0:T(8,128)(2,1)S(1)}, u32[]{:S(2)}, u32[]{:S(2)}) collective-permute-start(bf16[256,384]{1,0:T(8,128)(2,1)S(1)} %collective-permute-done.32.refs_4_), channel_id=1, source_target_pairs={{0,1},{1,0},{2,3},{3,2},{4,5},{5,4},{6,7},{7,6},{8,9},{9,8},{10,11... | collective-permute-start | bytes 589832 | tf_op jit(solution)/shard_map/ppermute | solution.py:281
  67.8 12.2 %collective-permute-start.13 = (bf16[256,384]{1,0:T(8,128)(2,1)S(1)}, bf16[256,384]{1,0:T(8,128)(2,1)S(1)}, u32[]{:S(2)}, u32[]{:S(2)}) collective-permute-start(bf16[256,384]{1,0:T(8,128)(2,1)S(1)} %get-tuple-element.36), channel_id=1, source_target_pairs={{0,2},{1,3},{2,0},{3,1},{4,6},{5,7},{6,4},{7,5},{8,10},{9,11},{10,... | collective-permute-start | bytes 589832 | tf_op jit(solution)/shard_map/ppermute | solution.py:281
  67.8 14.5 %collective-permute-start.15 = (bf16[256,384]{1,0:T(8,128)(2,1)S(1)}, bf16[256,384]{1,0:T(8,128)(2,1)S(1)}, u32[]{:S(2)}, u32[]{:S(2)}) collective-permute-start(bf16[256,384]{1,0:T(8,128)(2,1)S(1)} %get-tuple-element.36), channel_id=1, source_target_pairs={{0,4},{1,5},{2,6},{3,7},{4,0},{5,1},{6,2},{7,3},{8,12},{9,13},{10,... | collective-permute-start | bytes 589832 | tf_op jit(solution)/shard_map/ppermute | solution.py:281
  70.2 13.6 %collective-permute-start.12 = (bf16[256,384]{1,0:T(8,128)(2,1)S(1)}, bf16[256,384]{1,0:T(8,128)(2,1)S(1)}, u32[]{:S(2)}, u32[]{:S(2)}) collective-permute-start(bf16[256,384]{1,0:T(8,128)(2,1)S(1)} %get-tuple-element.35.refs_0_), channel_id=1, source_target_pairs={{0,1},{1,0},{2,3},{3,2},{4,5},{5,4},{6,7},{7,6},{8,9},{9,8},{10,11... | collective-permute-start | bytes 589832 | tf_op jit(solution)/shard_map/ppermute | solution.py:281
  74.4 10.6 %collective-permute-start.43 = (bf16[384,256]{1,0:T(8,128)(2,1)S(1)}, bf16[384,256]{1,0:T(8,128)(2,1)S(1)}, u32[]{:S(2)}, u32[]{:S(2)}) collective-permute-start(bf16[384,256]{1,0:T(8,128)(2,1)S(1)} %get-tuple-element.31), channel_id=1, source_target_pairs={{0,2},{1,3},{2,0},{3,1},{4,6},{5,7},{6,4},{7,5},{8,10},{9,11},{10,... | collective-permute-start | bytes 589832 | tf_op jit(solution)/shard_map/ppermute | solution.py:281
  74.8 10.3 %collective-permute-start.41 = (bf16[384,256]{1,0:T(8,128)(2,1)S(1)}, bf16[384,256]{1,0:T(8,128)(2,1)S(1)}, u32[]{:S(2)}, u32[]{:S(2)}) collective-permute-start(bf16[384,256]{1,0:T(8,128)(2,1)S(1)} %get-tuple-element.32.refs_0_), channel_id=1, source_target_pairs={{0,1},{1,0},{2,3},{3,2},{4,5},{5,4},{6,7},{7,6},{8,9},{9,8},{10,11... | collective-permute-start | bytes 589832 | tf_op jit(solution)/shard_map/ppermute | solution.py:281
  83.8 11.9 %collective-permute-start.16 = (bf16[256,384]{1,0:T(8,128)(2,1)S(1)}, bf16[256,384]{1,0:T(8,128)(2,1)S(1)}, u32[]{:S(2)}, u32[]{:S(2)}) collective-permute-start(bf16[256,384]{1,0:T(8,128)(2,1)S(1)} %collective-permute-done.15.refs_4_), channel_id=1, source_target_pairs={{0,1},{1,0},{2,3},{3,2},{4,5},{5,4},{6,7},{7,6},{8,9},{9,8},{10,11... | collective-permute-start | bytes 589832 | tf_op jit(solution)/shard_map/ppermute | solution.py:281
  85.0 18.2 %collective-permute-start.40 = (bf16[384,256]{1,0:T(8,128)(2,1)S(1)}, bf16[384,256]{1,0:T(8,128)(2,1)S(1)}, u32[]{:S(2)}, u32[]{:S(2)}) collective-permute-start(bf16[384,256]{1,0:T(8,128)(2,1)S(1)} %get-tuple-element.32.refs_0_), channel_id=1, source_target_pairs={{0,8},{1,9},{2,10},{3,11},{4,12},{5,13},{6,14},{7,15},{8,0},{9,1},... | collective-permute-start | bytes 589832 | tf_op jit(solution)/shard_map/ppermute | solution.py:281
  85.0 18.8 %collective-permute-start.6 = (bf16[384,256]{1,0:T(8,128)(2,1)S(1)}, bf16[384,256]{1,0:T(8,128)(2,1)S(1)}, u32[]{:S(2)}, u32[]{:S(2)}) collective-permute-start(bf16[384,256]{1,0:T(8,128)(2,1)S(1)} %get-tuple-element.32.refs_0_), channel_id=1, source_target_pairs={{0,6},{1,7},{2,4},{3,5},{4,2},{5,3},{6,0},{7,1},{8,14},{9,15},{10,... | collective-permute-start | bytes 589832 | tf_op jit(solution)/shard_map/ppermute | solution.py:281
  87.8 17.6 %collective-permute-start.2 = (bf16[384,256]{1,0:T(8,128)(2,1)S(1)}, bf16[384,256]{1,0:T(8,128)(2,1)S(1)}, u32[]{:S(2)}, u32[]{:S(2)}) collective-permute-start(bf16[384,256]{1,0:T(8,128)(2,1)S(1)} %get-tuple-element.31), channel_id=1, source_target_pairs={{0,4},{1,5},{2,6},{3,7},{4,0},{5,1},{6,2},{7,3},{8,12},{9,13},{10,... | collective-permute-start | bytes 589832 | tf_op jit(solution)/shard_map/ppermute | solution.py:281
  92.0 14.9 %collective-permute-start.45 = (bf16[384,256]{1,0:T(8,128)(2,1)S(1)}, bf16[384,256]{1,0:T(8,128)(2,1)S(1)}, u32[]{:S(2)}, u32[]{:S(2)}) collective-permute-start(bf16[384,256]{1,0:T(8,128)(2,1)S(1)} %collective-permute-done.43.refs_4_), channel_id=1, source_target_pairs={{0,1},{1,0},{2,3},{3,2},{4,5},{5,4},{6,7},{7,6},{8,9},{9,8},{10,11... | collective-permute-start | bytes 589832 | tf_op jit(solution)/shard_map/ppermute | solution.py:281
  95.7 11.7 %collective-permute-start.42 = (bf16[384,256]{1,0:T(8,128)(2,1)S(1)}, bf16[384,256]{1,0:T(8,128)(2,1)S(1)}, u32[]{:S(2)}, u32[]{:S(2)}) collective-permute-start(bf16[384,256]{1,0:T(8,128)(2,1)S(1)} %collective-permute-done.41.refs_2_), channel_id=1, source_target_pairs={{0,8},{1,9},{2,10},{3,11},{4,12},{5,13},{6,14},{7,15},{8,0},{9,1},... | collective-permute-start | bytes 589832 | tf_op jit(solution)/shard_map/ppermute | solution.py:281
  103.3 12.6 %collective-permute-start.36 = (bf16[320,384]{1,0:T(8,128)(2,1)S(1)}, bf16[320,384]{1,0:T(8,128)(2,1)S(1)}, u32[]{:S(2)}, u32[]{:S(2)}) collective-permute-start(bf16[320,384]{1,0:T(8,128)(2,1)S(1)} %get-tuple-element.42), channel_id=1, source_target_pairs={{0,8},{1,9},{2,10},{3,11},{4,12},{5,13},{6,14},{7,15},{8,0},{9,1},... | collective-permute-start | bytes 737288 | tf_op jit(solution)/shard_map/ppermute | solution.py:281
  107.4 10.9 %collective-permute-start.7 = (bf16[384,256]{1,0:T(8,128)(2,1)S(1)}, bf16[384,256]{1,0:T(8,128)(2,1)S(1)}, u32[]{:S(2)}, u32[]{:S(2)}) collective-permute-start(bf16[384,256]{1,0:T(8,128)(2,1)S(1)} %collective-permute-done.6.refs_4_), channel_id=1, source_target_pairs={{0,8},{1,9},{2,10},{3,11},{4,12},{5,13},{6,14},{7,15},{8,0},{9,1},... | collective-permute-start | bytes 589832 | tf_op jit(solution)/shard_map/ppermute | solution.py:281
  118.3 10.3 %collective-permute-start.48 = (bf16[80,1024]{1,0:T(8,128)(2,1)S(1)}, bf16[80,1024]{1,0:T(8,128)(2,1)S(1)}, u32[]{:S(2)}, u32[]{:S(2)}) collective-permute-start(bf16[80,1024]{1,0:T(8,128)(2,1)S(1)} %get-tuple-element.49), channel_id=1, source_target_pairs={{0,16},{1,17},{2,18},{3,19},{4,20},{5,21},{6,22},{7,23},{8,24},{9,... | collective-permute-start | bytes 491528 | tf_op jit(solution)/shard_map/ppermute | solution.py:281
  118.8 9.8 %collective-permute-start.49 = (bf16[80,1024]{1,0:T(8,128)(2,1)S(1)}, bf16[80,1024]{1,0:T(8,128)(2,1)S(1)}, u32[]{:S(2)}, u32[]{:S(2)}) collective-permute-start(bf16[80,1024]{1,0:T(8,128)(2,1)S(1)} %get-tuple-element.50), channel_id=1, source_target_pairs={{0,18},{1,19},{2,16},{3,17},{4,22},{5,23},{6,20},{7,21},{8,26},{9,... | collective-permute-start | bytes 491528 | tf_op jit(solution)/shard_map/ppermute | solution.py:281
  122.9 11.8 %collective-permute-start.38 = (bf16[80,1024]{1,0:T(8,128)(2,1)S(1)}, bf16[80,1024]{1,0:T(8,128)(2,1)S(1)}, u32[]{:S(2)}, u32[]{:S(2)}) collective-permute-start(bf16[80,1024]{1,0:T(8,128)(2,1)S(1)} %get-tuple-element.45), channel_id=1, source_target_pairs={{0,16},{1,17},{2,18},{3,19},{4,20},{5,21},{6,22},{7,23},{8,24},{9,... | collective-permute-start | bytes 491528 | tf_op jit(solution)/shard_map/ppermute | solution.py:281
  124.1 10.6 %collective-permute-start.39 = (bf16[80,1024]{1,0:T(8,128)(2,1)S(1)}, bf16[80,1024]{1,0:T(8,128)(2,1)S(1)}, u32[]{:S(2)}, u32[]{:S(2)}) collective-permute-start(bf16[80,1024]{1,0:T(8,128)(2,1)S(1)} %get-tuple-element.46), channel_id=1, source_target_pairs={{0,18},{1,19},{2,16},{3,17},{4,22},{5,23},{6,20},{7,21},{8,26},{9,... | collective-permute-start | bytes 491528 | tf_op jit(solution)/shard_map/ppermute | solution.py:281
  (21 other events, 127.4 us)

commit v3 on v2

--- a/solution.py
+++ b/solution.py
@@ -80,9 +80,10 @@
     slots = lax.broadcasted_iota(jnp.int32, (CAP, rows), 0).astype(F32)
     taken = [slots == places[k : k + 1, :] for k in range(VISITS)]
     copy.wait()
+    ones = jnp.concatenate([jnp.where(mask, 1.0, 0.0) for mask in taken], axis=0).astype(BF16)
+    found = jnp.dot(ones, held[...], preferred_element_type=F32).astype(BF16)
     for k in range(VISITS):
-        one = jnp.where(taken[k], 1.0, 0.0).astype(BF16)
-        picks[k][...] = jnp.dot(one, held[...], preferred_element_type=F32).astype(BF16)
+        picks[k][...] = found[k * CAP : (k + 1) * CAP]
     spread = jnp.concatenate([jnp.where(taken[k], weights[k], 0.0) for k in range(VISITS)], axis=0)
     top = spread.astype(BF16).astype(F32)
     shares[...] = jnp.concatenate([top, spread - top], axis=0).T.astype(BF16)
@@ -208,57 +209,48 @@
             out[...] = far[n]
 
 
-def load_blocks(sides, keys, blocks, held, sem, spots=None):
-    _, c, _, z, y, _ = place(sides)
-    copies = []
-    for n, ((plane_bits, side_bits, core), block) in enumerate(zip(keys, blocks)):
-        rows, columns = block.shape
-        if spots is None:
-            piece = (z ^ plane_bits) * sides + (y ^ side_bits)
-            spot = held.at[pl.ds(pl.multiple_of(piece * rows, 128), rows), :]
-        else:
-            tile, moves = spots[plane_bits]
-            piece = (tile + ((z ^ plane_bits) & 1 if moves else 0)) * sides + (y ^ side_bits)
-            first = pl.ds(pl.multiple_of((c ^ core) * rows, 128), rows)
-            spot = held.at[first, pl.ds(pl.multiple_of(piece * columns, 128), columns)]
-        copies.append(pltpu.make_async_copy(block, spot, sem.at[n]))
-    for copy in copies:
-        copy.start()
-    for copy in copies:
-        copy.wait()
+def product(sides, keys, blocks, rows):
+    _, _, _, z, y, _ = place(sides)
+    total = None
+    for (plane_bits, side_bits, _), block in zip(keys, blocks):
+        size = block.shape[0]
+        piece = pl.ds(pl.multiple_of(((z ^ plane_bits) * sides + (y ^ side_bits)) * size, 128), size)
+        part = jnp.dot(
+            jnp.concatenate([ref[:, piece] for ref in rows], axis=0), block[...], preferred_element_type=F32
+        )
+        total = part if total is None else total + part
+    return total
 
 
 def gate_kernel(sides, keys, *refs):
-    blocks, rows = refs[: len(keys)], refs[len(keys) : len(keys) + 2 * VISITS]
-    out, held, sem = refs[len(keys) + 2 * VISITS :]
-    load_blocks(sides, keys, blocks, held, sem)
+    blocks, rows, out = refs[: len(keys)], refs[len(keys) : len(keys) + 2 * VISITS], refs[-1]
     for side in range(2):
-        picked = jnp.concatenate([ref[...] for ref in rows[side * VISITS : (side + 1) * VISITS]], axis=0)
-        out[side] = jnp.dot(picked, held[...], preferred_element_type=F32)
+        out[side] = product(sides, keys, blocks, rows[side * VISITS : (side + 1) * VISITS])
 
 
 def up_kernel(sides, keys, *refs):
     blocks, rows = refs[: len(keys)], refs[len(keys) : len(keys) + 2 * VISITS]
-    gate, own, partner, held, sem = refs[len(keys) + 2 * VISITS :]
-    load_blocks(sides, keys, blocks, held, sem)
+    gate, own, partner = refs[len(keys) + 2 * VISITS :]
     for side, out in enumerate((own, partner)):
-        picked = jnp.concatenate([ref[...] for ref in rows[side * VISITS : (side + 1) * VISITS]], axis=0)
-        up = jnp.dot(picked, held[...], preferred_element_type=F32)
+        up = product(sides, keys, blocks, rows[side * VISITS : (side + 1) * VISITS])
         out[...] = (jax.nn.silu(gate[side]) * up).astype(BF16)
 
 
 def down_kernel(sides, keys, spots, *refs):
     count = len(keys)
-    blocks, (own, partner), outs = refs[:count], refs[count : count + 2], refs[count + 2 : count + 2 + VISITS]
-    held, hidden, sem = refs[count + 2 + VISITS :]
-    _, c, _, _, _, _ = place(sides)
-    inner = own.shape[1]
-    hidden[:, pl.ds(pl.multiple_of(c * inner, 128), inner)] = own[...]
-    hidden[:, pl.ds(pl.multiple_of((1 - c) * inner, 128), inner)] = partner[...]
-    load_blocks(sides, keys, blocks, held, sem, spots)
-    out = jnp.dot(hidden[...], held[...], preferred_element_type=F32).astype(BF16)
-    for k in range(VISITS):
-        outs[k][...] = out[k * CAP : (k + 1) * CAP]
+    blocks, hidden, outs = refs[:count], refs[count : count + 2], refs[count + 2 :]
+    _, _, _, z, y, _ = place(sides)
+    pairs = {}
+    for (plane_bits, side_bits, core), block in zip(keys, blocks):
+        pairs.setdefault((plane_bits, side_bits), {})[core] = block
+    for (plane_bits, side_bits), pair in pairs.items():
+        part = jnp.dot(hidden[0][...], pair[0][...], preferred_element_type=F32)
+        part = (part + jnp.dot(hidden[1][...], pair[1][...], preferred_element_type=F32)).astype(BF16)
+        columns = part.shape[1]
+        tile, moves = spots[plane_bits]
+        piece = (tile + ((z ^ plane_bits) & 1 if moves else 0)) * sides + (y ^ side_bits)
+        for k in range(VISITS):
+            outs[k][:, pl.ds(pl.multiple_of(piece * columns, 128), columns)] = part[k * CAP : (k + 1) * CAP]
 
 
 def body(mesh, tokens, routing, mixing, visited, gate_matrix, up_matrix, down_matrix):
@@ -280,8 +272,7 @@
                 pairs.append((one * groups + two, (one ^ expert_bits) * groups + other))
         return lax.ppermute(value, AXES, pairs)
 
-    (theirs,) = cut(sides, visited, gate_matrix, 1, (1,))
-    (mine,) = cut(sides, visited, gate_matrix, 1, (0,))
+    theirs, mine = cut(sides, visited, gate_matrix, 1, (1, 0))
     others, axes = (up_matrix, down_matrix), (1, 0)
     outs = call(
         functools.partial(pick_kernel, sides, axes),
@@ -372,18 +363,16 @@
     gate = call(
         functools.partial(gate_kernel, sides, keys),
         shape((2, total, inner // 2), F32),
-        [ANY] * len(keys) + [VMEM] * len(rows),
+        [VMEM] * (len(keys) + len(rows)),
         (*blocks, *rows),
-        [pltpu.VMEM((width, inner // 2), BF16), pltpu.SemaphoreType.DMA((len(keys),))],
         flops=work,
     )
     keys, blocks = pieces[1]
     own, partner = call(
         functools.partial(up_kernel, sides, keys),
         [shape((total, inner // 2), BF16)] * 2,
-        [ANY] * len(keys) + [VMEM] * (len(rows) + 1),
+        [VMEM] * (len(keys) + len(rows) + 1),
         (*blocks, *rows, gate),
-        [pltpu.VMEM((width, inner // 2), BF16), pltpu.SemaphoreType.DMA((len(keys),))],
         flops=work,
     )
     partner = swap(partner, expert_bits=1)
@@ -400,13 +389,8 @@
         outs = call(
             functools.partial(down_kernel, sides, [keys[n] for n in chosen], spots),
             [shape((CAP, columns), BF16)] * VISITS,
-            [ANY] * len(chosen) + [VMEM] * 2,
+            [VMEM] * (len(chosen) + 2),
             (*(blocks[n] for n in chosen), own, partner),
-            [
-                pltpu.VMEM((inner, columns), BF16),
-                pltpu.VMEM((total, inner), BF16),
-                pltpu.SemaphoreType.DMA((len(chosen),)),
-            ],
             flops=work * len(group) // planes,
         )
         back = [

time: 137 us -> 134 us (0.978)
  Pallas kernels: 27.2 us -> 20.1 us
  waiting for transfers between devices: 57 us -> 62.2 us
  starting transfers between devices: 50.2 us -> 48.7 us
    pallas_call x15 -> x14, Pallas kernels: 23.2 us -> 16 us  [call(): pl.pallas_call(kernel, out_shape=out_shape, in_specs=in_specs, out_specs=...]
    ppermute x50, waiting for transfers between devices: 57 us -> 62.2 us  [swap(): return lax.ppermute(value, AXES, pairs)]
    ppermute x50, starting transfers between devices: 50.2 us -> 48.7 us  [swap(): return lax.ppermute(value, AXES, pairs)]
  transfers between devices with their start and end apart: 50 -> 50, of which waited for: 22 -> 24; matrix products, arithmetic and copies ran while one was open for 0% -> 0% of each run, Pallas kernels for 15% -> 10%
where the time goes in v3:
time: 134 us; the launch traced here: 133 us
  waiting for transfers between devices  62.2 us (46%)
  starting transfers between devices  48.7 us (36%)
  Pallas kernels  20.1 us (15%)
  local copies, waits for them, and re-layouts  2.09 us (2%)
    ppermute x50, waiting for transfers between devices, swap(): return lax.ppermute(value, AXES, pairs)  62.2 us
    ppermute x50, starting transfers between devices, swap(): return lax.ppermute(value, AXES, pairs)  48.7 us
    pallas_call x14, Pallas kernels, call(): pl.pallas_call(kernel, out_shape=out_shape, in_specs=in_specs, out_specs=...  16 us
    pallas_call x2, Pallas kernels, merge(): pl.pallas_call(merge_kernel, grid_spec=pltpu.PrefetchScalarGridSpec(num_s...  4.07 us
  transfers between devices with their start and end apart: 50, of which 24 were waited for; matrix products, arithmetic and copies ran while one was open for 0% of the time, Pallas kernels for 10%

profile of v3, /device:TPU:0, one launch (start us, length us, event | category | flops | bytes accessed | tf_op | source)
XLA Modules:
  0.0 133.3 jit_solution(6014938495850910289)
XLA Ops:
  2.1 4.3 %shard_map.73 = (bf16[80,2048]{1,0:T(8,128)(2,1)S(1)}, bf16[80,2048]{1,0:T(8,128)(2,1)S(1)}, bf16[80,2048]{1,0:T(8,128)(2,1)S(1)}, bf16[80,2048]{1,0:T(8,128)(2,...) custom-call(s32[4]{0:T(128)S(1)} %copy-done, ...), custom_call_target="tpu_custom_call" | custom-call | bytes 13533200 | tf_op jit(solution)/shard_map/pallas_call | solution.py:41
  6.4 3.1 %collective-permute-start.19 = (bf16[80,2048]{1,0:T(8,128)(2,1)S(1)}, bf16[80,2048]{1,0:T(8,128)(2,1)S(1)}, u32[]{:S(2)}, u32[]{:S(2)}) collective-permute-start(bf16[80,2048]{1,0:T(8,128)(2,1)S(1)} %get-tuple-element.40), channel_id=1, source_target_pairs={{0,2},{1,3},{2,0},{3,1},{4,6},{5,7},{6,4},{7,5},{8,10},{9,11},{10,... | collective-permute-start | bytes 983048 | tf_op jit(solution)/shard_map/ppermute | solution.py:273
  9.5 2.1 %shard_map.78 = (bf16[4,256,384]{2,1,0:T(8,128)(2,1)S(1)}, bf16[4,256,384]{2,1,0:T(8,128)(2,1)S(1)}) custom-call(s32[4]{0:T(128)S(1)} %copy-done, bf16[8,256,768]{2,1,0:T(8,128)(2,1)} %matrix.1), custom_call_target="tpu_custom_call" | custom-call | bytes 4718608 | tf_op jit(solution)/shard_map/pallas_call | solution.py:41
  13.7 4.4 %collective-permute-done.19.refs_9_ = bf16[80,2048]{1,0:T(8,128)(2,1)S(1)} collective-permute-done((bf16[80,2048]{1,0:T(8,128)(2,1)S(1)}, bf16[80,2048]{1,0:T(8,128)(2,1)S(1)}, u32[]{:S(2)}, u32[]{:S(2)}) %collective-permute-start.19) | collective-permute-done | bytes 327712 | tf_op jit(solution)/shard_map/ppermute | solution.py:273
  18.1 10.8 %collective-permute-done.20.refs_10_ = bf16[80,2048]{1,0:T(8,128)(2,1)S(1)} collective-permute-done((bf16[80,2048]{1,0:T(8,128)(2,1)S(1)}, bf16[80,2048]{1,0:T(8,128)(2,1)S(1)}, u32[]{:S(2)}, u32[]{:S(2)}) %collective-permute-start.20) | collective-permute-done | bytes 327712 | tf_op jit(solution)/shard_map/ppermute | solution.py:273
  31.7 1.6 %collective-permute-start.27 = (bf16[1,256,384]{2,1,0:T(8,128)(2,1)S(1)}, bf16[1,256,384]{2,1,0:T(8,128)(2,1)S(1)}, u32[]{:S(2)}, u32[]{:S(2)}) collective-permute-start(bf16[1,256,384]{2,1,0:T(8,128)(2,1)S(1)} %shard_map.79), channel_id=1, source_target_pairs={{0,16},{1,17},{2,18},{3,19},{4,20},{5,21},{6,22},{7,23},{8,24},{9,... | collective-permute-start | bytes 589832 | tf_op jit(solution)/shard_map/ppermute | solution.py:273
  35.1 4.4 %collective-permute-done.27.far = bf16[1,256,384]{2,1,0:T(8,128)(2,1)S(1)} collective-permute-done((bf16[1,256,384]{2,1,0:T(8,128)(2,1)S(1)}, bf16[1,256,384]{2,1,0:T(8,128)(2,1)S(1)}, u32[]{:S(2)}, u32[]{:S(2)}) %collective-permute-start.27) | collective-permute-done | bytes 196640 | tf_op jit(solution)/shard_map/ppermute | solution.py:273
  41.6 2.5 %collective-permute-start.34 = (bf16[256,384]{1,0:T(8,128)(2,1)S(1)}, bf16[256,384]{1,0:T(8,128)(2,1)S(1)}, u32[]{:S(2)}, u32[]{:S(2)}) collective-permute-start(bf16[256,384]{1,0:T(8,128)(2,1)S(1)} %shard_map.80.refs_0_), channel_id=1, source_target_pairs={{0,6},{1,7},{2,4},{3,5},{4,2},{5,3},{6,0},{7,1},{8,14},{9,15},{10,... | collective-permute-start | bytes 589832 | tf_op jit(solution)/shard_map/ppermute | solution.py:273
  46.8 2.2 %collective-permute-start.32 = (bf16[256,384]{1,0:T(8,128)(2,1)S(1)}, bf16[256,384]{1,0:T(8,128)(2,1)S(1)}, u32[]{:S(2)}, u32[]{:S(2)}) collective-permute-start(bf16[256,384]{1,0:T(8,128)(2,1)S(1)} %shard_map.82), channel_id=1, source_target_pairs={{0,4},{1,5},{2,6},{3,7},{4,0},{5,1},{6,2},{7,3},{8,12},{9,13},{10,... | collective-permute-start | bytes 589832 | tf_op jit(solution)/shard_map/ppermute | solution.py:273
  49.7 1.5 %collective-permute-start.28 = (bf16[256,384]{1,0:T(8,128)(2,1)S(1)}, bf16[256,384]{1,0:T(8,128)(2,1)S(1)}, u32[]{:S(2)}, u32[]{:S(2)}) collective-permute-start(bf16[256,384]{1,0:T(8,128)(2,1)S(1)} %shard_map.80.refs_0_), channel_id=1, source_target_pairs={{0,1},{1,0},{2,3},{3,2},{4,5},{5,4},{6,7},{7,6},{8,9},{9,8},{10,11... | collective-permute-start | bytes 589832 | tf_op jit(solution)/shard_map/ppermute | solution.py:273
  51.2 2.7 %collective-permute-done.30.refs_2_ = bf16[256,384]{1,0:T(8,128)(2,1)S(1)} collective-permute-done((bf16[256,384]{1,0:T(8,128)(2,1)S(1)}, bf16[256,384]{1,0:T(8,128)(2,1)S(1)}, u32[]{:S(2)}, u32[]{:S(2)}) %collective-permute-start.30) | collective-permute-done | bytes 196640 | tf_op jit(solution)/shard_map/ppermute | solution.py:273
  55.4 4.7 %collective-permute-done.32.refs_4_ = bf16[256,384]{1,0:T(8,128)(2,1)S(1)} collective-permute-done((bf16[256,384]{1,0:T(8,128)(2,1)S(1)}, bf16[256,384]{1,0:T(8,128)(2,1)S(1)}, u32[]{:S(2)}, u32[]{:S(2)}) %collective-permute-start.32) | collective-permute-done | bytes 196640 | tf_op jit(solution)/shard_map/ppermute | solution.py:273
  60.2 1.5 %collective-permute-start.31 = (bf16[256,384]{1,0:T(8,128)(2,1)S(1)}, bf16[256,384]{1,0:T(8,128)(2,1)S(1)}, u32[]{:S(2)}, u32[]{:S(2)}) collective-permute-start(bf16[256,384]{1,0:T(8,128)(2,1)S(1)} %collective-permute-done.30.refs_2_), channel_id=1, source_target_pairs={{0,1},{1,0},{2,3},{3,2},{4,5},{5,4},{6,7},{7,6},{8,9},{9,8},{10,11... | collective-permute-start | bytes 589832 | tf_op jit(solution)/shard_map/ppermute | solution.py:273
  62.8 2.7 %collective-permute-start.17 = (bf16[256,384]{1,0:T(8,128)(2,1)S(1)}, bf16[256,384]{1,0:T(8,128)(2,1)S(1)}, u32[]{:S(2)}, u32[]{:S(2)}) collective-permute-start(bf16[256,384]{1,0:T(8,128)(2,1)S(1)} %get-tuple-element.37.refs_0_), channel_id=1, source_target_pairs={{0,6},{1,7},{2,4},{3,5},{4,2},{5,3},{6,0},{7,1},{8,14},{9,15},{10,... | collective-permute-start | bytes 589832 | tf_op jit(solution)/shard_map/ppermute | solution.py:273
  65.5 2.4 %collective-permute-start.15 = (bf16[256,384]{1,0:T(8,128)(2,1)S(1)}, bf16[256,384]{1,0:T(8,128)(2,1)S(1)}, u32[]{:S(2)}, u32[]{:S(2)}) collective-permute-start(bf16[256,384]{1,0:T(8,128)(2,1)S(1)} %get-tuple-element.38), channel_id=1, source_target_pairs={{0,4},{1,5},{2,6},{3,7},{4,0},{5,1},{6,2},{7,3},{8,12},{9,13},{10,... | collective-permute-start | bytes 589832 | tf_op jit(solution)/shard_map/ppermute | solution.py:273
  70.1 2.1 %collective-permute-done.33.refs_5_ = bf16[256,384]{1,0:T(8,128)(2,1)S(1)} collective-permute-done((bf16[256,384]{1,0:T(8,128)(2,1)S(1)}, bf16[256,384]{1,0:T(8,128)(2,1)S(1)}, u32[]{:S(2)}, u32[]{:S(2)}) %collective-permute-start.33) | collective-permute-done | bytes 196640 | tf_op jit(solution)/shard_map/ppermute | solution.py:273
  74.0 3.7 %collective-permute-done.13.refs_2_ = bf16[256,384]{1,0:T(8,128)(2,1)S(1)} collective-permute-done((bf16[256,384]{1,0:T(8,128)(2,1)S(1)}, bf16[256,384]{1,0:T(8,128)(2,1)S(1)}, u32[]{:S(2)}, u32[]{:S(2)}) %collective-permute-start.13) | collective-permute-done | bytes 196640 | tf_op jit(solution)/shard_map/ppermute | solution.py:273
  77.7 1.5 %collective-permute-start.18 = (bf16[256,384]{1,0:T(8,128)(2,1)S(1)}, bf16[256,384]{1,0:T(8,128)(2,1)S(1)}, u32[]{:S(2)}, u32[]{:S(2)}) collective-permute-start(bf16[256,384]{1,0:T(8,128)(2,1)S(1)} %collective-permute-done.17.refs_6_), channel_id=1, source_target_pairs={{0,1},{1,0},{2,3},{3,2},{4,5},{5,4},{6,7},{7,6},{8,9},{9,8},{10,11... | collective-permute-start | bytes 589832 | tf_op jit(solution)/shard_map/ppermute | solution.py:273
  82.8 2.5 %collective-permute-start.6 = (bf16[384,256]{1,0:T(8,128)(2,1)S(1)}, bf16[384,256]{1,0:T(8,128)(2,1)S(1)}, u32[]{:S(2)}, u32[]{:S(2)}) collective-permute-start(bf16[384,256]{1,0:T(8,128)(2,1)S(1)} %get-tuple-element.34.refs_0_), channel_id=1, source_target_pairs={{0,6},{1,7},{2,4},{3,5},{4,2},{5,3},{6,0},{7,1},{8,14},{9,15},{10,... | collective-permute-start | bytes 589832 | tf_op jit(solution)/shard_map/ppermute | solution.py:273
  85.5 3.2 %collective-permute-start.2 = (bf16[384,256]{1,0:T(8,128)(2,1)S(1)}, bf16[384,256]{1,0:T(8,128)(2,1)S(1)}, u32[]{:S(2)}, u32[]{:S(2)}) collective-permute-start(bf16[384,256]{1,0:T(8,128)(2,1)S(1)} %get-tuple-element.33), channel_id=1, source_target_pairs={{0,4},{1,5},{2,6},{3,7},{4,0},{5,1},{6,2},{7,3},{8,12},{9,13},{10,... | collective-permute-start | bytes 589832 | tf_op jit(solution)/shard_map/ppermute | solution.py:273
  91.2 2.2 %collective-permute-done.16.refs_5_ = bf16[256,384]{1,0:T(8,128)(2,1)S(1)} collective-permute-done((bf16[256,384]{1,0:T(8,128)(2,1)S(1)}, bf16[256,384]{1,0:T(8,128)(2,1)S(1)}, u32[]{:S(2)}, u32[]{:S(2)}) %collective-permute-start.16) | collective-permute-done | bytes 196640 | tf_op jit(solution)/shard_map/ppermute | solution.py:273
  93.4 1.5 %shard_map.83.refs_16_ = f32[2,320,384]{2,1,0:T(8,128)S(1)} custom-call(bf16[256,384]{1,0:T(8,128)(2,1)S(1)} %shard_map.80.refs_0_, bf16[256,384]{1,0:T(8,128)(2,1)S(1)} %collective-permute-done.28.refs_1_, bf16[256,384]{1,0:T(8,128)(2,1)S(1)} %collective-permute-done.30.refs_2_, bf16[256,384]{1,0:T(8,128)(2,1)S(1)} %collective-permute-done.31.refs_3_, ...), custom_call_target="tpu_custom_call" | custom-call | flops 1006632960 | bytes 5177344 | tf_op jit(solution)/shard_map/pallas_call | solution.py:41
  95.0 1.5 %shard_map.84 = (bf16[320,384]{1,0:T(8,128)(2,1)S(1)}, bf16[320,384]{1,0:T(8,128)(2,1)S(1)}) custom-call(bf16[256,384]{1,0:T(8,128)(2,1)S(1)} %get-tuple-element.37.refs_0_, bf16[256,384]{1,0:T(8,128)(2,1)S(1)} %collective-permute-done.12.refs_1_, bf16[256,384]{1,0:T(8,128)(2,1)S(1)} %collective-permute-done.13.refs_2_, ...), custom_call_target="tpu_custom_call" | custom-call | flops 1006632960 | bytes 5668864 | tf_op jit(solution)/shard_map/pallas_call | solution.py:41
  97.2 5.9 %collective-permute-done.2.refs_0_ = bf16[384,256]{1,0:T(8,128)(2,1)S(1)} collective-permute-done((bf16[384,256]{1,0:T(8,128)(2,1)S(1)}, bf16[384,256]{1,0:T(8,128)(2,1)S(1)}, u32[]{:S(2)}, u32[]{:S(2)}) %collective-permute-start.2) | collective-permute-done | bytes 196640 | tf_op jit(solution)/shard_map/ppermute | solution.py:273
  105.6 5.2 %collective-permute-done.8.refs_6_ = bf16[384,256]{1,0:T(8,128)(2,1)S(1)} collective-permute-done((bf16[384,256]{1,0:T(8,128)(2,1)S(1)}, bf16[384,256]{1,0:T(8,128)(2,1)S(1)}, u32[]{:S(2)}, u32[]{:S(2)}) %collective-permute-start.8) | collective-permute-done | bytes 196640 | tf_op jit(solution)/shard_map/ppermute | solution.py:273
  110.9 2.2 %collective-permute-done.4.refs_2_ = bf16[384,256]{1,0:T(8,128)(2,1)S(1)} collective-permute-done((bf16[384,256]{1,0:T(8,128)(2,1)S(1)}, bf16[384,256]{1,0:T(8,128)(2,1)S(1)}, u32[]{:S(2)}, u32[]{:S(2)}) %collective-permute-start.4) | collective-permute-done | bytes 196640 | tf_op jit(solution)/shard_map/ppermute | solution.py:273
  115.2 2.8 %collective-permute-start.49 = (bf16[80,1024]{1,0:T(8,128)(2,1)S(1)}, bf16[80,1024]{1,0:T(8,128)(2,1)S(1)}, u32[]{:S(2)}, u32[]{:S(2)}) collective-permute-start(bf16[80,1024]{1,0:T(8,128)(2,1)S(1)} %get-tuple-element.54), channel_id=1, source_target_pairs={{0,18},{1,19},{2,16},{3,17},{4,22},{5,23},{6,20},{7,21},{8,26},{9,... | collective-permute-start | bytes 491528 | tf_op jit(solution)/shard_map/ppermute | solution.py:273
  119.6 2.0 %collective-permute-done.47.refs_1_ = bf16[80,1024]{1,0:T(8,128)(2,1)S(1)} collective-permute-done((bf16[80,1024]{1,0:T(8,128)(2,1)S(1)}, bf16[80,1024]{1,0:T(8,128)(2,1)S(1)}, u32[]{:S(2)}, u32[]{:S(2)}) %collective-permute-start.47) | collective-permute-done | bytes 163872 | tf_op jit(solution)/shard_map/ppermute | solution.py:273
  122.4 1.9 %collective-permute-done.48.refs_2_ = bf16[80,1024]{1,0:T(8,128)(2,1)S(1)} collective-permute-done((bf16[80,1024]{1,0:T(8,128)(2,1)S(1)}, bf16[80,1024]{1,0:T(8,128)(2,1)S(1)}, u32[]{:S(2)}, u32[]{:S(2)}) %collective-permute-start.48) | collective-permute-done | bytes 163872 | tf_op jit(solution)/shard_map/ppermute | solution.py:273
  125.1 2.0 %shard_map.87.refs_4_ = bf16[512,2048]{1,0:T(8,128)(2,1)} custom-call(s32[1]{0:T(128)} %bitcast.4.half, s32[1]{0:T(128)} %bitcast.1.parity, bf16[512,640]{1,0:T(8,128)(2,1)S(1)} %get-tuple-element.30.shares, bf16[80,1024]{1,0:T(8,128)(2,1)S(1)} %get-tuple-element.51.refs_0_, bf16[80,1024]{1,0:T(8,128)(2,1)S(1)} %collective-permute-done.47.refs_1_, ...), custom_call_target="tpu_custom_call" | custom-call | flops 671088640 | bytes 1310720 | tf_op jit(solution)/shard_map/pallas_call | solution.py:118
  128.7 2.5 %collective-permute-done.39.refs_3_ = bf16[80,1024]{1,0:T(8,128)(2,1)S(1)} collective-permute-done((bf16[80,1024]{1,0:T(8,128)(2,1)S(1)}, bf16[80,1024]{1,0:T(8,128)(2,1)S(1)}, u32[]{:S(2)}, u32[]{:S(2)}) %collective-permute-start.39) | collective-permute-done | bytes 163872 | tf_op jit(solution)/shard_map/ppermute | solution.py:273
  131.2 2.0 %shard_map.88 = bf16[512,2048]{1,0:T(8,128)(2,1)} custom-call(s32[1]{0:T(128)} %bitcast.half, s32[1]{0:T(128)} %bitcast.1.parity, bf16[512,640]{1,0:T(8,128)(2,1)S(1)} %get-tuple-element.30.shares, bf16[80,1024]{1,0:T(8,128)(2,1)S(1)} %get-tuple-element.47.refs_0_, ...), custom_call_target="tpu_custom_call", output_to_operand_aliasing={{}: (7, {})} | custom-call | flops 671088640 | bytes 1310720 | tf_op jit(solution)/shard_map/pallas_call | solution.py:118
  (90 shorter events, 37.1 us)
Async XLA Ops:
  6.4 11.7 %collective-permute-start.19 = (bf16[80,2048]{1,0:T(8,128)(2,1)S(1)}, bf16[80,2048]{1,0:T(8,128)(2,1)S(1)}, u32[]{:S(2)}, u32[]{:S(2)}) collective-permute-start(bf16[80,2048]{1,0:T(8,128)(2,1)S(1)} %get-tuple-element.40), channel_id=1, source_target_pairs={{0,2},{1,3},{2,0},{3,1},{4,6},{5,7},{6,4},{7,5},{8,10},{9,11},{10,... | collective-permute-start | bytes 983048 | tf_op jit(solution)/shard_map/ppermute | solution.py:273
  11.6 19.1 %collective-permute-start.26 = (bf16[4,256,384]{2,1,0:T(8,128)(2,1)S(1)}, bf16[4,256,384]{2,1,0:T(8,128)(2,1)S(1)}, u32[]{:S(2)}, u32[]{:S(2)}) collective-permute-start(bf16[4,256,384]{2,1,0:T(8,128)(2,1)S(1)} %get-tuple-element.44), channel_id=1, source_target_pairs={{0,8},{1,9},{2,10},{3,11},{4,12},{5,13},{6,14},{7,15},{8,0},{9,1},... | collective-permute-start | bytes 2359304 | tf_op jit(solution)/shard_map/ppermute | solution.py:273
  11.7 22.1 %collective-permute-start.10 = (bf16[4,256,384]{2,1,0:T(8,128)(2,1)S(1)}, bf16[4,256,384]{2,1,0:T(8,128)(2,1)S(1)}, u32[]{:S(2)}, u32[]{:S(2)}) collective-permute-start(bf16[4,256,384]{2,1,0:T(8,128)(2,1)S(1)} %get-tuple-element.36), channel_id=1, source_target_pairs={{0,8},{1,9},{2,10},{3,11},{4,12},{5,13},{6,14},{7,15},{8,0},{9,1},... | collective-permute-start | bytes 2359304 | tf_op jit(solution)/shard_map/ppermute | solution.py:273
  12.2 16.7 %collective-permute-start.20 = (bf16[80,2048]{1,0:T(8,128)(2,1)S(1)}, bf16[80,2048]{1,0:T(8,128)(2,1)S(1)}, u32[]{:S(2)}, u32[]{:S(2)}) collective-permute-start(bf16[80,2048]{1,0:T(8,128)(2,1)S(1)} %get-tuple-element.41), channel_id=1, source_target_pairs={{0,16},{1,17},{2,18},{3,19},{4,20},{5,21},{6,22},{7,23},{8,24},{9,... | collective-permute-start | bytes 983048 | tf_op jit(solution)/shard_map/ppermute | solution.py:273
  13.7 15.2 %collective-permute-start.21 = (bf16[80,2048]{1,0:T(8,128)(2,1)S(1)}, bf16[80,2048]{1,0:T(8,128)(2,1)S(1)}, u32[]{:S(2)}, u32[]{:S(2)}) collective-permute-start(bf16[80,2048]{1,0:T(8,128)(2,1)S(1)} %get-tuple-element.42), channel_id=1, source_target_pairs={{0,18},{1,19},{2,16},{3,17},{4,22},{5,23},{6,20},{7,21},{8,26},{9,... | collective-permute-start | bytes 983048 | tf_op jit(solution)/shard_map/ppermute | solution.py:273
  18.1 23.5 %collective-permute-start = (bf16[4,384,256]{2,1,0:T(8,128)(2,1)S(1)}, bf16[4,384,256]{2,1,0:T(8,128)(2,1)S(1)}, u32[]{:S(2)}, u32[]{:S(2)}) collective-permute-start(bf16[4,384,256]{2,1,0:T(8,128)(2,1)S(1)} %get-tuple-element.32), channel_id=1, source_target_pairs={{0,8},{1,9},{2,10},{3,11},{4,12},{5,13},{6,14},{7,15},{8,0},{9,1},... | collective-permute-start | bytes 2359304 | tf_op jit(solution)/shard_map/ppermute | solution.py:273
  30.6 15.4 %collective-permute-start.24 = (bf16[80,2048]{1,0:T(8,128)(2,1)S(1)}, bf16[80,2048]{1,0:T(8,128)(2,1)S(1)}, u32[]{:S(2)}, u32[]{:S(2)}) collective-permute-start(bf16[80,2048]{1,0:T(8,128)(2,1)S(1)} %collective-permute-done.20.refs_10_), channel_id=1, source_target_pairs={{0,8},{1,9},{2,10},{3,11},{4,12},{5,13},{6,14},{7,15},{8,0},{9,1},... | collective-permute-start | bytes 983048 | tf_op jit(solution)/shard_map/ppermute | solution.py:273
  30.7 16.0 %collective-permute-start.25 = (bf16[80,2048]{1,0:T(8,128)(2,1)S(1)}, bf16[80,2048]{1,0:T(8,128)(2,1)S(1)}, u32[]{:S(2)}, u32[]{:S(2)}) collective-permute-start(bf16[80,2048]{1,0:T(8,128)(2,1)S(1)} %collective-permute-done.21.refs_11_), channel_id=1, source_target_pairs={{0,8},{1,9},{2,10},{3,11},{4,12},{5,13},{6,14},{7,15},{8,0},{9,1},... | collective-permute-start | bytes 983048 | tf_op jit(solution)/shard_map/ppermute | solution.py:273
  33.8 10.9 %collective-permute-start.29 = (bf16[1,256,384]{2,1,0:T(8,128)(2,1)S(1)}, bf16[1,256,384]{2,1,0:T(8,128)(2,1)S(1)}, u32[]{:S(2)}, u32[]{:S(2)}) collective-permute-start(bf16[1,256,384]{2,1,0:T(8,128)(2,1)S(1)} %shard_map.81), channel_id=1, source_target_pairs={{0,16},{1,17},{2,18},{3,19},{4,20},{5,21},{6,22},{7,23},{8,24},{9,... | collective-permute-start | bytes 589832 | tf_op jit(solution)/shard_map/ppermute | solution.py:273
  39.5 22.2 %collective-permute-start.11 = (bf16[2,256,384]{2,1,0:T(8,128)(2,1)S(1)}, bf16[2,256,384]{2,1,0:T(8,128)(2,1)S(1)}, u32[]{:S(2)}, u32[]{:S(2)}) collective-permute-start(bf16[2,256,384]{2,1,0:T(8,128)(2,1)S(1)} %shard_map.76), channel_id=1, source_target_pairs={{0,16},{1,17},{2,18},{3,19},{4,20},{5,21},{6,22},{7,23},{8,24},{9,... | collective-permute-start | bytes 1179656 | tf_op jit(solution)/shard_map/ppermute | solution.py:273
  44.8 20.7 %collective-permute-start.1 = (bf16[2,384,256]{2,1,0:T(8,128)(2,1)S(1)}, bf16[2,384,256]{2,1,0:T(8,128)(2,1)S(1)}, u32[]{:S(2)}, u32[]{:S(2)}) collective-permute-start(bf16[2,384,256]{2,1,0:T(8,128)(2,1)S(1)} %shard_map.74), channel_id=1, source_target_pairs={{0,16},{1,17},{2,18},{3,19},{4,20},{5,21},{6,22},{7,23},{8,24},{9,... | collective-permute-start | bytes 1179656 | tf_op jit(solution)/shard_map/ppermute | solution.py:273
  46.8 13.4 %collective-permute-start.32 = (bf16[256,384]{1,0:T(8,128)(2,1)S(1)}, bf16[256,384]{1,0:T(8,128)(2,1)S(1)}, u32[]{:S(2)}, u32[]{:S(2)}) collective-permute-start(bf16[256,384]{1,0:T(8,128)(2,1)S(1)} %shard_map.82), channel_id=1, source_target_pairs={{0,4},{1,5},{2,6},{3,7},{4,0},{5,1},{6,2},{7,3},{8,12},{9,13},{10,... | collective-permute-start | bytes 589832 | tf_op jit(solution)/shard_map/ppermute | solution.py:273
  49.7 13.1 %collective-permute-start.28 = (bf16[256,384]{1,0:T(8,128)(2,1)S(1)}, bf16[256,384]{1,0:T(8,128)(2,1)S(1)}, u32[]{:S(2)}, u32[]{:S(2)}) collective-permute-start(bf16[256,384]{1,0:T(8,128)(2,1)S(1)} %shard_map.80.refs_0_), channel_id=1, source_target_pairs={{0,1},{1,0},{2,3},{3,2},{4,5},{5,4},{6,7},{7,6},{8,9},{9,8},{10,11... | collective-permute-start | bytes 589832 | tf_op jit(solution)/shard_map/ppermute | solution.py:273
  53.9 11.6 %collective-permute-start.35 = (bf16[256,384]{1,0:T(8,128)(2,1)S(1)}, bf16[256,384]{1,0:T(8,128)(2,1)S(1)}, u32[]{:S(2)}, u32[]{:S(2)}) collective-permute-start(bf16[256,384]{1,0:T(8,128)(2,1)S(1)} %collective-permute-done.34.refs_6_), channel_id=1, source_target_pairs={{0,1},{1,0},{2,3},{3,2},{4,5},{5,4},{6,7},{7,6},{8,9},{9,8},{10,11... | collective-permute-start | bytes 589832 | tf_op jit(solution)/shard_map/ppermute | solution.py:273
  61.7 10.5 %collective-permute-start.33 = (bf16[256,384]{1,0:T(8,128)(2,1)S(1)}, bf16[256,384]{1,0:T(8,128)(2,1)S(1)}, u32[]{:S(2)}, u32[]{:S(2)}) collective-permute-start(bf16[256,384]{1,0:T(8,128)(2,1)S(1)} %collective-permute-done.32.refs_4_), channel_id=1, source_target_pairs={{0,1},{1,0},{2,3},{3,2},{4,5},{5,4},{6,7},{7,6},{8,9},{9,8},{10,11... | collective-permute-start | bytes 589832 | tf_op jit(solution)/shard_map/ppermute | solution.py:273
  65.5 12.2 %collective-permute-start.13 = (bf16[256,384]{1,0:T(8,128)(2,1)S(1)}, bf16[256,384]{1,0:T(8,128)(2,1)S(1)}, u32[]{:S(2)}, u32[]{:S(2)}) collective-permute-start(bf16[256,384]{1,0:T(8,128)(2,1)S(1)} %get-tuple-element.38), channel_id=1, source_target_pairs={{0,2},{1,3},{2,0},{3,1},{4,6},{5,7},{6,4},{7,5},{8,10},{9,11},{10,... | collective-permute-start | bytes 589832 | tf_op jit(solution)/shard_map/ppermute | solution.py:273
  65.5 14.5 %collective-permute-start.15 = (bf16[256,384]{1,0:T(8,128)(2,1)S(1)}, bf16[256,384]{1,0:T(8,128)(2,1)S(1)}, u32[]{:S(2)}, u32[]{:S(2)}) collective-permute-start(bf16[256,384]{1,0:T(8,128)(2,1)S(1)} %get-tuple-element.38), channel_id=1, source_target_pairs={{0,4},{1,5},{2,6},{3,7},{4,0},{5,1},{6,2},{7,3},{8,12},{9,13},{10,... | collective-permute-start | bytes 589832 | tf_op jit(solution)/shard_map/ppermute | solution.py:273
  67.9 13.6 %collective-permute-start.12 = (bf16[256,384]{1,0:T(8,128)(2,1)S(1)}, bf16[256,384]{1,0:T(8,128)(2,1)S(1)}, u32[]{:S(2)}, u32[]{:S(2)}) collective-permute-start(bf16[256,384]{1,0:T(8,128)(2,1)S(1)} %get-tuple-element.37.refs_0_), channel_id=1, source_target_pairs={{0,1},{1,0},{2,3},{3,2},{4,5},{5,4},{6,7},{7,6},{8,9},{9,8},{10,11... | collective-permute-start | bytes 589832 | tf_op jit(solution)/shard_map/ppermute | solution.py:273
  72.1 10.6 %collective-permute-start.43 = (bf16[384,256]{1,0:T(8,128)(2,1)S(1)}, bf16[384,256]{1,0:T(8,128)(2,1)S(1)}, u32[]{:S(2)}, u32[]{:S(2)}) collective-permute-start(bf16[384,256]{1,0:T(8,128)(2,1)S(1)} %get-tuple-element.33), channel_id=1, source_target_pairs={{0,2},{1,3},{2,0},{3,1},{4,6},{5,7},{6,4},{7,5},{8,10},{9,11},{10,... | collective-permute-start | bytes 589832 | tf_op jit(solution)/shard_map/ppermute | solution.py:273
  72.5 10.3 %collective-permute-start.41 = (bf16[384,256]{1,0:T(8,128)(2,1)S(1)}, bf16[384,256]{1,0:T(8,128)(2,1)S(1)}, u32[]{:S(2)}, u32[]{:S(2)}) collective-permute-start(bf16[384,256]{1,0:T(8,128)(2,1)S(1)} %get-tuple-element.34.refs_0_), channel_id=1, source_target_pairs={{0,1},{1,0},{2,3},{3,2},{4,5},{5,4},{6,7},{7,6},{8,9},{9,8},{10,11... | collective-permute-start | bytes 589832 | tf_op jit(solution)/shard_map/ppermute | solution.py:273
  81.6 11.9 %collective-permute-start.16 = (bf16[256,384]{1,0:T(8,128)(2,1)S(1)}, bf16[256,384]{1,0:T(8,128)(2,1)S(1)}, u32[]{:S(2)}, u32[]{:S(2)}) collective-permute-start(bf16[256,384]{1,0:T(8,128)(2,1)S(1)} %collective-permute-done.15.refs_4_), channel_id=1, source_target_pairs={{0,1},{1,0},{2,3},{3,2},{4,5},{5,4},{6,7},{7,6},{8,9},{9,8},{10,11... | collective-permute-start | bytes 589832 | tf_op jit(solution)/shard_map/ppermute | solution.py:273
  82.7 13.8 %collective-permute-start.40 = (bf16[384,256]{1,0:T(8,128)(2,1)S(1)}, bf16[384,256]{1,0:T(8,128)(2,1)S(1)}, u32[]{:S(2)}, u32[]{:S(2)}) collective-permute-start(bf16[384,256]{1,0:T(8,128)(2,1)S(1)} %get-tuple-element.34.refs_0_), channel_id=1, source_target_pairs={{0,8},{1,9},{2,10},{3,11},{4,12},{5,13},{6,14},{7,15},{8,0},{9,1},... | collective-permute-start | bytes 589832 | tf_op jit(solution)/shard_map/ppermute | solution.py:273
  82.8 14.4 %collective-permute-start.6 = (bf16[384,256]{1,0:T(8,128)(2,1)S(1)}, bf16[384,256]{1,0:T(8,128)(2,1)S(1)}, u32[]{:S(2)}, u32[]{:S(2)}) collective-permute-start(bf16[384,256]{1,0:T(8,128)(2,1)S(1)} %get-tuple-element.34.refs_0_), channel_id=1, source_target_pairs={{0,6},{1,7},{2,4},{3,5},{4,2},{5,3},{6,0},{7,1},{8,14},{9,15},{10,... | collective-permute-start | bytes 589832 | tf_op jit(solution)/shard_map/ppermute | solution.py:273
  85.5 17.6 %collective-permute-start.2 = (bf16[384,256]{1,0:T(8,128)(2,1)S(1)}, bf16[384,256]{1,0:T(8,128)(2,1)S(1)}, u32[]{:S(2)}, u32[]{:S(2)}) collective-permute-start(bf16[384,256]{1,0:T(8,128)(2,1)S(1)} %get-tuple-element.33), channel_id=1, source_target_pairs={{0,4},{1,5},{2,6},{3,7},{4,0},{5,1},{6,2},{7,3},{8,12},{9,13},{10,... | collective-permute-start | bytes 589832 | tf_op jit(solution)/shard_map/ppermute | solution.py:273
  89.7 14.9 %collective-permute-start.45 = (bf16[384,256]{1,0:T(8,128)(2,1)S(1)}, bf16[384,256]{1,0:T(8,128)(2,1)S(1)}, u32[]{:S(2)}, u32[]{:S(2)}) collective-permute-start(bf16[384,256]{1,0:T(8,128)(2,1)S(1)} %collective-permute-done.43.refs_4_), channel_id=1, source_target_pairs={{0,1},{1,0},{2,3},{3,2},{4,5},{5,4},{6,7},{7,6},{8,9},{9,8},{10,11... | collective-permute-start | bytes 589832 | tf_op jit(solution)/shard_map/ppermute | solution.py:273
  93.4 11.7 %collective-permute-start.42 = (bf16[384,256]{1,0:T(8,128)(2,1)S(1)}, bf16[384,256]{1,0:T(8,128)(2,1)S(1)}, u32[]{:S(2)}, u32[]{:S(2)}) collective-permute-start(bf16[384,256]{1,0:T(8,128)(2,1)S(1)} %collective-permute-done.41.refs_2_), channel_id=1, source_target_pairs={{0,8},{1,9},{2,10},{3,11},{4,12},{5,13},{6,14},{7,15},{8,0},{9,1},... | collective-permute-start | bytes 589832 | tf_op jit(solution)/shard_map/ppermute | solution.py:273
  96.5 17.1 %collective-permute-start.36 = (bf16[320,384]{1,0:T(8,128)(2,1)S(1)}, bf16[320,384]{1,0:T(8,128)(2,1)S(1)}, u32[]{:S(2)}, u32[]{:S(2)}) collective-permute-start(bf16[320,384]{1,0:T(8,128)(2,1)S(1)} %get-tuple-element.46), channel_id=1, source_target_pairs={{0,8},{1,9},{2,10},{3,11},{4,12},{5,13},{6,14},{7,15},{8,0},{9,1},... | collective-permute-start | bytes 737288 | tf_op jit(solution)/shard_map/ppermute | solution.py:273
  114.6 9.7 %collective-permute-start.48 = (bf16[80,1024]{1,0:T(8,128)(2,1)S(1)}, bf16[80,1024]{1,0:T(8,128)(2,1)S(1)}, u32[]{:S(2)}, u32[]{:S(2)}) collective-permute-start(bf16[80,1024]{1,0:T(8,128)(2,1)S(1)} %get-tuple-element.53), channel_id=1, source_target_pairs={{0,16},{1,17},{2,18},{3,19},{4,20},{5,21},{6,22},{7,23},{8,24},{9,... | collective-permute-start | bytes 491528 | tf_op jit(solution)/shard_map/ppermute | solution.py:273
  115.2 10.0 %collective-permute-start.49 = (bf16[80,1024]{1,0:T(8,128)(2,1)S(1)}, bf16[80,1024]{1,0:T(8,128)(2,1)S(1)}, u32[]{:S(2)}, u32[]{:S(2)}) collective-permute-start(bf16[80,1024]{1,0:T(8,128)(2,1)S(1)} %get-tuple-element.54), channel_id=1, source_target_pairs={{0,18},{1,19},{2,16},{3,17},{4,22},{5,23},{6,20},{7,21},{8,26},{9,... | collective-permute-start | bytes 491528 | tf_op jit(solution)/shard_map/ppermute | solution.py:273
  118.9 9.8 %collective-permute-start.37 = (bf16[80,1024]{1,0:T(8,128)(2,1)S(1)}, bf16[80,1024]{1,0:T(8,128)(2,1)S(1)}, u32[]{:S(2)}, u32[]{:S(2)}) collective-permute-start(bf16[80,1024]{1,0:T(8,128)(2,1)S(1)} %get-tuple-element.48), channel_id=1, source_target_pairs={{0,2},{1,3},{2,0},{3,1},{4,6},{5,7},{6,4},{7,5},{8,10},{9,11},{10,... | collective-permute-start | bytes 491528 | tf_op jit(solution)/shard_map/ppermute | solution.py:273
  119.0 9.7 %collective-permute-start.38 = (bf16[80,1024]{1,0:T(8,128)(2,1)S(1)}, bf16[80,1024]{1,0:T(8,128)(2,1)S(1)}, u32[]{:S(2)}, u32[]{:S(2)}) collective-permute-start(bf16[80,1024]{1,0:T(8,128)(2,1)S(1)} %get-tuple-element.49), channel_id=1, source_target_pairs={{0,16},{1,17},{2,18},{3,19},{4,20},{5,21},{6,22},{7,23},{8,24},{9,... | collective-permute-start | bytes 491528 | tf_op jit(solution)/shard_map/ppermute | solution.py:273
  121.6 9.7 %collective-permute-start.39 = (bf16[80,1024]{1,0:T(8,128)(2,1)S(1)}, bf16[80,1024]{1,0:T(8,128)(2,1)S(1)}, u32[]{:S(2)}, u32[]{:S(2)}) collective-permute-start(bf16[80,1024]{1,0:T(8,128)(2,1)S(1)} %get-tuple-element.50), channel_id=1, source_target_pairs={{0,18},{1,19},{2,16},{3,17},{4,22},{5,23},{6,20},{7,21},{8,26},{9,... | collective-permute-start | bytes 491528 | tf_op jit(solution)/shard_map/ppermute | solution.py:273
  (21 other events, 128.1 us)

commit v4 on v3

--- a/solution.py
+++ b/solution.py
@@ -17,7 +17,7 @@
 
 STEPS = (((1,), (0,)), ((1, 0),), ((1, 0),))
 
-GROUPS = ((0, 1), (2, 3))
+GROUPS = ((0, 1), (2,), (3,))
 
 VMEM = pl.BlockSpec(memory_space=pltpu.VMEM)
 SMEM = pl.BlockSpec(memory_space=pltpu.SMEM)
@@ -273,13 +273,13 @@
         return lax.ppermute(value, AXES, pairs)
 
     theirs, mine = cut(sides, visited, gate_matrix, 1, (1, 0))
-    others, axes = (up_matrix, down_matrix), (1, 0)
+    others, axes = (up_matrix,), (1,)
     outs = call(
         functools.partial(pick_kernel, sides, axes),
         [shape((CAP, width), BF16)] * VISITS
         + [shape((count, 2 * total), BF16)]
         + [half_shape(matrix, axis) for matrix, axis in zip(others, axes) for _ in range(2)],
-        [SMEM, VMEM, VMEM] + [HBM] * 3,
+        [SMEM, VMEM, VMEM] + [HBM] * (1 + len(others)),
         (
             visited,
             routing.T,
@@ -289,13 +289,14 @@
         [
             pltpu.VMEM(tokens.shape, BF16),
             pltpu.SemaphoreType.DMA,
-            pltpu.SemaphoreType.DMA((2, 2 * VISITS)),
+            pltpu.SemaphoreType.DMA((len(others), 2 * VISITS)),
         ],
         limit=12,
     )
     picked, shares = outs[:VISITS], outs[VISITS]
+    downs = cut(sides, visited, down_matrix, 0, (0, 1))
     matrices = []
-    for mine, theirs in ((mine, theirs), outs[VISITS + 1 : VISITS + 3], outs[VISITS + 3 :]):
+    for mine, theirs in ((mine, theirs), outs[VISITS + 1 :], downs):
         bit = 4
         while bit < experts:
             got = swap(jnp.concatenate([mine, theirs], axis=0), expert_bits=bit)

time: 134 us -> 127 us (0.948)
  waiting for transfers between devices: 62.2 us -> 52.7 us
  starting transfers between devices: 48.7 us -> 51.9 us
  Pallas kernels: 20.1 us -> 21.6 us
  local copies, waits for them, and re-layouts: 2.09 us -> 0.67 us
    ppermute x50 -> x53, waiting for transfers between devices: 62.2 us -> 52.7 us  [swap(): return lax.ppermute(value, AXES, pairs)]
    ppermute x50 -> x53, starting transfers between devices: 48.7 us -> 51.9 us  [swap(): return lax.ppermute(value, AXES, pairs)]
    pallas_call x14 -> x16, Pallas kernels: 16 us -> 17.6 us  [call(): pl.pallas_call(kernel, out_shape=out_shape, in_specs=in_specs, out_specs=...]
    unnamed x6 -> x8, local copies, waits for them, and re-layouts: 2.09 us -> 0.67 us
  transfers between devices with their start and end apart: 50 -> 53, of which waited for: 24 -> 18; matrix products, arithmetic and copies ran while one was open for 0% -> 0% of each run, Pallas kernels for 10% -> 14%
where the time goes in v4:
time: 127 us
  waiting for transfers between devices  52.7 us (41%)
  starting transfers between devices  51.9 us (41%)
  Pallas kernels  21.6 us (17%)
    ppermute x53, waiting for transfers between devices, swap(): return lax.ppermute(value, AXES, pairs)  52.7 us
    ppermute x53, starting transfers between devices, swap(): return lax.ppermute(value, AXES, pairs)  51.9 us
    pallas_call x16, Pallas kernels, call(): pl.pallas_call(kernel, out_shape=out_shape, in_specs=in_specs, out_specs=...  17.6 us
    pallas_call x2, Pallas kernels, merge(): pl.pallas_call(merge_kernel, grid_spec=pltpu.PrefetchScalarGridSpec(num_s...  4 us
  transfers between devices with their start and end apart: 53, of which 18 were waited for; matrix products, arithmetic and copies ran while one was open for 0% of the time, Pallas kernels for 14%

profile of v4, /device:TPU:0, one launch (start us, length us, event | category | flops | bytes accessed | tf_op | source)
XLA Modules:
  0.0 127.2 jit_solution(13706644004949952883)
XLA Ops:
  0.7 2.1 %shard_map.79 = (bf16[4,256,384]{2,1,0:T(8,128)(2,1)S(1)}, bf16[4,256,384]{2,1,0:T(8,128)(2,1)S(1)}) custom-call(s32[4]{0:T(128)S(1)} %copy-done, bf16[8,256,768]{2,1,0:T(8,128)(2,1)} %matrix.3), custom_call_target="tpu_custom_call" | custom-call | bytes 4718608 | tf_op jit(solution)/shard_map/pallas_call | solution.py:41
  3.3 3.7 %shard_map.73 = (bf16[80,2048]{1,0:T(8,128)(2,1)S(1)}, bf16[80,2048]{1,0:T(8,128)(2,1)S(1)}, bf16[80,2048]{1,0:T(8,128)(2,1)S(1)}, bf16[80,2048]{1,0:T(8,128)(2,...) custom-call(s32[4]{0:T(128)S(1)} %copy-done.1, ...), custom_call_target="tpu_custom_call" | custom-call | bytes 8814608 | tf_op jit(solution)/shard_map/pallas_call | solution.py:41
  7.1 3.0 %collective-permute-start.15 = (bf16[80,2048]{1,0:T(8,128)(2,1)S(1)}, bf16[80,2048]{1,0:T(8,128)(2,1)S(1)}, u32[]{:S(2)}, u32[]{:S(2)}) collective-permute-start(bf16[80,2048]{1,0:T(8,128)(2,1)S(1)} %get-tuple-element.43), channel_id=1, source_target_pairs={{0,2},{1,3},{2,0},{3,1},{4,6},{5,7},{6,4},{7,5},{8,10},{9,11},{10,... | collective-permute-start | bytes 983048 | tf_op jit(solution)/shard_map/ppermute | solution.py:273
  11.7 2.1 %shard_map.74 = (bf16[4,384,256]{2,1,0:T(8,128)(2,1)S(1)}, bf16[4,384,256]{2,1,0:T(8,128)(2,1)S(1)}) custom-call(s32[4]{0:T(128)S(1)} %copy-done.1, bf16[8,768,256]{2,1,0:T(8,128)(2,1)} %matrix.2), custom_call_target="tpu_custom_call" | custom-call | bytes 4718608 | tf_op jit(solution)/shard_map/pallas_call | solution.py:41
  13.8 4.3 %collective-permute-done.15.refs_9_ = bf16[80,2048]{1,0:T(8,128)(2,1)S(1)} collective-permute-done((bf16[80,2048]{1,0:T(8,128)(2,1)S(1)}, bf16[80,2048]{1,0:T(8,128)(2,1)S(1)}, u32[]{:S(2)}, u32[]{:S(2)}) %collective-permute-start.15) | collective-permute-done | bytes 327712 | tf_op jit(solution)/shard_map/ppermute | solution.py:273
  18.1 2.7 %collective-permute-start.17 = (bf16[80,2048]{1,0:T(8,128)(2,1)S(1)}, bf16[80,2048]{1,0:T(8,128)(2,1)S(1)}, u32[]{:S(2)}, u32[]{:S(2)}) collective-permute-start(bf16[80,2048]{1,0:T(8,128)(2,1)S(1)} %get-tuple-element.45), channel_id=1, source_target_pairs={{0,18},{1,19},{2,16},{3,17},{4,22},{5,23},{6,20},{7,21},{8,26},{9,... | collective-permute-start | bytes 983048 | tf_op jit(solution)/shard_map/ppermute | solution.py:273
  21.9 6.2 %collective-permute-done.17.refs_11_ = bf16[80,2048]{1,0:T(8,128)(2,1)S(1)} collective-permute-done((bf16[80,2048]{1,0:T(8,128)(2,1)S(1)}, bf16[80,2048]{1,0:T(8,128)(2,1)S(1)}, u32[]{:S(2)}, u32[]{:S(2)}) %collective-permute-start.17) | collective-permute-done | bytes 327712 | tf_op jit(solution)/shard_map/ppermute | solution.py:273
  32.0 2.3 %collective-permute-done.23.far = bf16[1,256,384]{2,1,0:T(8,128)(2,1)S(1)} collective-permute-done((bf16[1,256,384]{2,1,0:T(8,128)(2,1)S(1)}, bf16[1,256,384]{2,1,0:T(8,128)(2,1)S(1)}, u32[]{:S(2)}, u32[]{:S(2)}) %collective-permute-start.23) | collective-permute-done | bytes 196640 | tf_op jit(solution)/shard_map/ppermute | solution.py:273
  34.3 2.1 %collective-permute-start.7 = (bf16[2,256,384]{2,1,0:T(8,128)(2,1)S(1)}, bf16[2,256,384]{2,1,0:T(8,128)(2,1)S(1)}, u32[]{:S(2)}, u32[]{:S(2)}) collective-permute-start(bf16[2,256,384]{2,1,0:T(8,128)(2,1)S(1)} %shard_map.77), channel_id=1, source_target_pairs={{0,16},{1,17},{2,18},{3,19},{4,20},{5,21},{6,22},{7,23},{8,24},{9,... | collective-permute-start | bytes 1179656 | tf_op jit(solution)/shard_map/ppermute | solution.py:273
  37.0 3.8 %collective-permute-start.30 = (bf16[256,384]{1,0:T(8,128)(2,1)S(1)}, bf16[256,384]{1,0:T(8,128)(2,1)S(1)}, u32[]{:S(2)}, u32[]{:S(2)}) collective-permute-start(bf16[256,384]{1,0:T(8,128)(2,1)S(1)} %shard_map.81.refs_0_), channel_id=1, source_target_pairs={{0,6},{1,7},{2,4},{3,5},{4,2},{5,3},{6,0},{7,1},{8,14},{9,15},{10,... | collective-permute-start | bytes 589832 | tf_op jit(solution)/shard_map/ppermute | solution.py:273
  42.9 2.6 %collective-permute-start.28 = (bf16[256,384]{1,0:T(8,128)(2,1)S(1)}, bf16[256,384]{1,0:T(8,128)(2,1)S(1)}, u32[]{:S(2)}, u32[]{:S(2)}) collective-permute-start(bf16[256,384]{1,0:T(8,128)(2,1)S(1)} %shard_map.83), channel_id=1, source_target_pairs={{0,4},{1,5},{2,6},{3,7},{4,0},{5,1},{6,2},{7,3},{8,12},{9,13},{10,... | collective-permute-start | bytes 589832 | tf_op jit(solution)/shard_map/ppermute | solution.py:273
  51.2 3.1 %collective-permute-done.28.refs_4_ = bf16[256,384]{1,0:T(8,128)(2,1)S(1)} collective-permute-done((bf16[256,384]{1,0:T(8,128)(2,1)S(1)}, bf16[256,384]{1,0:T(8,128)(2,1)S(1)}, u32[]{:S(2)}, u32[]{:S(2)}) %collective-permute-start.28) | collective-permute-done | bytes 196640 | tf_op jit(solution)/shard_map/ppermute | solution.py:273
  55.9 2.5 %collective-permute-start.13 = (bf16[256,384]{1,0:T(8,128)(2,1)S(1)}, bf16[256,384]{1,0:T(8,128)(2,1)S(1)}, u32[]{:S(2)}, u32[]{:S(2)}) collective-permute-start(bf16[256,384]{1,0:T(8,128)(2,1)S(1)} %get-tuple-element.40.refs_0_), channel_id=1, source_target_pairs={{0,6},{1,7},{2,4},{3,5},{4,2},{5,3},{6,0},{7,1},{8,14},{9,15},{10,... | collective-permute-start | bytes 589832 | tf_op jit(solution)/shard_map/ppermute | solution.py:273
  58.4 1.9 %collective-permute-start.11 = (bf16[256,384]{1,0:T(8,128)(2,1)S(1)}, bf16[256,384]{1,0:T(8,128)(2,1)S(1)}, u32[]{:S(2)}, u32[]{:S(2)}) collective-permute-start(bf16[256,384]{1,0:T(8,128)(2,1)S(1)} %get-tuple-element.41), channel_id=1, source_target_pairs={{0,4},{1,5},{2,6},{3,7},{4,0},{5,1},{6,2},{7,3},{8,12},{9,13},{10,... | collective-permute-start | bytes 589832 | tf_op jit(solution)/shard_map/ppermute | solution.py:273
  62.6 2.9 %collective-permute-done.29.refs_5_ = bf16[256,384]{1,0:T(8,128)(2,1)S(1)} collective-permute-done((bf16[256,384]{1,0:T(8,128)(2,1)S(1)}, bf16[256,384]{1,0:T(8,128)(2,1)S(1)}, u32[]{:S(2)}, u32[]{:S(2)}) %collective-permute-start.29) | collective-permute-done | bytes 196640 | tf_op jit(solution)/shard_map/ppermute | solution.py:273
  65.6 1.6 %collective-permute-start.46 = (bf16[384,256]{1,0:T(8,128)(2,1)S(1)}, bf16[384,256]{1,0:T(8,128)(2,1)S(1)}, u32[]{:S(2)}, u32[]{:S(2)}) collective-permute-start(bf16[384,256]{1,0:T(8,128)(2,1)S(1)} %get-tuple-element.37), channel_id=1, source_target_pairs={{0,2},{1,3},{2,0},{3,1},{4,6},{5,7},{6,4},{7,5},{8,10},{9,11},{10,... | collective-permute-start | bytes 589832 | tf_op jit(solution)/shard_map/ppermute | solution.py:273
  67.1 2.3 %collective-permute-start.44 = (bf16[384,256]{1,0:T(8,128)(2,1)S(1)}, bf16[384,256]{1,0:T(8,128)(2,1)S(1)}, u32[]{:S(2)}, u32[]{:S(2)}) collective-permute-start(bf16[384,256]{1,0:T(8,128)(2,1)S(1)} %get-tuple-element.54.refs_0_), channel_id=1, source_target_pairs={{0,1},{1,0},{2,3},{3,2},{4,5},{5,4},{6,7},{7,6},{8,9},{9,8},{10,11... | collective-permute-start | bytes 589832 | tf_op jit(solution)/shard_map/ppermute | solution.py:273
  70.2 3.6 %collective-permute-done.11.refs_4_ = bf16[256,384]{1,0:T(8,128)(2,1)S(1)} collective-permute-done((bf16[256,384]{1,0:T(8,128)(2,1)S(1)}, bf16[256,384]{1,0:T(8,128)(2,1)S(1)}, u32[]{:S(2)}, u32[]{:S(2)}) %collective-permute-start.11) | collective-permute-done | bytes 196640 | tf_op jit(solution)/shard_map/ppermute | solution.py:273
  78.5 4.1 %collective-permute-done.36.refs_0_ = bf16[384,256]{1,0:T(8,128)(2,1)S(1)} collective-permute-done((bf16[384,256]{1,0:T(8,128)(2,1)S(1)}, bf16[384,256]{1,0:T(8,128)(2,1)S(1)}, u32[]{:S(2)}, u32[]{:S(2)}) %collective-permute-start.36) | collective-permute-done | bytes 196640 | tf_op jit(solution)/shard_map/ppermute | solution.py:273
  83.1 8.0 %collective-permute-done.2.refs_0_ = bf16[384,256]{1,0:T(8,128)(2,1)S(1)} collective-permute-done((bf16[384,256]{1,0:T(8,128)(2,1)S(1)}, bf16[384,256]{1,0:T(8,128)(2,1)S(1)}, u32[]{:S(2)}, u32[]{:S(2)}) %collective-permute-start.2) | collective-permute-done | bytes 196640 | tf_op jit(solution)/shard_map/ppermute | solution.py:273
  92.0 1.5 %shard_map.84.refs_16_ = f32[2,320,384]{2,1,0:T(8,128)S(1)} custom-call(bf16[256,384]{1,0:T(8,128)(2,1)S(1)} %shard_map.81.refs_0_, bf16[256,384]{1,0:T(8,128)(2,1)S(1)} %collective-permute-done.24.refs_1_, bf16[256,384]{1,0:T(8,128)(2,1)S(1)} %collective-permute-done.26.refs_2_, bf16[256,384]{1,0:T(8,128)(2,1)S(1)} %collective-permute-done.27.refs_3_, ...), custom_call_target="tpu_custom_call" | custom-call | flops 1006632960 | bytes 5177344 | tf_op jit(solution)/shard_map/pallas_call | solution.py:41
  93.6 1.7 %collective-permute-start.4 = (bf16[384,256]{1,0:T(8,128)(2,1)S(1)}, bf16[384,256]{1,0:T(8,128)(2,1)S(1)}, u32[]{:S(2)}, u32[]{:S(2)}) collective-permute-start(bf16[384,256]{1,0:T(8,128)(2,1)S(1)} %collective-permute-done.2.refs_0_), channel_id=1, source_target_pairs={{0,1},{1,0},{2,3},{3,2},{4,5},{5,4},{6,7},{7,6},{8,9},{9,8},{10,11... | collective-permute-start | bytes 589832 | tf_op jit(solution)/shard_map/ppermute | solution.py:273
  95.3 1.5 %shard_map.85 = (bf16[320,384]{1,0:T(8,128)(2,1)S(1)}, bf16[320,384]{1,0:T(8,128)(2,1)S(1)}) custom-call(bf16[256,384]{1,0:T(8,128)(2,1)S(1)} %get-tuple-element.40.refs_0_, bf16[256,384]{1,0:T(8,128)(2,1)S(1)} %collective-permute-done.8.refs_1_, bf16[256,384]{1,0:T(8,128)(2,1)S(1)} %collective-permute-done.9.refs_2_, ...), custom_call_target="tpu_custom_call" | custom-call | flops 1006632960 | bytes 5668864 | tf_op jit(solution)/shard_map/pallas_call | solution.py:41
  97.5 2.7 %collective-permute-done.38.refs_2_ = bf16[384,256]{1,0:T(8,128)(2,1)S(1)} collective-permute-done((bf16[384,256]{1,0:T(8,128)(2,1)S(1)}, bf16[384,256]{1,0:T(8,128)(2,1)S(1)}, u32[]{:S(2)}, u32[]{:S(2)}) %collective-permute-start.38) | collective-permute-done | bytes 196640 | tf_op jit(solution)/shard_map/ppermute | solution.py:273
  100.2 3.4 %collective-permute-done.4.refs_2_ = bf16[384,256]{1,0:T(8,128)(2,1)S(1)} collective-permute-done((bf16[384,256]{1,0:T(8,128)(2,1)S(1)}, bf16[384,256]{1,0:T(8,128)(2,1)S(1)}, u32[]{:S(2)}, u32[]{:S(2)}) %collective-permute-start.4) | collective-permute-done | bytes 196640 | tf_op jit(solution)/shard_map/ppermute | solution.py:273
  105.1 3.4 %collective-permute-start.52 = (bf16[80,1024]{1,0:T(8,128)(2,1)S(1)}, bf16[80,1024]{1,0:T(8,128)(2,1)S(1)}, u32[]{:S(2)}, u32[]{:S(2)}) collective-permute-start(bf16[80,1024]{1,0:T(8,128)(2,1)S(1)} %get-tuple-element.62), channel_id=1, source_target_pairs={{0,18},{1,19},{2,16},{3,17},{4,22},{5,23},{6,20},{7,21},{8,26},{9,... | collective-permute-start | bytes 491528 | tf_op jit(solution)/shard_map/ppermute | solution.py:273
  110.2 6.3 %collective-permute-done.40.refs_5_ = bf16[80,512]{1,0:T(8,128)(2,1)S(1)} collective-permute-done((bf16[80,512]{1,0:T(8,128)(2,1)S(1)}, bf16[80,512]{1,0:T(8,128)(2,1)S(1)}, u32[]{:S(2)}, u32[]{:S(2)}) %collective-permute-start.40) | collective-permute-done | bytes 81952 | tf_op jit(solution)/shard_map/ppermute | solution.py:273
  117.7 2.2 %collective-permute-start.34 = (bf16[80,512]{1,0:T(8,128)(2,1)S(1)}, bf16[80,512]{1,0:T(8,128)(2,1)S(1)}, u32[]{:S(2)}, u32[]{:S(2)}) collective-permute-start(bf16[80,512]{1,0:T(8,128)(2,1)S(1)} %get-tuple-element.52), channel_id=1, source_target_pairs={{0,16},{1,17},{2,18},{3,19},{4,20},{5,21},{6,22},{7,23},{8,24},{9,... | collective-permute-start | bytes 245768 | tf_op jit(solution)/shard_map/ppermute | solution.py:273
  119.9 2.0 %shard_map.89.refs_8_ = bf16[512,2048]{1,0:T(8,128)(2,1)} custom-call(s32[1]{0:T(128)} %bitcast.4.half, s32[1]{0:T(128)} %bitcast.1.parity, bf16[512,640]{1,0:T(8,128)(2,1)S(1)} %get-tuple-element.34.shares, bf16[80,1024]{1,0:T(8,128)(2,1)S(1)} %get-tuple-element.59.refs_0_, bf16[80,1024]{1,0:T(8,128)(2,1)S(1)} %collective-permute-done.50.refs_1_, ...), custom_call_target="tpu_custom_call" | custom-call | flops 671088640 | bytes 1310720 | tf_op jit(solution)/shard_map/pallas_call | solution.py:118
  122.0 1.5 %collective-permute-done.34.refs_2_ = bf16[80,512]{1,0:T(8,128)(2,1)S(1)} collective-permute-done((bf16[80,512]{1,0:T(8,128)(2,1)S(1)}, bf16[80,512]{1,0:T(8,128)(2,1)S(1)}, u32[]{:S(2)}, u32[]{:S(2)}) %collective-permute-start.34) | collective-permute-done | bytes 81952 | tf_op jit(solution)/shard_map/ppermute | solution.py:273
  123.5 1.7 %collective-permute-done.35.refs_3_ = bf16[80,512]{1,0:T(8,128)(2,1)S(1)} collective-permute-done((bf16[80,512]{1,0:T(8,128)(2,1)S(1)}, bf16[80,512]{1,0:T(8,128)(2,1)S(1)}, u32[]{:S(2)}, u32[]{:S(2)}) %collective-permute-start.35) | collective-permute-done | bytes 81952 | tf_op jit(solution)/shard_map/ppermute | solution.py:273
  125.3 2.0 %shard_map.90 = bf16[512,2048]{1,0:T(8,128)(2,1)} custom-call(s32[1]{0:T(128)} %bitcast.half, s32[1]{0:T(128)} %bitcast.1.parity, bf16[512,640]{1,0:T(8,128)(2,1)S(1)} %get-tuple-element.34.shares, bf16[80,512]{1,0:T(8,128)(2,1)S(1)} %get-tuple-element.50.refs_0_, ...), custom_call_target="tpu_custom_call", output_to_operand_aliasing={{}: (11, {})} | custom-call | flops 671088640 | bytes 1310720 | tf_op jit(solution)/shard_map/pallas_call | solution.py:118
  (100 shorter events, 32.1 us)
Async XLA Ops:
  2.8 18.0 %collective-permute-start.22 = (bf16[4,256,384]{2,1,0:T(8,128)(2,1)S(1)}, bf16[4,256,384]{2,1,0:T(8,128)(2,1)S(1)}, u32[]{:S(2)}, u32[]{:S(2)}) collective-permute-start(bf16[4,256,384]{2,1,0:T(8,128)(2,1)S(1)} %get-tuple-element.47), channel_id=1, source_target_pairs={{0,8},{1,9},{2,10},{3,11},{4,12},{5,13},{6,14},{7,15},{8,0},{9,1},... | collective-permute-start | bytes 2359304 | tf_op jit(solution)/shard_map/ppermute | solution.py:273
  7.0 23.6 %collective-permute-start.6 = (bf16[4,256,384]{2,1,0:T(8,128)(2,1)S(1)}, bf16[4,256,384]{2,1,0:T(8,128)(2,1)S(1)}, u32[]{:S(2)}, u32[]{:S(2)}) collective-permute-start(bf16[4,256,384]{2,1,0:T(8,128)(2,1)S(1)} %get-tuple-element.39), channel_id=1, source_target_pairs={{0,8},{1,9},{2,10},{3,11},{4,12},{5,13},{6,14},{7,15},{8,0},{9,1},... | collective-permute-start | bytes 2359304 | tf_op jit(solution)/shard_map/ppermute | solution.py:273
  7.1 11.0 %collective-permute-start.15 = (bf16[80,2048]{1,0:T(8,128)(2,1)S(1)}, bf16[80,2048]{1,0:T(8,128)(2,1)S(1)}, u32[]{:S(2)}, u32[]{:S(2)}) collective-permute-start(bf16[80,2048]{1,0:T(8,128)(2,1)S(1)} %get-tuple-element.43), channel_id=1, source_target_pairs={{0,2},{1,3},{2,0},{3,1},{4,6},{5,7},{6,4},{7,5},{8,10},{9,11},{10,... | collective-permute-start | bytes 983048 | tf_op jit(solution)/shard_map/ppermute | solution.py:273
  10.2 10.6 %collective-permute-start.16 = (bf16[80,2048]{1,0:T(8,128)(2,1)S(1)}, bf16[80,2048]{1,0:T(8,128)(2,1)S(1)}, u32[]{:S(2)}, u32[]{:S(2)}) collective-permute-start(bf16[80,2048]{1,0:T(8,128)(2,1)S(1)} %get-tuple-element.44), channel_id=1, source_target_pairs={{0,16},{1,17},{2,18},{3,19},{4,20},{5,21},{6,22},{7,23},{8,24},{9,... | collective-permute-start | bytes 983048 | tf_op jit(solution)/shard_map/ppermute | solution.py:273
  13.8 23.2 %collective-permute-start = (bf16[4,384,256]{2,1,0:T(8,128)(2,1)S(1)}, bf16[4,384,256]{2,1,0:T(8,128)(2,1)S(1)}, u32[]{:S(2)}, u32[]{:S(2)}) collective-permute-start(bf16[4,384,256]{2,1,0:T(8,128)(2,1)S(1)} %get-tuple-element.36), channel_id=1, source_target_pairs={{0,8},{1,9},{2,10},{3,11},{4,12},{5,13},{6,14},{7,15},{8,0},{9,1},... | collective-permute-start | bytes 2359304 | tf_op jit(solution)/shard_map/ppermute | solution.py:273
  18.1 10.0 %collective-permute-start.17 = (bf16[80,2048]{1,0:T(8,128)(2,1)S(1)}, bf16[80,2048]{1,0:T(8,128)(2,1)S(1)}, u32[]{:S(2)}, u32[]{:S(2)}) collective-permute-start(bf16[80,2048]{1,0:T(8,128)(2,1)S(1)} %get-tuple-element.45), channel_id=1, source_target_pairs={{0,18},{1,19},{2,16},{3,17},{4,22},{5,23},{6,20},{7,21},{8,26},{9,... | collective-permute-start | bytes 983048 | tf_op jit(solution)/shard_map/ppermute | solution.py:273
  29.5 12.5 %collective-permute-start.20 = (bf16[80,2048]{1,0:T(8,128)(2,1)S(1)}, bf16[80,2048]{1,0:T(8,128)(2,1)S(1)}, u32[]{:S(2)}, u32[]{:S(2)}) collective-permute-start(bf16[80,2048]{1,0:T(8,128)(2,1)S(1)} %collective-permute-done.16.refs_10_), channel_id=1, source_target_pairs={{0,8},{1,9},{2,10},{3,11},{4,12},{5,13},{6,14},{7,15},{8,0},{9,1},... | collective-permute-start | bytes 983048 | tf_op jit(solution)/shard_map/ppermute | solution.py:273
  29.5 13.4 %collective-permute-start.21 = (bf16[80,2048]{1,0:T(8,128)(2,1)S(1)}, bf16[80,2048]{1,0:T(8,128)(2,1)S(1)}, u32[]{:S(2)}, u32[]{:S(2)}) collective-permute-start(bf16[80,2048]{1,0:T(8,128)(2,1)S(1)} %collective-permute-done.17.refs_11_), channel_id=1, source_target_pairs={{0,8},{1,9},{2,10},{3,11},{4,12},{5,13},{6,14},{7,15},{8,0},{9,1},... | collective-permute-start | bytes 983048 | tf_op jit(solution)/shard_map/ppermute | solution.py:273
  30.6 10.7 %collective-permute-start.25 = (bf16[1,256,384]{2,1,0:T(8,128)(2,1)S(1)}, bf16[1,256,384]{2,1,0:T(8,128)(2,1)S(1)}, u32[]{:S(2)}, u32[]{:S(2)}) collective-permute-start(bf16[1,256,384]{2,1,0:T(8,128)(2,1)S(1)} %shard_map.82), channel_id=1, source_target_pairs={{0,16},{1,17},{2,18},{3,19},{4,20},{5,21},{6,22},{7,23},{8,24},{9,... | collective-permute-start | bytes 589832 | tf_op jit(solution)/shard_map/ppermute | solution.py:273
  34.3 13.3 %collective-permute-start.7 = (bf16[2,256,384]{2,1,0:T(8,128)(2,1)S(1)}, bf16[2,256,384]{2,1,0:T(8,128)(2,1)S(1)}, u32[]{:S(2)}, u32[]{:S(2)}) collective-permute-start(bf16[2,256,384]{2,1,0:T(8,128)(2,1)S(1)} %shard_map.77), channel_id=1, source_target_pairs={{0,16},{1,17},{2,18},{3,19},{4,20},{5,21},{6,22},{7,23},{8,24},{9,... | collective-permute-start | bytes 1179656 | tf_op jit(solution)/shard_map/ppermute | solution.py:273
  41.4 17.0 %collective-permute-start.1 = (bf16[2,384,256]{2,1,0:T(8,128)(2,1)S(1)}, bf16[2,384,256]{2,1,0:T(8,128)(2,1)S(1)}, u32[]{:S(2)}, u32[]{:S(2)}) collective-permute-start(bf16[2,384,256]{2,1,0:T(8,128)(2,1)S(1)} %shard_map.75), channel_id=1, source_target_pairs={{0,16},{1,17},{2,18},{3,19},{4,20},{5,21},{6,22},{7,23},{8,24},{9,... | collective-permute-start | bytes 1179656 | tf_op jit(solution)/shard_map/ppermute | solution.py:273
  42.9 11.4 %collective-permute-start.28 = (bf16[256,384]{1,0:T(8,128)(2,1)S(1)}, bf16[256,384]{1,0:T(8,128)(2,1)S(1)}, u32[]{:S(2)}, u32[]{:S(2)}) collective-permute-start(bf16[256,384]{1,0:T(8,128)(2,1)S(1)} %shard_map.83), channel_id=1, source_target_pairs={{0,4},{1,5},{2,6},{3,7},{4,0},{5,1},{6,2},{7,3},{8,12},{9,13},{10,... | collective-permute-start | bytes 589832 | tf_op jit(solution)/shard_map/ppermute | solution.py:273
  46.1 9.8 %collective-permute-start.24 = (bf16[256,384]{1,0:T(8,128)(2,1)S(1)}, bf16[256,384]{1,0:T(8,128)(2,1)S(1)}, u32[]{:S(2)}, u32[]{:S(2)}) collective-permute-start(bf16[256,384]{1,0:T(8,128)(2,1)S(1)} %shard_map.81.refs_0_), channel_id=1, source_target_pairs={{0,1},{1,0},{2,3},{3,2},{4,5},{5,4},{6,7},{7,6},{8,9},{9,8},{10,11... | collective-permute-start | bytes 589832 | tf_op jit(solution)/shard_map/ppermute | solution.py:273
  47.6 10.8 %collective-permute-start.31 = (bf16[256,384]{1,0:T(8,128)(2,1)S(1)}, bf16[256,384]{1,0:T(8,128)(2,1)S(1)}, u32[]{:S(2)}, u32[]{:S(2)}) collective-permute-start(bf16[256,384]{1,0:T(8,128)(2,1)S(1)} %collective-permute-done.30.refs_6_), channel_id=1, source_target_pairs={{0,1},{1,0},{2,3},{3,2},{4,5},{5,4},{6,7},{7,6},{8,9},{9,8},{10,11... | collective-permute-start | bytes 589832 | tf_op jit(solution)/shard_map/ppermute | solution.py:273
  49.7 11.6 %collective-permute-start.27 = (bf16[256,384]{1,0:T(8,128)(2,1)S(1)}, bf16[256,384]{1,0:T(8,128)(2,1)S(1)}, u32[]{:S(2)}, u32[]{:S(2)}) collective-permute-start(bf16[256,384]{1,0:T(8,128)(2,1)S(1)} %collective-permute-done.26.refs_2_), channel_id=1, source_target_pairs={{0,1},{1,0},{2,3},{3,2},{4,5},{5,4},{6,7},{7,6},{8,9},{9,8},{10,11... | collective-permute-start | bytes 589832 | tf_op jit(solution)/shard_map/ppermute | solution.py:273
  54.4 11.2 %collective-permute-start.29 = (bf16[256,384]{1,0:T(8,128)(2,1)S(1)}, bf16[256,384]{1,0:T(8,128)(2,1)S(1)}, u32[]{:S(2)}, u32[]{:S(2)}) collective-permute-start(bf16[256,384]{1,0:T(8,128)(2,1)S(1)} %collective-permute-done.28.refs_4_), channel_id=1, source_target_pairs={{0,1},{1,0},{2,3},{3,2},{4,5},{5,4},{6,7},{7,6},{8,9},{9,8},{10,11... | collective-permute-start | bytes 589832 | tf_op jit(solution)/shard_map/ppermute | solution.py:273
  55.9 11.2 %collective-permute-start.13 = (bf16[256,384]{1,0:T(8,128)(2,1)S(1)}, bf16[256,384]{1,0:T(8,128)(2,1)S(1)}, u32[]{:S(2)}, u32[]{:S(2)}) collective-permute-start(bf16[256,384]{1,0:T(8,128)(2,1)S(1)} %get-tuple-element.40.refs_0_), channel_id=1, source_target_pairs={{0,6},{1,7},{2,4},{3,5},{4,2},{5,3},{6,0},{7,1},{8,14},{9,15},{10,... | collective-permute-start | bytes 589832 | tf_op jit(solution)/shard_map/ppermute | solution.py:273
  58.4 11.8 %collective-permute-start.9 = (bf16[256,384]{1,0:T(8,128)(2,1)S(1)}, bf16[256,384]{1,0:T(8,128)(2,1)S(1)}, u32[]{:S(2)}, u32[]{:S(2)}) collective-permute-start(bf16[256,384]{1,0:T(8,128)(2,1)S(1)} %get-tuple-element.41), channel_id=1, source_target_pairs={{0,2},{1,3},{2,0},{3,1},{4,6},{5,7},{6,4},{7,5},{8,10},{9,11},{10,... | collective-permute-start | bytes 589832 | tf_op jit(solution)/shard_map/ppermute | solution.py:273
  58.4 15.4 %collective-permute-start.11 = (bf16[256,384]{1,0:T(8,128)(2,1)S(1)}, bf16[256,384]{1,0:T(8,128)(2,1)S(1)}, u32[]{:S(2)}, u32[]{:S(2)}) collective-permute-start(bf16[256,384]{1,0:T(8,128)(2,1)S(1)} %get-tuple-element.41), channel_id=1, source_target_pairs={{0,4},{1,5},{2,6},{3,7},{4,0},{5,1},{6,2},{7,3},{8,12},{9,13},{10,... | collective-permute-start | bytes 589832 | tf_op jit(solution)/shard_map/ppermute | solution.py:273
  61.4 13.5 %collective-permute-start.8 = (bf16[256,384]{1,0:T(8,128)(2,1)S(1)}, bf16[256,384]{1,0:T(8,128)(2,1)S(1)}, u32[]{:S(2)}, u32[]{:S(2)}) collective-permute-start(bf16[256,384]{1,0:T(8,128)(2,1)S(1)} %get-tuple-element.40.refs_0_), channel_id=1, source_target_pairs={{0,1},{1,0},{2,3},{3,2},{4,5},{5,4},{6,7},{7,6},{8,9},{9,8},{10,11... | collective-permute-start | bytes 589832 | tf_op jit(solution)/shard_map/ppermute | solution.py:273
  65.6 10.3 %collective-permute-start.46 = (bf16[384,256]{1,0:T(8,128)(2,1)S(1)}, bf16[384,256]{1,0:T(8,128)(2,1)S(1)}, u32[]{:S(2)}, u32[]{:S(2)}) collective-permute-start(bf16[384,256]{1,0:T(8,128)(2,1)S(1)} %get-tuple-element.37), channel_id=1, source_target_pairs={{0,2},{1,3},{2,0},{3,1},{4,6},{5,7},{6,4},{7,5},{8,10},{9,11},{10,... | collective-permute-start | bytes 589832 | tf_op jit(solution)/shard_map/ppermute | solution.py:273
  67.1 9.4 %collective-permute-start.44 = (bf16[384,256]{1,0:T(8,128)(2,1)S(1)}, bf16[384,256]{1,0:T(8,128)(2,1)S(1)}, u32[]{:S(2)}, u32[]{:S(2)}) collective-permute-start(bf16[384,256]{1,0:T(8,128)(2,1)S(1)} %get-tuple-element.54.refs_0_), channel_id=1, source_target_pairs={{0,1},{1,0},{2,3},{3,2},{4,5},{5,4},{6,7},{7,6},{8,9},{9,8},{10,11... | collective-permute-start | bytes 589832 | tf_op jit(solution)/shard_map/ppermute | solution.py:273
  74.8 16.3 %collective-permute-start.2 = (bf16[384,256]{1,0:T(8,128)(2,1)S(1)}, bf16[384,256]{1,0:T(8,128)(2,1)S(1)}, u32[]{:S(2)}, u32[]{:S(2)}) collective-permute-start(bf16[384,256]{1,0:T(8,128)(2,1)S(1)} %get-tuple-element.37), channel_id=1, source_target_pairs={{0,4},{1,5},{2,6},{3,7},{4,0},{5,1},{6,2},{7,3},{8,12},{9,13},{10,... | collective-permute-start | bytes 589832 | tf_op jit(solution)/shard_map/ppermute | solution.py:273
  75.8 15.3 %collective-permute-start.14 = (bf16[256,384]{1,0:T(8,128)(2,1)S(1)}, bf16[256,384]{1,0:T(8,128)(2,1)S(1)}, u32[]{:S(2)}, u32[]{:S(2)}) collective-permute-start(bf16[256,384]{1,0:T(8,128)(2,1)S(1)} %collective-permute-done.13.refs_6_), channel_id=1, source_target_pairs={{0,1},{1,0},{2,3},{3,2},{4,5},{5,4},{6,7},{7,6},{8,9},{9,8},{10,11... | collective-permute-start | bytes 589832 | tf_op jit(solution)/shard_map/ppermute | solution.py:273
  76.5 15.1 %collective-permute-start.10 = (bf16[256,384]{1,0:T(8,128)(2,1)S(1)}, bf16[256,384]{1,0:T(8,128)(2,1)S(1)}, u32[]{:S(2)}, u32[]{:S(2)}) collective-permute-start(bf16[256,384]{1,0:T(8,128)(2,1)S(1)} %collective-permute-done.9.refs_2_), channel_id=1, source_target_pairs={{0,1},{1,0},{2,3},{3,2},{4,5},{5,4},{6,7},{7,6},{8,9},{9,8},{10,11... | collective-permute-start | bytes 589832 | tf_op jit(solution)/shard_map/ppermute | solution.py:273
  77.9 15.7 %collective-permute-start.12 = (bf16[256,384]{1,0:T(8,128)(2,1)S(1)}, bf16[256,384]{1,0:T(8,128)(2,1)S(1)}, u32[]{:S(2)}, u32[]{:S(2)}) collective-permute-start(bf16[256,384]{1,0:T(8,128)(2,1)S(1)} %collective-permute-done.11.refs_4_), channel_id=1, source_target_pairs={{0,1},{1,0},{2,3},{3,2},{4,5},{5,4},{6,7},{7,6},{8,9},{9,8},{10,11... | collective-permute-start | bytes 589832 | tf_op jit(solution)/shard_map/ppermute | solution.py:273
  82.6 14.2 %collective-permute-start.48 = (bf16[384,256]{1,0:T(8,128)(2,1)S(1)}, bf16[384,256]{1,0:T(8,128)(2,1)S(1)}, u32[]{:S(2)}, u32[]{:S(2)}) collective-permute-start(bf16[384,256]{1,0:T(8,128)(2,1)S(1)} %collective-permute-done.46.refs_4_), channel_id=1, source_target_pairs={{0,1},{1,0},{2,3},{3,2},{4,5},{5,4},{6,7},{7,6},{8,9},{9,8},{10,11... | collective-permute-start | bytes 589832 | tf_op jit(solution)/shard_map/ppermute | solution.py:273
  93.6 10.0 %collective-permute-start.4 = (bf16[384,256]{1,0:T(8,128)(2,1)S(1)}, bf16[384,256]{1,0:T(8,128)(2,1)S(1)}, u32[]{:S(2)}, u32[]{:S(2)}) collective-permute-start(bf16[384,256]{1,0:T(8,128)(2,1)S(1)} %collective-permute-done.2.refs_0_), channel_id=1, source_target_pairs={{0,1},{1,0},{2,3},{3,2},{4,5},{5,4},{6,7},{7,6},{8,9},{9,8},{10,11... | collective-permute-start | bytes 589832 | tf_op jit(solution)/shard_map/ppermute | solution.py:273
  104.9 11.5 %collective-permute-start.50 = (bf16[80,1024]{1,0:T(8,128)(2,1)S(1)}, bf16[80,1024]{1,0:T(8,128)(2,1)S(1)}, u32[]{:S(2)}, u32[]{:S(2)}) collective-permute-start(bf16[80,1024]{1,0:T(8,128)(2,1)S(1)} %get-tuple-element.60), channel_id=1, source_target_pairs={{0,2},{1,3},{2,0},{3,1},{4,6},{5,7},{6,4},{7,5},{8,10},{9,11},{10,... | collective-permute-start | bytes 491528 | tf_op jit(solution)/shard_map/ppermute | solution.py:273
  105.1 12.6 %collective-permute-start.51 = (bf16[80,1024]{1,0:T(8,128)(2,1)S(1)}, bf16[80,1024]{1,0:T(8,128)(2,1)S(1)}, u32[]{:S(2)}, u32[]{:S(2)}) collective-permute-start(bf16[80,1024]{1,0:T(8,128)(2,1)S(1)} %get-tuple-element.61), channel_id=1, source_target_pairs={{0,16},{1,17},{2,18},{3,19},{4,20},{5,21},{6,22},{7,23},{8,24},{9,... | collective-permute-start | bytes 491528 | tf_op jit(solution)/shard_map/ppermute | solution.py:273
  105.1 14.8 %collective-permute-start.52 = (bf16[80,1024]{1,0:T(8,128)(2,1)S(1)}, bf16[80,1024]{1,0:T(8,128)(2,1)S(1)}, u32[]{:S(2)}, u32[]{:S(2)}) collective-permute-start(bf16[80,1024]{1,0:T(8,128)(2,1)S(1)} %get-tuple-element.62), channel_id=1, source_target_pairs={{0,18},{1,19},{2,16},{3,17},{4,22},{5,23},{6,20},{7,21},{8,26},{9,... | collective-permute-start | bytes 491528 | tf_op jit(solution)/shard_map/ppermute | solution.py:273
  109.2 12.8 %collective-permute-start.41 = (bf16[80,512]{1,0:T(8,128)(2,1)S(1)}, bf16[80,512]{1,0:T(8,128)(2,1)S(1)}, u32[]{:S(2)}, u32[]{:S(2)}) collective-permute-start(bf16[80,512]{1,0:T(8,128)(2,1)S(1)} %get-tuple-element.57), channel_id=1, source_target_pairs={{0,16},{1,17},{2,18},{3,19},{4,20},{5,21},{6,22},{7,23},{8,24},{9,... | collective-permute-start | bytes 245768 | tf_op jit(solution)/shard_map/ppermute | solution.py:273
  (25 other events, 153.4 us)

commit v5 on v4

--- a/solution.py
+++ b/solution.py
@@ -10,6 +10,7 @@
 
 VISITS = 4
 CAP = 80
+CUTS = 2
 AXES = ("expert", "group")
 F32 = jnp.float32
 BF16 = jnp.bfloat16
@@ -94,7 +95,7 @@
 def merge_kernel(half, parity, shares, *refs):
     pieces, out = refs[:-1], refs[-1]
     if len(pieces) >= 2 * VISITS:
-        first = pl.program_id(0) == parity[0]
+        first = pl.program_id(0) // CUTS == parity[0]
         values = []
         for k in range(VISITS):
             one, two = pieces[k][...], pieces[VISITS + k][...]
@@ -105,11 +106,11 @@
 
 
 def merge(half, parity, shares, pieces, before, width):
-    rows, tile = shares.shape[0], width // VISITS
+    rows, tile = shares.shape[0], width // VISITS // CUTS
     ins = [pl.BlockSpec(shares.shape, lambda i, half, parity: (0, 0))]
     for array, first, step in pieces:
         ins.append(
-            pl.BlockSpec((array.shape[0], tile), lambda i, half, parity, first=first, step=step: (0, first + step * i))
+            pl.BlockSpec((array.shape[0], tile), lambda i, half, parity, first=first, step=step: (0, (first + step * (i // CUTS)) * CUTS + i % CUTS))
         )
     args = [half, parity, shares, *(array for array, _, _ in pieces)]
     if before is not None:
@@ -119,9 +120,9 @@
         merge_kernel,
         grid_spec=pltpu.PrefetchScalarGridSpec(
             num_scalar_prefetch=2,
-            grid=(2,),
+            grid=(2 * CUTS,),
             in_specs=ins,
-            out_specs=pl.BlockSpec((rows, tile), lambda i, half, parity: (0, half[0] * 2 + i)),
+            out_specs=pl.BlockSpec((rows, tile), lambda i, half, parity: (0, half[0] * 2 * CUTS + i)),
         ),
         out_shape=jax.ShapeDtypeStruct((rows, width), BF16),
         input_output_aliases={} if before is None else {len(args) - 1: 0},

time: 127 us -> 128 us (level)
  Pallas kernels: 21.6 us -> 23 us
    pallas_call x2, Pallas kernels: 4 us -> 5.37 us  [merge(): pl.pallas_call(merge_kernel, grid_spec=pltpu.PrefetchScalarGridSpec(num_s...]
where the time goes in v5:
time: 128 us
  waiting for transfers between devices  52.1 us (41%)
  starting transfers between devices  51.9 us (41%)
  Pallas kernels  23 us (18%)
    ppermute x53, waiting for transfers between devices, swap(): return lax.ppermute(value, AXES, pairs)  52.1 us
    ppermute x53, starting transfers between devices, swap(): return lax.ppermute(value, AXES, pairs)  51.9 us
    pallas_call x16, Pallas kernels, call(): pl.pallas_call(kernel, out_shape=out_shape, in_specs=in_specs, out_specs=...  17.6 us
    pallas_call x2, Pallas kernels, merge(): pl.pallas_call(merge_kernel, grid_spec=pltpu.PrefetchScalarGridSpec(num_s...  5.37 us
  transfers between devices with their start and end apart: 53, of which 18 were waited for; matrix products, arithmetic and copies ran while one was open for 0% of the time, Pallas kernels for 14%

profile of v5, /device:TPU:0, one launch (start us, length us, event | category | flops | bytes accessed | tf_op | source)
XLA Modules:
  0.0 128.0 jit_solution(16384222856715072186)
XLA Ops:
  0.7 2.1 %shard_map.79 = (bf16[4,256,384]{2,1,0:T(8,128)(2,1)S(1)}, bf16[4,256,384]{2,1,0:T(8,128)(2,1)S(1)}) custom-call(s32[4]{0:T(128)S(1)} %copy-done, bf16[8,256,768]{2,1,0:T(8,128)(2,1)} %matrix.3), custom_call_target="tpu_custom_call" | custom-call | bytes 4718608 | tf_op jit(solution)/shard_map/pallas_call | solution.py:42
  3.3 3.7 %shard_map.73 = (bf16[80,2048]{1,0:T(8,128)(2,1)S(1)}, bf16[80,2048]{1,0:T(8,128)(2,1)S(1)}, bf16[80,2048]{1,0:T(8,128)(2,1)S(1)}, bf16[80,2048]{1,0:T(8,128)(2,...) custom-call(s32[4]{0:T(128)S(1)} %copy-done.1, ...), custom_call_target="tpu_custom_call" | custom-call | bytes 8814608 | tf_op jit(solution)/shard_map/pallas_call | solution.py:42
  7.1 3.0 %collective-permute-start.15 = (bf16[80,2048]{1,0:T(8,128)(2,1)S(1)}, bf16[80,2048]{1,0:T(8,128)(2,1)S(1)}, u32[]{:S(2)}, u32[]{:S(2)}) collective-permute-start(bf16[80,2048]{1,0:T(8,128)(2,1)S(1)} %get-tuple-element.43), channel_id=1, source_target_pairs={{0,2},{1,3},{2,0},{3,1},{4,6},{5,7},{6,4},{7,5},{8,10},{9,11},{10,... | collective-permute-start | bytes 983048 | tf_op jit(solution)/shard_map/ppermute | solution.py:274
  11.7 2.1 %shard_map.74 = (bf16[4,384,256]{2,1,0:T(8,128)(2,1)S(1)}, bf16[4,384,256]{2,1,0:T(8,128)(2,1)S(1)}) custom-call(s32[4]{0:T(128)S(1)} %copy-done.1, bf16[8,768,256]{2,1,0:T(8,128)(2,1)} %matrix.2), custom_call_target="tpu_custom_call" | custom-call | bytes 4718608 | tf_op jit(solution)/shard_map/pallas_call | solution.py:42
  13.8 4.3 %collective-permute-done.15.refs_9_ = bf16[80,2048]{1,0:T(8,128)(2,1)S(1)} collective-permute-done((bf16[80,2048]{1,0:T(8,128)(2,1)S(1)}, bf16[80,2048]{1,0:T(8,128)(2,1)S(1)}, u32[]{:S(2)}, u32[]{:S(2)}) %collective-permute-start.15) | collective-permute-done | bytes 327712 | tf_op jit(solution)/shard_map/ppermute | solution.py:274
  18.1 2.7 %collective-permute-start.17 = (bf16[80,2048]{1,0:T(8,128)(2,1)S(1)}, bf16[80,2048]{1,0:T(8,128)(2,1)S(1)}, u32[]{:S(2)}, u32[]{:S(2)}) collective-permute-start(bf16[80,2048]{1,0:T(8,128)(2,1)S(1)} %get-tuple-element.45), channel_id=1, source_target_pairs={{0,18},{1,19},{2,16},{3,17},{4,22},{5,23},{6,20},{7,21},{8,26},{9,... | collective-permute-start | bytes 983048 | tf_op jit(solution)/shard_map/ppermute | solution.py:274
  21.9 6.2 %collective-permute-done.17.refs_11_ = bf16[80,2048]{1,0:T(8,128)(2,1)S(1)} collective-permute-done((bf16[80,2048]{1,0:T(8,128)(2,1)S(1)}, bf16[80,2048]{1,0:T(8,128)(2,1)S(1)}, u32[]{:S(2)}, u32[]{:S(2)}) %collective-permute-start.17) | collective-permute-done | bytes 327712 | tf_op jit(solution)/shard_map/ppermute | solution.py:274
  32.0 2.3 %collective-permute-done.23.far = bf16[1,256,384]{2,1,0:T(8,128)(2,1)S(1)} collective-permute-done((bf16[1,256,384]{2,1,0:T(8,128)(2,1)S(1)}, bf16[1,256,384]{2,1,0:T(8,128)(2,1)S(1)}, u32[]{:S(2)}, u32[]{:S(2)}) %collective-permute-start.23) | collective-permute-done | bytes 196640 | tf_op jit(solution)/shard_map/ppermute | solution.py:274
  34.3 2.1 %collective-permute-start.7 = (bf16[2,256,384]{2,1,0:T(8,128)(2,1)S(1)}, bf16[2,256,384]{2,1,0:T(8,128)(2,1)S(1)}, u32[]{:S(2)}, u32[]{:S(2)}) collective-permute-start(bf16[2,256,384]{2,1,0:T(8,128)(2,1)S(1)} %shard_map.77), channel_id=1, source_target_pairs={{0,16},{1,17},{2,18},{3,19},{4,20},{5,21},{6,22},{7,23},{8,24},{9,... | collective-permute-start | bytes 1179656 | tf_op jit(solution)/shard_map/ppermute | solution.py:274
  37.0 3.8 %collective-permute-start.30 = (bf16[256,384]{1,0:T(8,128)(2,1)S(1)}, bf16[256,384]{1,0:T(8,128)(2,1)S(1)}, u32[]{:S(2)}, u32[]{:S(2)}) collective-permute-start(bf16[256,384]{1,0:T(8,128)(2,1)S(1)} %shard_map.81.refs_0_), channel_id=1, source_target_pairs={{0,6},{1,7},{2,4},{3,5},{4,2},{5,3},{6,0},{7,1},{8,14},{9,15},{10,... | collective-permute-start | bytes 589832 | tf_op jit(solution)/shard_map/ppermute | solution.py:274
  42.9 2.6 %collective-permute-start.28 = (bf16[256,384]{1,0:T(8,128)(2,1)S(1)}, bf16[256,384]{1,0:T(8,128)(2,1)S(1)}, u32[]{:S(2)}, u32[]{:S(2)}) collective-permute-start(bf16[256,384]{1,0:T(8,128)(2,1)S(1)} %shard_map.83), channel_id=1, source_target_pairs={{0,4},{1,5},{2,6},{3,7},{4,0},{5,1},{6,2},{7,3},{8,12},{9,13},{10,... | collective-permute-start | bytes 589832 | tf_op jit(solution)/shard_map/ppermute | solution.py:274
  46.1 1.5 %collective-permute-start.24 = (bf16[256,384]{1,0:T(8,128)(2,1)S(1)}, bf16[256,384]{1,0:T(8,128)(2,1)S(1)}, u32[]{:S(2)}, u32[]{:S(2)}) collective-permute-start(bf16[256,384]{1,0:T(8,128)(2,1)S(1)} %shard_map.81.refs_0_), channel_id=1, source_target_pairs={{0,1},{1,0},{2,3},{3,2},{4,5},{5,4},{6,7},{7,6},{8,9},{9,8},{10,11... | collective-permute-start | bytes 589832 | tf_op jit(solution)/shard_map/ppermute | solution.py:274
  51.2 3.1 %collective-permute-done.28.refs_4_ = bf16[256,384]{1,0:T(8,128)(2,1)S(1)} collective-permute-done((bf16[256,384]{1,0:T(8,128)(2,1)S(1)}, bf16[256,384]{1,0:T(8,128)(2,1)S(1)}, u32[]{:S(2)}, u32[]{:S(2)}) %collective-permute-start.28) | collective-permute-done | bytes 196640 | tf_op jit(solution)/shard_map/ppermute | solution.py:274
  55.9 2.5 %collective-permute-start.13 = (bf16[256,384]{1,0:T(8,128)(2,1)S(1)}, bf16[256,384]{1,0:T(8,128)(2,1)S(1)}, u32[]{:S(2)}, u32[]{:S(2)}) collective-permute-start(bf16[256,384]{1,0:T(8,128)(2,1)S(1)} %get-tuple-element.40.refs_0_), channel_id=1, source_target_pairs={{0,6},{1,7},{2,4},{3,5},{4,2},{5,3},{6,0},{7,1},{8,14},{9,15},{10,... | collective-permute-start | bytes 589832 | tf_op jit(solution)/shard_map/ppermute | solution.py:274
  58.4 1.9 %collective-permute-start.11 = (bf16[256,384]{1,0:T(8,128)(2,1)S(1)}, bf16[256,384]{1,0:T(8,128)(2,1)S(1)}, u32[]{:S(2)}, u32[]{:S(2)}) collective-permute-start(bf16[256,384]{1,0:T(8,128)(2,1)S(1)} %get-tuple-element.41), channel_id=1, source_target_pairs={{0,4},{1,5},{2,6},{3,7},{4,0},{5,1},{6,2},{7,3},{8,12},{9,13},{10,... | collective-permute-start | bytes 589832 | tf_op jit(solution)/shard_map/ppermute | solution.py:274
  62.6 2.9 %collective-permute-done.29.refs_5_ = bf16[256,384]{1,0:T(8,128)(2,1)S(1)} collective-permute-done((bf16[256,384]{1,0:T(8,128)(2,1)S(1)}, bf16[256,384]{1,0:T(8,128)(2,1)S(1)}, u32[]{:S(2)}, u32[]{:S(2)}) %collective-permute-start.29) | collective-permute-done | bytes 196640 | tf_op jit(solution)/shard_map/ppermute | solution.py:274
  65.6 1.6 %collective-permute-start.46 = (bf16[384,256]{1,0:T(8,128)(2,1)S(1)}, bf16[384,256]{1,0:T(8,128)(2,1)S(1)}, u32[]{:S(2)}, u32[]{:S(2)}) collective-permute-start(bf16[384,256]{1,0:T(8,128)(2,1)S(1)} %get-tuple-element.37), channel_id=1, source_target_pairs={{0,2},{1,3},{2,0},{3,1},{4,6},{5,7},{6,4},{7,5},{8,10},{9,11},{10,... | collective-permute-start | bytes 589832 | tf_op jit(solution)/shard_map/ppermute | solution.py:274
  67.1 2.3 %collective-permute-start.44 = (bf16[384,256]{1,0:T(8,128)(2,1)S(1)}, bf16[384,256]{1,0:T(8,128)(2,1)S(1)}, u32[]{:S(2)}, u32[]{:S(2)}) collective-permute-start(bf16[384,256]{1,0:T(8,128)(2,1)S(1)} %get-tuple-element.54.refs_0_), channel_id=1, source_target_pairs={{0,1},{1,0},{2,3},{3,2},{4,5},{5,4},{6,7},{7,6},{8,9},{9,8},{10,11... | collective-permute-start | bytes 589832 | tf_op jit(solution)/shard_map/ppermute | solution.py:274
  70.2 3.6 %collective-permute-done.11.refs_4_ = bf16[256,384]{1,0:T(8,128)(2,1)S(1)} collective-permute-done((bf16[256,384]{1,0:T(8,128)(2,1)S(1)}, bf16[256,384]{1,0:T(8,128)(2,1)S(1)}, u32[]{:S(2)}, u32[]{:S(2)}) %collective-permute-start.11) | collective-permute-done | bytes 196640 | tf_op jit(solution)/shard_map/ppermute | solution.py:274
  78.5 4.1 %collective-permute-done.36.refs_0_ = bf16[384,256]{1,0:T(8,128)(2,1)S(1)} collective-permute-done((bf16[384,256]{1,0:T(8,128)(2,1)S(1)}, bf16[384,256]{1,0:T(8,128)(2,1)S(1)}, u32[]{:S(2)}, u32[]{:S(2)}) %collective-permute-start.36) | collective-permute-done | bytes 196640 | tf_op jit(solution)/shard_map/ppermute | solution.py:274
  83.1 8.0 %collective-permute-done.2.refs_0_ = bf16[384,256]{1,0:T(8,128)(2,1)S(1)} collective-permute-done((bf16[384,256]{1,0:T(8,128)(2,1)S(1)}, bf16[384,256]{1,0:T(8,128)(2,1)S(1)}, u32[]{:S(2)}, u32[]{:S(2)}) %collective-permute-start.2) | collective-permute-done | bytes 196640 | tf_op jit(solution)/shard_map/ppermute | solution.py:274
  92.0 1.5 %shard_map.84.refs_16_ = f32[2,320,384]{2,1,0:T(8,128)S(1)} custom-call(bf16[256,384]{1,0:T(8,128)(2,1)S(1)} %shard_map.81.refs_0_, bf16[256,384]{1,0:T(8,128)(2,1)S(1)} %collective-permute-done.24.refs_1_, bf16[256,384]{1,0:T(8,128)(2,1)S(1)} %collective-permute-done.26.refs_2_, bf16[256,384]{1,0:T(8,128)(2,1)S(1)} %collective-permute-done.27.refs_3_, ...), custom_call_target="tpu_custom_call" | custom-call | flops 1006632960 | bytes 5177344 | tf_op jit(solution)/shard_map/pallas_call | solution.py:42
  93.6 1.7 %collective-permute-start.4 = (bf16[384,256]{1,0:T(8,128)(2,1)S(1)}, bf16[384,256]{1,0:T(8,128)(2,1)S(1)}, u32[]{:S(2)}, u32[]{:S(2)}) collective-permute-start(bf16[384,256]{1,0:T(8,128)(2,1)S(1)} %collective-permute-done.2.refs_0_), channel_id=1, source_target_pairs={{0,1},{1,0},{2,3},{3,2},{4,5},{5,4},{6,7},{7,6},{8,9},{9,8},{10,11... | collective-permute-start | bytes 589832 | tf_op jit(solution)/shard_map/ppermute | solution.py:274
  95.3 1.5 %shard_map.85 = (bf16[320,384]{1,0:T(8,128)(2,1)S(1)}, bf16[320,384]{1,0:T(8,128)(2,1)S(1)}) custom-call(bf16[256,384]{1,0:T(8,128)(2,1)S(1)} %get-tuple-element.40.refs_0_, bf16[256,384]{1,0:T(8,128)(2,1)S(1)} %collective-permute-done.8.refs_1_, bf16[256,384]{1,0:T(8,128)(2,1)S(1)} %collective-permute-done.9.refs_2_, ...), custom_call_target="tpu_custom_call" | custom-call | flops 1006632960 | bytes 5668864 | tf_op jit(solution)/shard_map/pallas_call | solution.py:42
  97.5 2.7 %collective-permute-done.38.refs_2_ = bf16[384,256]{1,0:T(8,128)(2,1)S(1)} collective-permute-done((bf16[384,256]{1,0:T(8,128)(2,1)S(1)}, bf16[384,256]{1,0:T(8,128)(2,1)S(1)}, u32[]{:S(2)}, u32[]{:S(2)}) %collective-permute-start.38) | collective-permute-done | bytes 196640 | tf_op jit(solution)/shard_map/ppermute | solution.py:274
  100.2 3.4 %collective-permute-done.4.refs_2_ = bf16[384,256]{1,0:T(8,128)(2,1)S(1)} collective-permute-done((bf16[384,256]{1,0:T(8,128)(2,1)S(1)}, bf16[384,256]{1,0:T(8,128)(2,1)S(1)}, u32[]{:S(2)}, u32[]{:S(2)}) %collective-permute-start.4) | collective-permute-done | bytes 196640 | tf_op jit(solution)/shard_map/ppermute | solution.py:274
  105.1 3.4 %collective-permute-start.52 = (bf16[80,1024]{1,0:T(8,128)(2,1)S(1)}, bf16[80,1024]{1,0:T(8,128)(2,1)S(1)}, u32[]{:S(2)}, u32[]{:S(2)}) collective-permute-start(bf16[80,1024]{1,0:T(8,128)(2,1)S(1)} %get-tuple-element.62), channel_id=1, source_target_pairs={{0,18},{1,19},{2,16},{3,17},{4,22},{5,23},{6,20},{7,21},{8,26},{9,... | collective-permute-start | bytes 491528 | tf_op jit(solution)/shard_map/ppermute | solution.py:274
  110.2 6.3 %collective-permute-done.40.refs_5_ = bf16[80,512]{1,0:T(8,128)(2,1)S(1)} collective-permute-done((bf16[80,512]{1,0:T(8,128)(2,1)S(1)}, bf16[80,512]{1,0:T(8,128)(2,1)S(1)}, u32[]{:S(2)}, u32[]{:S(2)}) %collective-permute-start.40) | collective-permute-done | bytes 81952 | tf_op jit(solution)/shard_map/ppermute | solution.py:274
  117.7 2.2 %collective-permute-start.34 = (bf16[80,512]{1,0:T(8,128)(2,1)S(1)}, bf16[80,512]{1,0:T(8,128)(2,1)S(1)}, u32[]{:S(2)}, u32[]{:S(2)}) collective-permute-start(bf16[80,512]{1,0:T(8,128)(2,1)S(1)} %get-tuple-element.52), channel_id=1, source_target_pairs={{0,16},{1,17},{2,18},{3,19},{4,20},{5,21},{6,22},{7,23},{8,24},{9,... | collective-permute-start | bytes 245768 | tf_op jit(solution)/shard_map/ppermute | solution.py:274
  119.9 2.7 %shard_map.89.refs_8_ = bf16[512,2048]{1,0:T(8,128)(2,1)} custom-call(s32[1]{0:T(128)} %bitcast.4.half, s32[1]{0:T(128)} %bitcast.1.parity, bf16[512,640]{1,0:T(8,128)(2,1)S(1)} %get-tuple-element.34.shares, bf16[80,1024]{1,0:T(8,128)(2,1)S(1)} %get-tuple-element.59.refs_0_, bf16[80,1024]{1,0:T(8,128)(2,1)S(1)} %collective-permute-done.50.refs_1_, ...), custom_call_target="tpu_custom_call" | custom-call | flops 335544320 | bytes 1310720 | tf_op jit(solution)/shard_map/pallas_call | solution.py:119
  123.5 1.7 %collective-permute-done.35.refs_3_ = bf16[80,512]{1,0:T(8,128)(2,1)S(1)} collective-permute-done((bf16[80,512]{1,0:T(8,128)(2,1)S(1)}, bf16[80,512]{1,0:T(8,128)(2,1)S(1)}, u32[]{:S(2)}, u32[]{:S(2)}) %collective-permute-start.35) | collective-permute-done | bytes 81952 | tf_op jit(solution)/shard_map/ppermute | solution.py:274
  125.3 2.7 %shard_map.90 = bf16[512,2048]{1,0:T(8,128)(2,1)} custom-call(s32[1]{0:T(128)} %bitcast.half, s32[1]{0:T(128)} %bitcast.1.parity, bf16[512,640]{1,0:T(8,128)(2,1)S(1)} %get-tuple-element.34.shares, bf16[80,512]{1,0:T(8,128)(2,1)S(1)} %get-tuple-element.50.refs_0_, ...), custom_call_target="tpu_custom_call", output_to_operand_aliasing={{}: (11, {})} | custom-call | flops 335544320 | bytes 1310720 | tf_op jit(solution)/shard_map/pallas_call | solution.py:119
  (100 shorter events, 31.5 us)
Async XLA Ops:
  2.8 18.0 %collective-permute-start.22 = (bf16[4,256,384]{2,1,0:T(8,128)(2,1)S(1)}, bf16[4,256,384]{2,1,0:T(8,128)(2,1)S(1)}, u32[]{:S(2)}, u32[]{:S(2)}) collective-permute-start(bf16[4,256,384]{2,1,0:T(8,128)(2,1)S(1)} %get-tuple-element.47), channel_id=1, source_target_pairs={{0,8},{1,9},{2,10},{3,11},{4,12},{5,13},{6,14},{7,15},{8,0},{9,1},... | collective-permute-start | bytes 2359304 | tf_op jit(solution)/shard_map/ppermute | solution.py:274
  7.0 23.6 %collective-permute-start.6 = (bf16[4,256,384]{2,1,0:T(8,128)(2,1)S(1)}, bf16[4,256,384]{2,1,0:T(8,128)(2,1)S(1)}, u32[]{:S(2)}, u32[]{:S(2)}) collective-permute-start(bf16[4,256,384]{2,1,0:T(8,128)(2,1)S(1)} %get-tuple-element.39), channel_id=1, source_target_pairs={{0,8},{1,9},{2,10},{3,11},{4,12},{5,13},{6,14},{7,15},{8,0},{9,1},... | collective-permute-start | bytes 2359304 | tf_op jit(solution)/shard_map/ppermute | solution.py:274
  7.1 11.0 %collective-permute-start.15 = (bf16[80,2048]{1,0:T(8,128)(2,1)S(1)}, bf16[80,2048]{1,0:T(8,128)(2,1)S(1)}, u32[]{:S(2)}, u32[]{:S(2)}) collective-permute-start(bf16[80,2048]{1,0:T(8,128)(2,1)S(1)} %get-tuple-element.43), channel_id=1, source_target_pairs={{0,2},{1,3},{2,0},{3,1},{4,6},{5,7},{6,4},{7,5},{8,10},{9,11},{10,... | collective-permute-start | bytes 983048 | tf_op jit(solution)/shard_map/ppermute | solution.py:274
  10.2 10.6 %collective-permute-start.16 = (bf16[80,2048]{1,0:T(8,128)(2,1)S(1)}, bf16[80,2048]{1,0:T(8,128)(2,1)S(1)}, u32[]{:S(2)}, u32[]{:S(2)}) collective-permute-start(bf16[80,2048]{1,0:T(8,128)(2,1)S(1)} %get-tuple-element.44), channel_id=1, source_target_pairs={{0,16},{1,17},{2,18},{3,19},{4,20},{5,21},{6,22},{7,23},{8,24},{9,... | collective-permute-start | bytes 983048 | tf_op jit(solution)/shard_map/ppermute | solution.py:274
  13.8 23.2 %collective-permute-start = (bf16[4,384,256]{2,1,0:T(8,128)(2,1)S(1)}, bf16[4,384,256]{2,1,0:T(8,128)(2,1)S(1)}, u32[]{:S(2)}, u32[]{:S(2)}) collective-permute-start(bf16[4,384,256]{2,1,0:T(8,128)(2,1)S(1)} %get-tuple-element.36), channel_id=1, source_target_pairs={{0,8},{1,9},{2,10},{3,11},{4,12},{5,13},{6,14},{7,15},{8,0},{9,1},... | collective-permute-start | bytes 2359304 | tf_op jit(solution)/shard_map/ppermute | solution.py:274
  18.1 10.0 %collective-permute-start.17 = (bf16[80,2048]{1,0:T(8,128)(2,1)S(1)}, bf16[80,2048]{1,0:T(8,128)(2,1)S(1)}, u32[]{:S(2)}, u32[]{:S(2)}) collective-permute-start(bf16[80,2048]{1,0:T(8,128)(2,1)S(1)} %get-tuple-element.45), channel_id=1, source_target_pairs={{0,18},{1,19},{2,16},{3,17},{4,22},{5,23},{6,20},{7,21},{8,26},{9,... | collective-permute-start | bytes 983048 | tf_op jit(solution)/shard_map/ppermute | solution.py:274
  29.5 12.5 %collective-permute-start.20 = (bf16[80,2048]{1,0:T(8,128)(2,1)S(1)}, bf16[80,2048]{1,0:T(8,128)(2,1)S(1)}, u32[]{:S(2)}, u32[]{:S(2)}) collective-permute-start(bf16[80,2048]{1,0:T(8,128)(2,1)S(1)} %collective-permute-done.16.refs_10_), channel_id=1, source_target_pairs={{0,8},{1,9},{2,10},{3,11},{4,12},{5,13},{6,14},{7,15},{8,0},{9,1},... | collective-permute-start | bytes 983048 | tf_op jit(solution)/shard_map/ppermute | solution.py:274
  29.5 13.4 %collective-permute-start.21 = (bf16[80,2048]{1,0:T(8,128)(2,1)S(1)}, bf16[80,2048]{1,0:T(8,128)(2,1)S(1)}, u32[]{:S(2)}, u32[]{:S(2)}) collective-permute-start(bf16[80,2048]{1,0:T(8,128)(2,1)S(1)} %collective-permute-done.17.refs_11_), channel_id=1, source_target_pairs={{0,8},{1,9},{2,10},{3,11},{4,12},{5,13},{6,14},{7,15},{8,0},{9,1},... | collective-permute-start | bytes 983048 | tf_op jit(solution)/shard_map/ppermute | solution.py:274
  30.6 10.7 %collective-permute-start.25 = (bf16[1,256,384]{2,1,0:T(8,128)(2,1)S(1)}, bf16[1,256,384]{2,1,0:T(8,128)(2,1)S(1)}, u32[]{:S(2)}, u32[]{:S(2)}) collective-permute-start(bf16[1,256,384]{2,1,0:T(8,128)(2,1)S(1)} %shard_map.82), channel_id=1, source_target_pairs={{0,16},{1,17},{2,18},{3,19},{4,20},{5,21},{6,22},{7,23},{8,24},{9,... | collective-permute-start | bytes 589832 | tf_op jit(solution)/shard_map/ppermute | solution.py:274
  34.3 13.3 %collective-permute-start.7 = (bf16[2,256,384]{2,1,0:T(8,128)(2,1)S(1)}, bf16[2,256,384]{2,1,0:T(8,128)(2,1)S(1)}, u32[]{:S(2)}, u32[]{:S(2)}) collective-permute-start(bf16[2,256,384]{2,1,0:T(8,128)(2,1)S(1)} %shard_map.77), channel_id=1, source_target_pairs={{0,16},{1,17},{2,18},{3,19},{4,20},{5,21},{6,22},{7,23},{8,24},{9,... | collective-permute-start | bytes 1179656 | tf_op jit(solution)/shard_map/ppermute | solution.py:274
  41.4 17.0 %collective-permute-start.1 = (bf16[2,384,256]{2,1,0:T(8,128)(2,1)S(1)}, bf16[2,384,256]{2,1,0:T(8,128)(2,1)S(1)}, u32[]{:S(2)}, u32[]{:S(2)}) collective-permute-start(bf16[2,384,256]{2,1,0:T(8,128)(2,1)S(1)} %shard_map.75), channel_id=1, source_target_pairs={{0,16},{1,17},{2,18},{3,19},{4,20},{5,21},{6,22},{7,23},{8,24},{9,... | collective-permute-start | bytes 1179656 | tf_op jit(solution)/shard_map/ppermute | solution.py:274
  42.9 11.4 %collective-permute-start.28 = (bf16[256,384]{1,0:T(8,128)(2,1)S(1)}, bf16[256,384]{1,0:T(8,128)(2,1)S(1)}, u32[]{:S(2)}, u32[]{:S(2)}) collective-permute-start(bf16[256,384]{1,0:T(8,128)(2,1)S(1)} %shard_map.83), channel_id=1, source_target_pairs={{0,4},{1,5},{2,6},{3,7},{4,0},{5,1},{6,2},{7,3},{8,12},{9,13},{10,... | collective-permute-start | bytes 589832 | tf_op jit(solution)/shard_map/ppermute | solution.py:274
  46.1 9.8 %collective-permute-start.24 = (bf16[256,384]{1,0:T(8,128)(2,1)S(1)}, bf16[256,384]{1,0:T(8,128)(2,1)S(1)}, u32[]{:S(2)}, u32[]{:S(2)}) collective-permute-start(bf16[256,384]{1,0:T(8,128)(2,1)S(1)} %shard_map.81.refs_0_), channel_id=1, source_target_pairs={{0,1},{1,0},{2,3},{3,2},{4,5},{5,4},{6,7},{7,6},{8,9},{9,8},{10,11... | collective-permute-start | bytes 589832 | tf_op jit(solution)/shard_map/ppermute | solution.py:274
  47.6 10.8 %collective-permute-start.31 = (bf16[256,384]{1,0:T(8,128)(2,1)S(1)}, bf16[256,384]{1,0:T(8,128)(2,1)S(1)}, u32[]{:S(2)}, u32[]{:S(2)}) collective-permute-start(bf16[256,384]{1,0:T(8,128)(2,1)S(1)} %collective-permute-done.30.refs_6_), channel_id=1, source_target_pairs={{0,1},{1,0},{2,3},{3,2},{4,5},{5,4},{6,7},{7,6},{8,9},{9,8},{10,11... | collective-permute-start | bytes 589832 | tf_op jit(solution)/shard_map/ppermute | solution.py:274
  49.7 11.6 %collective-permute-start.27 = (bf16[256,384]{1,0:T(8,128)(2,1)S(1)}, bf16[256,384]{1,0:T(8,128)(2,1)S(1)}, u32[]{:S(2)}, u32[]{:S(2)}) collective-permute-start(bf16[256,384]{1,0:T(8,128)(2,1)S(1)} %collective-permute-done.26.refs_2_), channel_id=1, source_target_pairs={{0,1},{1,0},{2,3},{3,2},{4,5},{5,4},{6,7},{7,6},{8,9},{9,8},{10,11... | collective-permute-start | bytes 589832 | tf_op jit(solution)/shard_map/ppermute | solution.py:274
  54.4 11.2 %collective-permute-start.29 = (bf16[256,384]{1,0:T(8,128)(2,1)S(1)}, bf16[256,384]{1,0:T(8,128)(2,1)S(1)}, u32[]{:S(2)}, u32[]{:S(2)}) collective-permute-start(bf16[256,384]{1,0:T(8,128)(2,1)S(1)} %collective-permute-done.28.refs_4_), channel_id=1, source_target_pairs={{0,1},{1,0},{2,3},{3,2},{4,5},{5,4},{6,7},{7,6},{8,9},{9,8},{10,11... | collective-permute-start | bytes 589832 | tf_op jit(solution)/shard_map/ppermute | solution.py:274
  55.9 11.2 %collective-permute-start.13 = (bf16[256,384]{1,0:T(8,128)(2,1)S(1)}, bf16[256,384]{1,0:T(8,128)(2,1)S(1)}, u32[]{:S(2)}, u32[]{:S(2)}) collective-permute-start(bf16[256,384]{1,0:T(8,128)(2,1)S(1)} %get-tuple-element.40.refs_0_), channel_id=1, source_target_pairs={{0,6},{1,7},{2,4},{3,5},{4,2},{5,3},{6,0},{7,1},{8,14},{9,15},{10,... | collective-permute-start | bytes 589832 | tf_op jit(solution)/shard_map/ppermute | solution.py:274
  58.4 11.8 %collective-permute-start.9 = (bf16[256,384]{1,0:T(8,128)(2,1)S(1)}, bf16[256,384]{1,0:T(8,128)(2,1)S(1)}, u32[]{:S(2)}, u32[]{:S(2)}) collective-permute-start(bf16[256,384]{1,0:T(8,128)(2,1)S(1)} %get-tuple-element.41), channel_id=1, source_target_pairs={{0,2},{1,3},{2,0},{3,1},{4,6},{5,7},{6,4},{7,5},{8,10},{9,11},{10,... | collective-permute-start | bytes 589832 | tf_op jit(solution)/shard_map/ppermute | solution.py:274
  58.4 15.4 %collective-permute-start.11 = (bf16[256,384]{1,0:T(8,128)(2,1)S(1)}, bf16[256,384]{1,0:T(8,128)(2,1)S(1)}, u32[]{:S(2)}, u32[]{:S(2)}) collective-permute-start(bf16[256,384]{1,0:T(8,128)(2,1)S(1)} %get-tuple-element.41), channel_id=1, source_target_pairs={{0,4},{1,5},{2,6},{3,7},{4,0},{5,1},{6,2},{7,3},{8,12},{9,13},{10,... | collective-permute-start | bytes 589832 | tf_op jit(solution)/shard_map/ppermute | solution.py:274
  61.4 13.5 %collective-permute-start.8 = (bf16[256,384]{1,0:T(8,128)(2,1)S(1)}, bf16[256,384]{1,0:T(8,128)(2,1)S(1)}, u32[]{:S(2)}, u32[]{:S(2)}) collective-permute-start(bf16[256,384]{1,0:T(8,128)(2,1)S(1)} %get-tuple-element.40.refs_0_), channel_id=1, source_target_pairs={{0,1},{1,0},{2,3},{3,2},{4,5},{5,4},{6,7},{7,6},{8,9},{9,8},{10,11... | collective-permute-start | bytes 589832 | tf_op jit(solution)/shard_map/ppermute | solution.py:274
  65.6 10.3 %collective-permute-start.46 = (bf16[384,256]{1,0:T(8,128)(2,1)S(1)}, bf16[384,256]{1,0:T(8,128)(2,1)S(1)}, u32[]{:S(2)}, u32[]{:S(2)}) collective-permute-start(bf16[384,256]{1,0:T(8,128)(2,1)S(1)} %get-tuple-element.37), channel_id=1, source_target_pairs={{0,2},{1,3},{2,0},{3,1},{4,6},{5,7},{6,4},{7,5},{8,10},{9,11},{10,... | collective-permute-start | bytes 589832 | tf_op jit(solution)/shard_map/ppermute | solution.py:274
  67.1 9.4 %collective-permute-start.44 = (bf16[384,256]{1,0:T(8,128)(2,1)S(1)}, bf16[384,256]{1,0:T(8,128)(2,1)S(1)}, u32[]{:S(2)}, u32[]{:S(2)}) collective-permute-start(bf16[384,256]{1,0:T(8,128)(2,1)S(1)} %get-tuple-element.54.refs_0_), channel_id=1, source_target_pairs={{0,1},{1,0},{2,3},{3,2},{4,5},{5,4},{6,7},{7,6},{8,9},{9,8},{10,11... | collective-permute-start | bytes 589832 | tf_op jit(solution)/shard_map/ppermute | solution.py:274
  74.8 16.3 %collective-permute-start.2 = (bf16[384,256]{1,0:T(8,128)(2,1)S(1)}, bf16[384,256]{1,0:T(8,128)(2,1)S(1)}, u32[]{:S(2)}, u32[]{:S(2)}) collective-permute-start(bf16[384,256]{1,0:T(8,128)(2,1)S(1)} %get-tuple-element.37), channel_id=1, source_target_pairs={{0,4},{1,5},{2,6},{3,7},{4,0},{5,1},{6,2},{7,3},{8,12},{9,13},{10,... | collective-permute-start | bytes 589832 | tf_op jit(solution)/shard_map/ppermute | solution.py:274
  75.8 15.3 %collective-permute-start.14 = (bf16[256,384]{1,0:T(8,128)(2,1)S(1)}, bf16[256,384]{1,0:T(8,128)(2,1)S(1)}, u32[]{:S(2)}, u32[]{:S(2)}) collective-permute-start(bf16[256,384]{1,0:T(8,128)(2,1)S(1)} %collective-permute-done.13.refs_6_), channel_id=1, source_target_pairs={{0,1},{1,0},{2,3},{3,2},{4,5},{5,4},{6,7},{7,6},{8,9},{9,8},{10,11... | collective-permute-start | bytes 589832 | tf_op jit(solution)/shard_map/ppermute | solution.py:274
  76.5 15.1 %collective-permute-start.10 = (bf16[256,384]{1,0:T(8,128)(2,1)S(1)}, bf16[256,384]{1,0:T(8,128)(2,1)S(1)}, u32[]{:S(2)}, u32[]{:S(2)}) collective-permute-start(bf16[256,384]{1,0:T(8,128)(2,1)S(1)} %collective-permute-done.9.refs_2_), channel_id=1, source_target_pairs={{0,1},{1,0},{2,3},{3,2},{4,5},{5,4},{6,7},{7,6},{8,9},{9,8},{10,11... | collective-permute-start | bytes 589832 | tf_op jit(solution)/shard_map/ppermute | solution.py:274
  77.9 15.7 %collective-permute-start.12 = (bf16[256,384]{1,0:T(8,128)(2,1)S(1)}, bf16[256,384]{1,0:T(8,128)(2,1)S(1)}, u32[]{:S(2)}, u32[]{:S(2)}) collective-permute-start(bf16[256,384]{1,0:T(8,128)(2,1)S(1)} %collective-permute-done.11.refs_4_), channel_id=1, source_target_pairs={{0,1},{1,0},{2,3},{3,2},{4,5},{5,4},{6,7},{7,6},{8,9},{9,8},{10,11... | collective-permute-start | bytes 589832 | tf_op jit(solution)/shard_map/ppermute | solution.py:274
  82.6 14.2 %collective-permute-start.48 = (bf16[384,256]{1,0:T(8,128)(2,1)S(1)}, bf16[384,256]{1,0:T(8,128)(2,1)S(1)}, u32[]{:S(2)}, u32[]{:S(2)}) collective-permute-start(bf16[384,256]{1,0:T(8,128)(2,1)S(1)} %collective-permute-done.46.refs_4_), channel_id=1, source_target_pairs={{0,1},{1,0},{2,3},{3,2},{4,5},{5,4},{6,7},{7,6},{8,9},{9,8},{10,11... | collective-permute-start | bytes 589832 | tf_op jit(solution)/shard_map/ppermute | solution.py:274
  93.6 10.0 %collective-permute-start.4 = (bf16[384,256]{1,0:T(8,128)(2,1)S(1)}, bf16[384,256]{1,0:T(8,128)(2,1)S(1)}, u32[]{:S(2)}, u32[]{:S(2)}) collective-permute-start(bf16[384,256]{1,0:T(8,128)(2,1)S(1)} %collective-permute-done.2.refs_0_), channel_id=1, source_target_pairs={{0,1},{1,0},{2,3},{3,2},{4,5},{5,4},{6,7},{7,6},{8,9},{9,8},{10,11... | collective-permute-start | bytes 589832 | tf_op jit(solution)/shard_map/ppermute | solution.py:274
  104.9 11.5 %collective-permute-start.50 = (bf16[80,1024]{1,0:T(8,128)(2,1)S(1)}, bf16[80,1024]{1,0:T(8,128)(2,1)S(1)}, u32[]{:S(2)}, u32[]{:S(2)}) collective-permute-start(bf16[80,1024]{1,0:T(8,128)(2,1)S(1)} %get-tuple-element.60), channel_id=1, source_target_pairs={{0,2},{1,3},{2,0},{3,1},{4,6},{5,7},{6,4},{7,5},{8,10},{9,11},{10,... | collective-permute-start | bytes 491528 | tf_op jit(solution)/shard_map/ppermute | solution.py:274
  105.1 12.6 %collective-permute-start.51 = (bf16[80,1024]{1,0:T(8,128)(2,1)S(1)}, bf16[80,1024]{1,0:T(8,128)(2,1)S(1)}, u32[]{:S(2)}, u32[]{:S(2)}) collective-permute-start(bf16[80,1024]{1,0:T(8,128)(2,1)S(1)} %get-tuple-element.61), channel_id=1, source_target_pairs={{0,16},{1,17},{2,18},{3,19},{4,20},{5,21},{6,22},{7,23},{8,24},{9,... | collective-permute-start | bytes 491528 | tf_op jit(solution)/shard_map/ppermute | solution.py:274
  105.1 14.8 %collective-permute-start.52 = (bf16[80,1024]{1,0:T(8,128)(2,1)S(1)}, bf16[80,1024]{1,0:T(8,128)(2,1)S(1)}, u32[]{:S(2)}, u32[]{:S(2)}) collective-permute-start(bf16[80,1024]{1,0:T(8,128)(2,1)S(1)} %get-tuple-element.62), channel_id=1, source_target_pairs={{0,18},{1,19},{2,16},{3,17},{4,22},{5,23},{6,20},{7,21},{8,26},{9,... | collective-permute-start | bytes 491528 | tf_op jit(solution)/shard_map/ppermute | solution.py:274
  109.2 13.4 %collective-permute-start.41 = (bf16[80,512]{1,0:T(8,128)(2,1)S(1)}, bf16[80,512]{1,0:T(8,128)(2,1)S(1)}, u32[]{:S(2)}, u32[]{:S(2)}) collective-permute-start(bf16[80,512]{1,0:T(8,128)(2,1)S(1)} %get-tuple-element.57), channel_id=1, source_target_pairs={{0,16},{1,17},{2,18},{3,19},{4,20},{5,21},{6,22},{7,23},{8,24},{9,... | collective-permute-start | bytes 245768 | tf_op jit(solution)/shard_map/ppermute | solution.py:274
  (25 other events, 154.6 us)
